TPU v7x, 256 devices: a whole 4x4x8 slice. The times are simulated.
256 devices in a mesh: dom: 32 (over x, z), cls: 8 (over y, core).
Axes of the slice: x: 4, y: 4, z: 8, core: 2. Of those that a mesh axis runs over, the one named last changes fastest.
Arguments:
- particles: bfloat16 [256, 1024, 9, 128], P(None, ('dom', 'cls')), may hold values from -6 to 6
- references: bfloat16 [256, 400, 128], P(None, 'cls'), may hold values from -6 to 6
- class_ids: int32 [1024, 3], P(('dom', 'cls')), may hold values from 0 to 399, all different within a row
- counts: int32 [1024], P(('dom', 'cls')), may hold values from 1 to 3
- shift_ids: int32 [1024, 3], P(('dom', 'cls')), may hold values from 0 to 8
- weights: bfloat16 [1024, 3], P(('dom', 'cls')), may hold values from 0.049804688 to 1
Outputs:
- best_scores: float32 [1024, 400], P('dom', 'cls')
- class_means: float32 [256, 400, 128], P('dom', 'cls')
Inputs may be any that keep to these rules, and one draw needn't show every extreme that they name: `class_ids`: each particle's row names 3 different classes and every class is named by some row; only the first counts entries of a row are significant.
All inputs are finite; a program needn't handle non-finite values.
Results may differ from a plain program's by a relative error of at most 0.0012.
Values may be sent and summed in bfloat16 or wider, within the bound.
No kernel may reach another device: no remote copies, remote signals or barrier semaphores. Data moves between devices by JAX's collectives and lax.ppermute only.
A program may use at most 128 MiB of HBM per device.

v0:
```python
import math

import jax
import jax.numpy as jnp
from jax import lax
from jax.sharding import PartitionSpec as P


def angle_table(angles):
    harmonic = jnp.arange(angles, dtype=jnp.int32)
    product = harmonic[:, None] * harmonic[None, :] % angles
    phase_angle = product.astype(jnp.float32) * (2.0 * math.pi / angles)
    return jnp.stack([jnp.cos(phase_angle), -jnp.sin(phase_angle)]).astype(jnp.bfloat16)


def real_form(references, cycles):
    real_part = references[:, :, :cycles]
    imag_part = references[:, :, cycles:]
    swapped = jnp.concatenate([-imag_part, real_part], axis=2)
    return jnp.concatenate([references, swapped], axis=1)


def on_device(particles, references, class_ids, counts, shift_ids, weights):
    cls_index = lax.axis_index("cls")
    angles = references.shape[0]
    class_count = references.shape[1]
    cycle_parts = references.shape[2]
    cycles = cycle_parts // 2
    shifts = particles.shape[2]
    list_length = class_ids.shape[1]
    all_images, all_ids, all_counts, all_shifts, all_weights = (
        lax.all_gather(particles, "cls", axis=1, tiled=True),
        lax.all_gather(class_ids, "cls", axis=0, tiled=True),
        lax.all_gather(counts, "cls", axis=0, tiled=True),
        lax.all_gather(shift_ids, "cls", axis=0, tiled=True),
        lax.all_gather(weights, "cls", axis=0, tiled=True),
    )
    group_rows = all_images.shape[1]
    table_rows = angle_table(angles)
    stacked = real_form(references, cycles)
    scale = 1.0 / math.sqrt(2.0 * cycles * angles)
    block_rows_each = 4

    def score_block(block_index):
        block = lax.dynamic_slice_in_dim(
            all_images, block_index * block_rows_each, block_rows_each, 1
        )
        flat_block = block.reshape(angles, block_rows_each * shifts, cycle_parts)
        products = jnp.einsum(
            "mnc,mqc->mnq", flat_block, stacked, preferred_element_type=jnp.float32
        )
        rounded = products.astype(jnp.bfloat16).reshape(
            angles, block_rows_each * shifts, 2, class_count
        )
        scores = jnp.einsum(
            "mnk,mp->nkp", rounded[:, :, 0], table_rows[0], preferred_element_type=jnp.float32
        )
        scores = scores + jnp.einsum(
            "mnk,mp->nkp", rounded[:, :, 1], table_rows[1], preferred_element_type=jnp.float32
        )
        scores = scores * scale
        return jnp.max(scores.reshape(block_rows_each, shifts, class_count, angles), axis=(1, 3))

    block_indices = jnp.arange(group_rows // block_rows_each, dtype=jnp.int32)
    best_scores = lax.map(score_block, block_indices).reshape(group_rows, class_count)
    local_ids = all_ids - cls_index * class_count
    valid_mask = jnp.arange(list_length, dtype=jnp.int32)[None, :] < all_counts[:, None]
    kept = jnp.where(valid_mask, all_weights, jnp.zeros_like(all_weights))
    class_hit = local_ids[:, :, None] == jnp.arange(class_count, dtype=jnp.int32)[None, None, :]
    selection = jnp.where(class_hit, kept[:, :, None], jnp.zeros((), jnp.bfloat16))
    shift_hit = (
        all_shifts[:, :, None] == jnp.arange(shifts, dtype=jnp.int32)[None, None, :]
    ).astype(jnp.bfloat16)
    mixing = jnp.einsum("ijk,ijs->isk", selection, shift_hit, preferred_element_type=jnp.float32)
    mixing = mixing.astype(jnp.bfloat16).reshape(group_rows * shifts, class_count)
    flat_images = all_images.reshape(angles, group_rows * shifts, cycle_parts)
    class_sums = lax.psum_scatter(
        jnp.einsum("nk,mnc->mkc", mixing, flat_images, preferred_element_type=jnp.float32),
        "dom",
        scatter_dimension=0,
        tiled=True,
    )
    totals = lax.psum(jnp.sum(selection.astype(jnp.float32), axis=(0, 1)), "dom")
    class_means = class_sums / jnp.maximum(totals, 1.0)[None, :, None]
    return (best_scores, class_means)


def solution(mesh):
    return jax.shard_map(
        on_device,
        mesh=mesh,
        in_specs=(
            P(None, ("dom", "cls"), None, None),
            P(None, "cls", None),
            P(("dom", "cls"), None),
            P(("dom", "cls")),
            P(("dom", "cls"), None),
            P(("dom", "cls"), None),
        ),
        out_specs=(P("dom", "cls"), P("dom", "cls", None)),
        check_vma=False,
    )
```

profile of v0, /device:TPU:8, one launch (start us, length us, event | category | flops | bytes accessed | tf_op | source)
XLA Modules:
  0.0 400.1 jit_solution(16314184417082529820)
XLA Ops:
  7.2 3.8 copy.57
  11.1 4.0 %copy.60 = bf16[256,50,128]{2,1,0:T(8,128)(2,1)} copy(bf16[256,50,128]{2,0,1:T(8,128)(2,1)S(1)} %copy-done.1) | data formatting | bytes 6553600 | tf_op args[1]
  15.2 11.9 %all-gather.1 = s32[8,4,3]{2,1,0:T(4,128)S(1)} all-gather(s32[1,4,3]{2,1,0:T(4,128)S(1)} %bitcast.60), channel_id=1, replica_groups=mesh['dom'=32,'cls'=8] {'cls'}, dimensions={0}, use_global_device_ids=true | all-gather | bytes 432 | tf_op jit(solution)/shard_map/all_gather | solution.py:33
  27.3 9.5 %all-gather.2 = bf16[8,4,3]{2,1,0:T(4,128)(2,1)S(1)} all-gather(bf16[1,4,3]{2,1,0:T(4,128)(2,1)S(1)} %bitcast.62), channel_id=1, replica_groups=mesh['dom'=32,'cls'=8] {'cls'}, dimensions={0}, use_global_device_ids=true | all-gather | bytes 216 | tf_op jit(solution)/shard_map/all_gather | solution.py:36
  38.4 7.1 %all-reduce = s32[32]{0:T(128)S(1)} all-reduce(s32[32]{0:T(128)S(1)} %dynamic-update-slice), channel_id=1, replica_groups=mesh['dom'=32,'cls'=8] {'cls'}, use_global_device_ids=true, to_apply=%add | all-reduce | flops 32 | bytes 256
  45.8 77.4 %psum.7 = f32[50]{0:T(128)S(1)} all-reduce(f32[50]{0:T(128)S(1)} %convert_reduce_fusion), channel_id=1, replica_groups=mesh['dom'=32,'cls'=8] {'dom'}, use_global_device_ids=true, to_apply=%region_6.7 | all-reduce | flops 50 | bytes 400 | tf_op jit(solution)/shard_map/psum | solution.py:83
  123.2 12.9 %all-gather = s32[8,4,3]{2,1,0:T(4,128)S(1)} all-gather(s32[1,4,3]{2,1,0:T(4,128)S(1)} %bitcast.61), channel_id=1, replica_groups=mesh['dom'=32,'cls'=8] {'cls'}, dimensions={0}, use_global_device_ids=true | all-gather | bytes 432 | tf_op jit(solution)/shard_map/all_gather | solution.py:35
  136.1 1.1 negate_convert_fusion
  137.6 4.8 %slice_negate_fusion = (bf16[256,50,64]{2,1,0:T(8,128)(2,1)S(1)}, bf16[256,50,64]{2,1,0:T(8,128)(2,1)S(1)}) fusion(bf16[256,50,128]{2,1,0:T(8,128)(2,1)} %copy.60), kind=kLoop, calls=%fused_computation.16 | loop fusion | flops 819200 | bytes 6553600 | tf_op jit(solution)/shard_map/neg | solution.py:19
  142.5 6.5 %maximum_maximum_fusion = bf16[256,100,128]{2,1,0:T(8,128)(2,1)} fusion(bf16[256,50,64]{2,1,0:T(8,128)(2,1)S(1)} %get-tuple-element.70, bf16[256,50,64]{2,1,0:T(8,128)(2,1)S(1)} %get-tuple-element.69, bf16[256,50,128]{2,1,0:T(8,128)(2,1)S(1)} %copy-done), kind=kLoop, calls=%fused_computation.15 | loop fusion | flops 19660800 | bytes 13107200 | tf_op jit(solution)/shard_map/concatenate | solution.py:20
  149.0 20.6 %fusion.12 = f32[256,50,128]{2,1,0:T(8,128)} fusion(bf16[256,32,9,128]{3,0,2,1:T(8,128)(2,1)} %all-gather.5.cloned.1.call-done, bf16[32,9,50]{2,1,0:T(8,128)(2,1)S(1)} %convolution_convert_fusion), kind=kOutput, calls=%fused_computation.17 | convolution fusion | flops 943718400 | bytes 25456768 | tf_op jit(solution)/shard_map/nk,mnc->mkc/dot_general | solution.py:78
  169.6 144.3 %while.10 = (s32[]{:T(128)}, f32[8,4,50]{2,1,0:T(4,128)S(1)}, s32[8]{0:T(128)S(1)}, bf16[256,32,9,128]{3,0,2,1:T(8,128)(2,1)}, bf16[256,100,128]{2,1,0:T(8,128)(...) while((s32[]{:T(128)}, f32[8,4,50]{2,1,0:T(4,128)S(1)}, ...), condition=%wide.region_3.4_spmd, body=%wide.region_0.3_spmd.sunk | while | flops 710092608 | bytes 29099100 | solution.py:65
  171.1 1.8 constant_dynamic-slice_fusion.2
  172.9 8.4 %fusion.44 = bf16[256,36,100]{2,1,0:T(8,128)(2,1)S(1)} fusion(bf16[256,100,128]{2,1,0:T(8,128)(2,1)} %get-tuple-element.140, bf16[256,36,128]{2,0,1:T(8,128)(2,1)S(1)} %bitcast.54), kind=kOutput, calls=%fused_computation.2.clone.1 | convolution fusion | flops 236851200 | bytes 10756096 | tf_op jit(solution)/shard_map/while/body/eval_jaxpr/mnc,mqc->mnq/dot_general | solution.py:49
  181.3 3.9 copy.101
  185.1 1.7 fusion.45
  189.2 1.8 constant_dynamic-slice_fusion.2
  191.0 8.2 %fusion.44 = bf16[256,36,100]{2,1,0:T(8,128)(2,1)S(1)} fusion(bf16[256,100,128]{2,1,0:T(8,128)(2,1)} %get-tuple-element.140, bf16[256,36,128]{2,0,1:T(8,128)(2,1)S(1)} %bitcast.54), kind=kOutput, calls=%fused_computation.2.clone.1 | convolution fusion | flops 236851200 | bytes 10756096 | tf_op jit(solution)/shard_map/while/body/eval_jaxpr/mnc,mqc->mnq/dot_general | solution.py:49
  199.2 3.9 copy.101
  203.1 1.7 fusion.45
  207.2 1.8 constant_dynamic-slice_fusion.2
  209.0 8.2 %fusion.44 = bf16[256,36,100]{2,1,0:T(8,128)(2,1)S(1)} fusion(bf16[256,100,128]{2,1,0:T(8,128)(2,1)} %get-tuple-element.140, bf16[256,36,128]{2,0,1:T(8,128)(2,1)S(1)} %bitcast.54), kind=kOutput, calls=%fused_computation.2.clone.1 | convolution fusion | flops 236851200 | bytes 10756096 | tf_op jit(solution)/shard_map/while/body/eval_jaxpr/mnc,mqc->mnq/dot_general | solution.py:49
  217.2 3.9 copy.101
  221.1 1.7 fusion.45
  225.1 1.9 constant_dynamic-slice_fusion.2
  227.0 8.3 %fusion.44 = bf16[256,36,100]{2,1,0:T(8,128)(2,1)S(1)} fusion(bf16[256,100,128]{2,1,0:T(8,128)(2,1)} %get-tuple-element.140, bf16[256,36,128]{2,0,1:T(8,128)(2,1)S(1)} %bitcast.54), kind=kOutput, calls=%fused_computation.2.clone.1 | convolution fusion | flops 236851200 | bytes 10756096 | tf_op jit(solution)/shard_map/while/body/eval_jaxpr/mnc,mqc->mnq/dot_general | solution.py:49
  235.3 3.9 copy.101
  239.1 1.7 fusion.45
  241.2 0.6 multiply_reduce_fusion.2
  243.1 1.8 constant_dynamic-slice_fusion.2
  245.0 8.2 %fusion.44 = bf16[256,36,100]{2,1,0:T(8,128)(2,1)S(1)} fusion(bf16[256,100,128]{2,1,0:T(8,128)(2,1)} %get-tuple-element.140, bf16[256,36,128]{2,0,1:T(8,128)(2,1)S(1)} %bitcast.54), kind=kOutput, calls=%fused_computation.2.clone.1 | convolution fusion | flops 236851200 | bytes 10756096 | tf_op jit(solution)/shard_map/while/body/eval_jaxpr/mnc,mqc->mnq/dot_general | solution.py:49
  253.2 3.9 copy.101
  257.1 1.7 fusion.45
  261.1 1.8 constant_dynamic-slice_fusion.2
  263.0 8.2 %fusion.44 = bf16[256,36,100]{2,1,0:T(8,128)(2,1)S(1)} fusion(bf16[256,100,128]{2,1,0:T(8,128)(2,1)} %get-tuple-element.140, bf16[256,36,128]{2,0,1:T(8,128)(2,1)S(1)} %bitcast.54), kind=kOutput, calls=%fused_computation.2.clone.1 | convolution fusion | flops 236851200 | bytes 10756096 | tf_op jit(solution)/shard_map/while/body/eval_jaxpr/mnc,mqc->mnq/dot_general | solution.py:49
  271.2 3.9 copy.101
  275.1 1.7 fusion.45
  279.1 1.8 constant_dynamic-slice_fusion.2
  280.9 8.3 %fusion.44 = bf16[256,36,100]{2,1,0:T(8,128)(2,1)S(1)} fusion(bf16[256,100,128]{2,1,0:T(8,128)(2,1)} %get-tuple-element.140, bf16[256,36,128]{2,0,1:T(8,128)(2,1)S(1)} %bitcast.54), kind=kOutput, calls=%fused_computation.2.clone.1 | convolution fusion | flops 236851200 | bytes 10756096 | tf_op jit(solution)/shard_map/while/body/eval_jaxpr/mnc,mqc->mnq/dot_general | solution.py:49
  289.2 3.9 copy.101
  293.1 1.7 fusion.45
  297.1 1.8 constant_dynamic-slice_fusion.2
  298.9 8.3 %fusion.44 = bf16[256,36,100]{2,1,0:T(8,128)(2,1)S(1)} fusion(bf16[256,100,128]{2,1,0:T(8,128)(2,1)} %get-tuple-element.140, bf16[256,36,128]{2,0,1:T(8,128)(2,1)S(1)} %bitcast.54), kind=kOutput, calls=%fused_computation.2.clone.1 | convolution fusion | flops 236851200 | bytes 10756096 | tf_op jit(solution)/shard_map/while/body/eval_jaxpr/mnc,mqc->mnq/dot_general | solution.py:49
  307.2 3.9 copy.101
  311.1 1.7 fusion.45
  313.9 77.6 %reduce-scatter.2.cloned.1.call-done = f32[8,50,128]{2,1,0:T(8,128)} async-done(((f32[256,50,128]{2,1,0:T(8,128)}), f32[8,50,128]{2,1,0:T(8,128)}) %reduce-scatter.2.cloned.1.call-update) | async-done | bytes 204816 | tf_op jit(solution)/shard_map/reduce_scatter | solution.py:77
  391.5 1.0 broadcast_divide_fusion
  392.5 0.7 copy.70
  (83 shorter events, 14.6 us)
Async XLA Ops:
  7.2 4.0 copy-start.1
  7.2 141.8 %all-gather.5.cloned.1.call-start = ((), (), s32[]{:S(2)}) async-start(), calls=%async_computation.1 | async-start | bytes 21233664 | tf_op jit(solution)/shard_map/all_gather | solution.py:32
  11.0 4.2 %copy-start.2 = (s32[4,3]{1,0:T(4,128)S(1)}, s32[4,3]{1,0:T(4,128)}, u32[]{:S(2)}) copy-start(s32[4,3]{1,0:T(4,128)} %param.10) | copy-start | bytes 148
  11.0 16.2 %copy-start.4 = (bf16[4,3]{1,0:T(4,128)(2,1)S(1)}, bf16[4,3]{1,0:T(4,128)(2,1)}, u32[]{:S(2)}) copy-start(bf16[4,3]{1,0:T(4,128)(2,1)} %param.13) | copy-start | bytes 76
  11.0 25.8 %copy-start.7 = (u32[256]{0:T(256)S(1)}, u32[256]{0:T(256)}, u32[]{:S(2)}) copy-start(u32[256]{0:T(256)} %constant.57) | copy-start | bytes 3076
  11.0 27.1 %copy-start.6 = (s32[4]{0:T(128)S(1)}, s32[4]{0:T(128)}, u32[]{:S(2)}) copy-start(s32[4]{0:T(128)} %param.11) | copy-start | bytes 52
  11.1 112.1 %copy-start.3 = (s32[4,3]{1,0:T(4,128)S(1)}, s32[4,3]{1,0:T(4,128)}, u32[]{:S(2)}) copy-start(s32[4,3]{1,0:T(4,128)} %param.12) | copy-start | bytes 148
  11.1 380.4 %reduce-scatter.2.cloned.1.call-start = ((), (), s32[]{:S(2)}) async-start(), calls=%async_computation.2 | async-start | bytes 7569408 | tf_op jit(solution)/shard_map/reduce_scatter | solution.py:77
  137.6 4.8 %copy-start = (bf16[256,50,128]{2,1,0:T(8,128)(2,1)S(1)}, bf16[256,50,128]{2,1,0:T(8,128)(2,1)}, u32[]{:S(2)}) copy-start(bf16[256,50,128]{2,1,0:T(8,128)(2,1)} %copy.60) | copy-start | bytes 9830404
  313.9 79.4 %copy-start.5 = (f32[8,4,50]{2,1,0:T(4,128)}, f32[8,4,50]{2,1,0:T(4,128)S(1)}, u32[]{:S(2)}) copy-start(f32[8,4,50]{2,1,0:T(4,128)S(1)} %get-tuple-element.34) | copy-start | bytes 19204
Sparse Core Ops, SparseCore 0:
  11.1 98.9 all-gather.4
  169.7 221.7 reduce-scatter.1
where the time goes:
time: 401 us; the launch traced here: 400 us
  blocking collectives  119 us (30%)
  matrix products  95.5 us (24%)
  waiting for transfers between devices  77.7 us (19%)
  local copies, waits for them, and re-layouts  73.6 us (18%)
  between operations  14.9 us (4%)
  other arithmetic  13.8 us (3%)
  loops' own time  5.81 us (1%)
    reduce_scatter x1, waiting for transfers between devices, on_device(): lax.psum_scatter(jnp.einsum('nk,mnc->mkc', mixing, flat_images, preferred...  77.6 us
    psum x1, blocking collectives, on_device(): lax.psum(jnp.sum(selection.astype(jnp.float32), axis=(0, 1)), 'dom')  77.4 us
    dot_general x8, matrix products, score_block(): jnp.einsum('mnc,mqc->mnq', flat_block, stacked, preferred_element_type=jn...  66.3 us
    convert_element_type x8, local copies, waits for them, and re-layouts, score_block(): products.astype(jnp.bfloat16)  30.8 us
    dot_general x1, matrix products, on_device(): jnp.einsum('nk,mnc->mkc', mixing, flat_images, preferred_element_type=jnp...  20.6 us
    dynamic_slice x8, local copies, waits for them, and re-layouts, score_block(): lax.dynamic_slice_in_dim(all_images, block_index * block_rows_each, block...  14.7 us
    slice x8, local copies, waits for them, and re-layouts, score_block(): rounded[:, :, 1]  13.4 us
    all_gather x1, blocking collectives, on_device(): lax.all_gather(shift_ids, 'cls', axis=0, tiled=True)  12.9 us
  transfers between devices with their start and end apart: 2, of which 1 were waited for; matrix products, arithmetic and copies ran while one was open for 39% of the time, Pallas kernels for 0%

commit v1 on v0

v1 whole, which is shorter than its diff:
```python
import functools
import math

import jax
import jax.numpy as jnp
from jax import lax
from jax.experimental import pallas as pl
from jax.experimental.pallas import tpu as pltpu
from jax.sharding import PartitionSpec as P


CHUNK = 16
LANES = 128


def folded_table(angles):
    half = angles // 2
    index = jnp.arange(half, dtype=jnp.int32)
    product = index[:, None] * index[None, :] % angles
    phase = product.astype(jnp.float32) * (2.0 * math.pi / angles)
    edge = (index[:, None] == 0) | (index[None, :] == 0)
    cosine = jnp.cos(phase)
    sine = jnp.where(edge, 0.0, -jnp.sin(phase))
    alternate = jnp.where(index % 2 == 0, 1.0, -1.0)
    nyquist = jnp.where(index[None, :] == 0, alternate[:, None], 0.0)
    last = jnp.concatenate([alternate, jnp.where(index == 0, 1.0, 0.0)])
    rows = [
        jnp.concatenate([cosine, nyquist], axis=1),
        jnp.concatenate([jnp.zeros_like(sine), sine], axis=1),
        jnp.broadcast_to(last[None, :], (8, angles)),
    ]
    return jnp.concatenate(rows, axis=0).astype(jnp.bfloat16)


def score_kernel(scale, rows, shifts, xa, xb, xc, sa, sb, sc, table_ref, out_ref, left_ref, fa, fb, folded):
    step_index = pl.program_id(0)
    lanes = sa.shape[1]
    half = folded.shape[0] // (2 * rows * (lanes // LANES))
    plane = 2 * rows * half
    cycles = LANES // 2
    lane = lax.broadcasted_iota(jnp.int32, (1, LANES), 1)
    sign = jnp.where(lane < cycles, 1.0, -1.0)
    fa[...] = xa[...].astype(jnp.float32)
    fb[pl.ds(0, CHUNK * rows), :] = xb[...].astype(jnp.float32)
    fb[pl.ds(CHUNK * rows, 2 * rows), :] = xc[...].astype(jnp.float32)
    paired = jnp.where(step_index == 0, 0.0, 1.0)
    for t in range(CHUNK):
        a = fa[pl.ds(t * rows, rows), :]
        b = fb[pl.ds((CHUNK - t) * rows, rows), :]
        a_turned = pltpu.roll(a, cycles, 1) * sign
        b_turned = pltpu.roll(b, cycles, 1) * (-sign)
        if t == 0:
            b_turned = b_turned * paired + b * (1.0 - paired)
            a_turned = a_turned * paired
            b = b * paired
        left_ref[pl.ds(0, rows), pl.ds(0, LANES)] = a
        left_ref[pl.ds(0, rows), pl.ds(LANES, LANES)] = b
        left_ref[pl.ds(rows, rows), pl.ds(0, LANES)] = a_turned
        left_ref[pl.ds(rows, rows), pl.ds(LANES, LANES)] = b_turned
        left = left_ref[...].astype(jnp.bfloat16)
        mirrored = sc[0] if t == 0 else sb[CHUNK - t]
        right = jnp.concatenate([sa[t], mirrored], axis=1)
        products = lax.dot_general(
            left, right, (((1,), (1,)), ((), ())), preferred_element_type=jnp.float32
        )
        for v in range(2 * rows // 8):
            for part in range(lanes // LANES):
                folded[pl.ds(part * plane + v * 8 * half + step_index * CHUNK + t, 8, stride=half), :] = products[
                    v * 8 : v * 8 + 8, part * LANES : (part + 1) * LANES
                ]

    @pl.when(step_index == pl.num_programs(0) - 1)
    def _():
        table = table_ref[...]
        each = rows // shifts
        group = 2 * LANES // lanes

        def column(n, part):
            even = folded[pl.ds(pl.multiple_of(part * plane + n * half, half), half), :]
            odd = folded[pl.ds(pl.multiple_of(part * plane + (rows + n) * half, half), half), :]
            return jnp.concatenate([even, odd], axis=0).astype(jnp.bfloat16)

        def one_shift(s, best):
            better = []
            for q in range(each // group):
                columns = [
                    column(s * each + i, part)
                    for i in range(group * q, group * q + group)
                    for part in range(lanes // LANES)
                ]
                turned = jnp.dot(table, jnp.concatenate(columns, axis=1), preferred_element_type=jnp.float32)
                both = turned[:half] + jnp.abs(turned[half : 2 * half])
                top = jnp.max(both.reshape(half // 8, 8, group * lanes), axis=0)
                top = jnp.maximum(top, turned[2 * half :])
                better.append(jnp.maximum(best[q], top))
            return tuple(better)

        start = tuple(jnp.full((8, group * lanes), -jnp.inf, jnp.float32) for _ in range(each // group))
        best = lax.fori_loop(0, shifts, one_shift, start)
        for q in range(each // group):
            top = jnp.max(best[q], axis=0, keepdims=True) * scale
            for i in range(group):
                out_ref[group * q + i : group * q + i + 1, :] = top[:, i * lanes : (i + 1) * lanes]


def best_of_group(lower, upper, upper_offset, stacked, table, shifts, rows, scale):
    angles, lanes, cycle_parts = stacked.shape
    half = angles // 2
    steps = half // CHUNK
    each = rows // shifts
    flops = 2 * half * 2 * rows * 2 * cycle_parts * lanes + 2 * rows * lanes * angles * (angles + 8)
    return pl.pallas_call(
        functools.partial(score_kernel, scale, rows, shifts),
        grid=(steps,),
        in_specs=[
            pl.BlockSpec((CHUNK * rows, cycle_parts), lambda j: (j, 0)),
            pl.BlockSpec((CHUNK * rows, cycle_parts), lambda j: (upper_offset // CHUNK + steps - 1 - j, 0)),
            pl.BlockSpec(
                (2 * rows, cycle_parts),
                lambda j: ((upper_offset + jnp.where(j == 0, 0, half - CHUNK * j)) // 2, 0),
            ),
            pl.BlockSpec((CHUNK, lanes, cycle_parts), lambda j: (j, 0, 0)),
            pl.BlockSpec((CHUNK, lanes, cycle_parts), lambda j: (2 * steps - 1 - j, 0, 0)),
            pl.BlockSpec((1, lanes, cycle_parts), lambda j: (jnp.where(j == 0, half, angles - CHUNK * j), 0, 0)),
            pl.BlockSpec((angles + 8, angles), lambda j: (0, 0)),
        ],
        out_specs=pl.BlockSpec((each, lanes), lambda j: (0, 0)),
        out_shape=jax.ShapeDtypeStruct((each, lanes), jnp.float32),
        scratch_shapes=[
            pltpu.VMEM((2 * rows, 2 * cycle_parts), jnp.float32),
            pltpu.VMEM((CHUNK * rows, cycle_parts), jnp.float32),
            pltpu.VMEM(((CHUNK + 2) * rows, cycle_parts), jnp.float32),
            pltpu.VMEM((2 * rows * half * (lanes // LANES), LANES), jnp.float32),
        ],
        compiler_params=pltpu.CompilerParams(vmem_limit_bytes=48 * 1024 * 1024),
        cost_estimate=pl.CostEstimate(flops=6 * flops, bytes_accessed=30_000_000, transcendentals=0),
        name="score",
    )(lower, upper, upper, stacked, stacked, stacked, table)


def on_device(particles, references, class_ids, counts, shift_ids, weights):
    cls_index = lax.axis_index("cls")
    core = cls_index % 2
    row = cls_index // 2
    angles, own, shifts, cycle_parts = particles.shape
    class_count = references.shape[1]
    list_length = class_ids.shape[1]
    half = angles // 2
    rows = shifts * own
    doms = 32
    chips = 4
    scale = 1.0 / math.sqrt(1.0 * cycle_parts * angles)

    def along(value, step):
        pairs = [(y * 2 + c, (y + step) % chips * 2 + c) for y in range(chips) for c in range(2)]
        return lax.ppermute(value, "cls", pairs)

    def across(value):
        return lax.ppermute(value, "cls", [(i, i ^ 1) for i in range(2 * chips)])

    native = jnp.transpose(particles, (0, 2, 1, 3))
    flat = native.reshape(angles * rows, cycle_parts)
    lower, upper = flat[: half * rows], flat[half * rows :]

    lower_before = along(lower, 1)
    upper_after = along(upper, -1)
    upper_before = along(upper, 1)
    lower_after = along(lower, -1)
    lower_far = along(lower_before, 1)
    upper_far = along(upper_after, -1)

    mate = across(references)
    pad = ((0, 0), (0, LANES // 2 - class_count), (0, 0))
    stacked = jnp.concatenate([jnp.pad(references, pad), jnp.pad(mate, pad)], axis=1)
    table = folded_table(angles)
    score = functools.partial(best_of_group, stacked=stacked, table=table, shifts=shifts, rows=rows, scale=scale)

    listings = own * list_length
    padded = 16
    listed_shift = shift_ids.reshape(listings)
    listed_image = jnp.arange(listings, dtype=jnp.int32) // list_length
    pick = (listed_shift[:, None, None] == jnp.arange(shifts, dtype=jnp.int32)[None, :, None]) & (
        listed_image[:, None, None] == jnp.arange(own, dtype=jnp.int32)[None, None, :]
    )
    pick = jnp.pad(pick.astype(jnp.bfloat16), ((0, padded - listings), (0, 0), (0, 0)))
    listed = jnp.einsum("lsi,msic->mlc", pick, native, preferred_element_type=jnp.float32).astype(jnp.bfloat16)
    valid = jnp.arange(list_length, dtype=jnp.int32)[None, :] < counts[:, None]
    kept = jnp.where(valid, weights, jnp.zeros_like(weights)).reshape(1, listings)
    flat_ids = class_ids.reshape(1, listings)
    notes = jnp.concatenate(
        [(flat_ids // 16).astype(jnp.bfloat16), (flat_ids % 16).astype(jnp.bfloat16), kept], axis=0
    )
    notes = jnp.pad(notes, ((listings, padded - listings - 3), (0, cycle_parts - listings)))
    payload = (listed + notes[None]).reshape(doms, angles // doms, padded, cycle_parts)
    arrived = lax.all_to_all(payload, "dom", 0, 0, tiled=True)
    noted = arrived[:, 0, listings : listings + 3, :listings]
    ids = noted[:, 0].astype(jnp.int32) * 16 + noted[:, 1].astype(jnp.int32)
    classes = 2 * chips * class_count
    hit = ids[None] == jnp.arange(classes, dtype=jnp.int32)[:, None, None]
    mixing = jnp.where(hit, noted[:, 2][None], jnp.zeros((), jnp.bfloat16))
    totals = jnp.sum(mixing.astype(jnp.float32), axis=(1, 2))
    mixing = jnp.pad(mixing, ((0, 0), (0, 0), (0, padded - listings)))
    sums = jnp.einsum("ksl,smlc->kmc", mixing, arrived, preferred_element_type=jnp.float32)
    depth = angles // doms
    sums = sums.reshape(chips, 2, class_count, depth, cycle_parts)
    totals = jnp.pad(totals.reshape(chips, 2, 1, 1, class_count), ((0, 0), (0, 0), (0, 0), (0, depth - 1), (0, cycle_parts - class_count)))
    sums = jnp.concatenate([sums, totals], axis=2)
    mine = lax.dynamic_index_in_dim(sums, core, 1, keepdims=False)
    other = lax.dynamic_index_in_dim(sums, 1 - core, 1, keepdims=False)
    pair_sums = mine + across(other)
    total = lax.dynamic_index_in_dim(pair_sums, row, 0, keepdims=False)
    for step in range(1, chips):
        block = lax.dynamic_index_in_dim(pair_sums, (row + step) % chips, 0, keepdims=False)
        total = total + along(block, step)
    weight_sums = total[class_count, 0, :class_count]
    class_means = total[:class_count] / jnp.maximum(weight_sums, 1.0)[:, None, None]
    class_means = jnp.transpose(class_means, (1, 0, 2))

    own_best = score(flat, flat, half)
    after_best = score(lower_after, upper_after, 0)
    before_best = score(lower_before, upper_before, 0)
    far_best = score(lower_far, upper_far, 0)
    best = jnp.stack([own_best, after_best, far_best, before_best])
    kept_best = best[:, :, :class_count]
    sent_best = across(best[:, :, LANES // 2 : LANES // 2 + class_count])
    first = jnp.where(core == 0, kept_best, sent_best)
    second = jnp.where(core == 0, sent_best, kept_best)
    by_chip = jnp.stack([first, second], axis=1)
    by_chip = jnp.roll(by_chip, row, axis=0)
    best_scores = by_chip.reshape(2 * chips * own, class_count)
    return (best_scores, class_means)


def solution(mesh):
    return jax.shard_map(
        on_device,
        mesh=mesh,
        in_specs=(
            P(None, ("dom", "cls"), None, None),
            P(None, "cls", None),
            P(("dom", "cls"), None),
            P(("dom", "cls")),
            P(("dom", "cls"), None),
            P(("dom", "cls"), None),
        ),
        out_specs=(P("dom", "cls"), P("dom", "cls", None)),
        check_vma=False,
    )
```

time: 401 us -> 160 us (0.40)
  blocking collectives: 119 us -> 0 us
  matrix products: 95.5 us -> 4.96 us
  local copies, waits for them, and re-layouts: 73.6 us -> 17.7 us
  Pallas kernels: 0 us -> 45.7 us
  starting transfers between devices: 0.08 us -> 25.9 us
  waiting for transfers between devices: 77.7 us -> 53.6 us
  between operations: 14.9 us -> 0.92 us
  loops' own time: 5.81 us -> 0 us
  other arithmetic: 13.8 us -> 8.48 us
    dot_general x26 -> x2, matrix products: 95.5 us -> 4.96 us  [the longest x1 4.04 us: on_device(): jnp.einsum('lsi,msic->mlc', pick, native, preferred_element_type=jnp.floa...]
    reduce_scatter x1 -> x0, waiting for transfers between devices: 77.6 us -> none  [on_device(): lax.psum_scatter(jnp.einsum('nk,mnc->mkc', mixing, flat_images, preferred...]
    psum x1 -> x0, blocking collectives: 77.4 us -> none  [on_device(): lax.psum(jnp.sum(selection.astype(jnp.float32), axis=(0, 1)), 'dom')]
    pallas_call x0 -> x4, Pallas kernels: none -> 45.7 us  [best_of_group(): pl.pallas_call(functools.partial(score_kernel, scale, rows, shifts), grid...]
    all_gather x3 -> x0, blocking collectives: 34.3 us -> none  [the longest x1 12.9 us: on_device(): lax.all_gather(shift_ids, 'cls', axis=0, tiled=True)]
    convert_element_type x8 -> x0, local copies, waits for them, and re-layouts: 30.8 us -> none  [score_block(): products.astype(jnp.bfloat16)]
    all_to_all x0 -> x1, waiting for transfers between devices: none -> 28.5 us  [on_device(): arrived = lax.all_to_all(payload, 'dom', 0, 0, tiled=True)]
    ppermute x0 -> x12, waiting for transfers between devices: none -> 25.1 us  [the longest x9 24.8 us: along(): return lax.ppermute(value, 'cls', pairs)]
  transfers between devices with their start and end apart: 2 -> 13, of which waited for: 1 -> 6; matrix products, arithmetic and copies ran while one was open for 39% -> 14% of each run, Pallas kernels for 0% -> 22%
where the time goes in v1:
time: 160 us; the launch traced here: 157 us
  waiting for transfers between devices  53.6 us (34%)
  Pallas kernels  45.7 us (29%)
  starting transfers between devices  25.9 us (16%)
  local copies, waits for them, and re-layouts  17.7 us (11%)
  other arithmetic  8.48 us (5%)
  matrix products  4.96 us (3%)
    pallas_call x4, Pallas kernels, best_of_group(): pl.pallas_call(functools.partial(score_kernel, scale, rows, shifts), grid...  45.7 us
    all_to_all x1, waiting for transfers between devices, on_device(): arrived = lax.all_to_all(payload, 'dom', 0, 0, tiled=True)  28.5 us
    ppermute x9, waiting for transfers between devices, along(): return lax.ppermute(value, 'cls', pairs)  24.8 us
    ppermute x9, starting transfers between devices, along(): return lax.ppermute(value, 'cls', pairs)  14.5 us
    all_to_all x1, starting transfers between devices, on_device(): arrived = lax.all_to_all(payload, 'dom', 0, 0, tiled=True)  11.3 us
    unnamed x8, local copies, waits for them, and re-layouts  7.23 us
    ppermute x1, local copies, waits for them, and re-layouts, across(): return lax.ppermute(value, 'cls', [(i, i ^ 1) for i in range(2 * chips)])  4.23 us
    dot_general x1, matrix products, on_device(): jnp.einsum('lsi,msic->mlc', pick, native, preferred_element_type=jnp.floa...  4.04 us
  transfers between devices with their start and end apart: 13, of which 6 were waited for; matrix products, arithmetic and copies ran while one was open for 14% of the time, Pallas kernels for 22%

profile of v1, /device:TPU:8, one launch (start us, length us, event | category | flops | bytes accessed | tf_op | source)
XLA Modules:
  0.0 157.4 jit_solution(9956283360864482989)
XLA Ops:
  0.6 0.8 fusion.37
  1.4 0.1 reshape.290
  1.5 0.8 reshape.289
  2.3 0.8 eq.102
  3.0 0.1 iota_compare_fusion.9
  3.1 0.1 broadcast_and_fusion
  3.2 4.0 %fusion.7 = bf16[16,256,128]{2,0,1:T(8,128)(2,1)} fusion(bf16[256,9,4,128]{3,2,1,0:T(4,128)(2,1)} %bitcast.57, bf16[16,128]{1,0:T(8,128)(2,1)S(1)} %select_maximum_fusion.1, pred[12,9,4]{1,0,2:T(8,128)(4,1)S(1)} %broadcast_and_fusion), kind=kOutput, calls=%fused_computation.11 | convolution fusion | flops 38797312 | bytes 3412400 | tf_op jit(solution)/shard_map/lsi,msic->mlc/dot_general | solution.py:186
  7.3 11.3 %all-to-all-start = ((bf16[32,8,16,128]{3,2,1,0:T(8,128)(2,1)}), bf16[32,8,16,128]{3,2,1,0:T(8,128)(2,1)S(1)}, u32[]{:S(2)}, u32[]{:S(2)}) async-start(bf16[32,8,16,128]{3,2,1,0:T(8,128)(2,1)} %bitcast.15), calls=%async_computation | async-start | bytes 2097152 | tf_op jit(solution)/shard_map/all_to_all | solution.py:195
  18.6 0.1 collective-permute-start
  18.7 28.5 %all-to-all-done = bf16[32,8,16,128]{3,2,1,0:T(8,128)(2,1)S(1)} async-done(((bf16[32,8,16,128]{3,2,1,0:T(8,128)(2,1)}), bf16[32,8,16,128]{3,2,1,0:T(8,128)(2,1)S(1)}, u32[]{:S(2)}, u32[]{:S(2)}) %all-to-all-start) | async-done | bytes 1048608 | tf_op jit(solution)/shard_map/all_to_all | solution.py:195
  47.2 0.1 copy.39
  47.3 0.2 convert_reduce_fusion
  47.5 0.1 reshape.293
  47.6 0.2 fusion.11
  47.8 0.9 convolution_bitcast_fusion
  48.7 0.5 copy.36
  49.3 0.1 select_maximum_fusion
  49.4 1.3 copy-done.2
  50.7 1.0 dynamic-slice_bitcast_fusion
  51.6 2.3 %fusion.43 = (bf16[128,9,4,128]{3,2,1,0:T(4,128)(2,1)}, bf16[128,9,4,128]{3,2,1,0:T(4,128)(2,1)}) fusion(bf16[256,9,4,128]{3,2,1,0:T(4,128)(2,1)S(1)} %bitcast.58), kind=kLoop, calls=%fused_computation.95 | loop fusion | bytes 4718592 | tf_op jit(solution)/shard_map/slice | solution.py:163
  53.9 1.6 %collective-permute-start.3 = (bf16[4608,128]{1,0:T(8,128)(2,1)}, bf16[4608,128]{1,0:T(8,128)(2,1)}, u32[]{:S(2)}, u32[]{:S(2)}) collective-permute-start(bf16[4608,128]{1,0:T(8,128)(2,1)} %bitcast.3), channel_id=1, source_target_pairs={{0,2},{1,3},{2,4},{3,5},{4,6},{5,7},{6,0},{7,1},{8,10},{9,11},{10,... | collective-permute-start | bytes 3538952 | tf_op jit(solution)/shard_map/ppermute | solution.py:156
  55.5 0.4 collective-permute-start.2
  55.9 5.9 %copy.30 = bf16[256,50,128]{2,1,0:T(8,128)(2,1)} copy(bf16[256,50,128]{2,0,1:T(8,128)(2,1)} %param.7) | data formatting | bytes 6553600 | tf_op args[1]
  61.8 0.3 cosine_convert_fusion
  62.1 0.3 select_convert_fusion
  62.3 0.1 select_convert_fusion.1
  62.4 1.5 bitcast_add_fusion
  64.0 1.7 %collective-permute-start.11 = (f32[51,8,128]{2,1,0:T(8,128)S(1)}, f32[51,8,128]{2,1,0:T(8,128)S(1)}, u32[]{:S(2)}, u32[]{:S(2)}) collective-permute-start(f32[51,8,128]{2,1,0:T(8,128)S(1)} %get-tuple-element.5), channel_id=1, source_target_pairs={{0,6},{1,7},{2,0},{3,1},{4,2},{5,3},{6,4},{7,5},{8,14},{9,15},{10,... | collective-permute-start | bytes 626696 | tf_op jit(solution)/shard_map/ppermute | solution.py:156
  65.7 1.4 collective-permute-start.10
  67.1 15.9 %collective-permute-done.3.xa = bf16[4608,128]{1,0:T(8,128)(2,1)} collective-permute-done((bf16[4608,128]{1,0:T(8,128)(2,1)}, bf16[4608,128]{1,0:T(8,128)(2,1)}, u32[]{:S(2)}, u32[]{:S(2)}) %collective-permute-start.3) | collective-permute-done | bytes 1179680 | tf_op jit(solution)/shard_map/ppermute | solution.py:156
  83.1 5.2 %collective-permute-start.9 = (f32[51,8,128]{2,1,0:T(8,128)S(1)}, f32[51,8,128]{2,1,0:T(8,128)S(1)}, u32[]{:S(2)}, u32[]{:S(2)}) collective-permute-start(f32[51,8,128]{2,1,0:T(8,128)S(1)} %get-tuple-element.4), channel_id=1, source_target_pairs={{0,2},{1,3},{2,4},{3,5},{4,6},{5,7},{6,0},{7,1},{8,10},{9,11},{10,... | collective-permute-start | bytes 626696 | tf_op jit(solution)/shard_map/ppermute | solution.py:156
  88.3 0.1 collective-permute-start.6
  88.4 2.0 %collective-permute-start.1 = (bf16[4608,128]{1,0:T(8,128)(2,1)}, bf16[4608,128]{1,0:T(8,128)(2,1)S(1)}, u32[]{:S(2)}, u32[]{:S(2)}) collective-permute-start(bf16[4608,128]{1,0:T(8,128)(2,1)} %bitcast.3), channel_id=1, source_target_pairs={{0,6},{1,7},{2,0},{3,1},{4,2},{5,3},{6,4},{7,5},{8,14},{9,15},{10,... | collective-permute-start | bytes 3538952 | tf_op jit(solution)/shard_map/ppermute | solution.py:156
  90.4 3.8 %collective-permute-done.10 = f32[51,8,128]{2,1,0:T(8,128)S(1)} collective-permute-done((f32[51,8,128]{2,1,0:T(8,128)S(1)}, f32[51,8,128]{2,1,0:T(8,128)S(1)}, u32[]{:S(2)}, u32[]{:S(2)}) %collective-permute-start.10) | collective-permute-done | bytes 208928 | tf_op jit(solution)/shard_map/ppermute | solution.py:156
  94.3 2.0 %collective-permute-start.5 = (bf16[4608,128]{1,0:T(8,128)(2,1)S(1)}, bf16[4608,128]{1,0:T(8,128)(2,1)S(1)}, u32[]{:S(2)}, u32[]{:S(2)}) collective-permute-start(bf16[4608,128]{1,0:T(8,128)(2,1)S(1)} %collective-permute-done.2.xb.xc), channel_id=1, source_target_pairs={{0,6},{1,7},{2,0},{3,1},{4,2},{5,3},{6,4},{7,5},{8,14},{9,15},{10,... | collective-permute-start | bytes 3538952 | tf_op jit(solution)/shard_map/ppermute | solution.py:156
  96.3 0.1 fusion.17
  96.4 4.2 %copy.31 = bf16[256,50,128]{2,1,0:T(8,128)(2,1)S(1)} copy(bf16[256,50,128]{2,0,1:T(8,128)(2,1)} %collective-permute-done) | data formatting | bytes 6553600 | tf_op jit(solution)/shard_map/ppermute | solution.py:159
  100.6 4.0 %fusion.2.sa.sb.sc = bf16[256,128,128]{2,1,0:T(8,128)(2,1)} fusion(bf16[256,50,128]{2,1,0:T(8,128)(2,1)S(1)} %copy.31, bf16[256,50,128]{2,1,0:T(8,128)(2,1)S(1)} %copy-done.1), kind=kLoop, calls=%fused_computation.4 | loop fusion | flops 33554432 | bytes 14942208 | tf_op jit(solution)/shard_map/concatenate | solution.py:174
  104.6 11.4 %score.4 = f32[4,128]{1,0:T(4,128)S(1)} custom-call(bf16[9216,128]{1,0:T(8,128)(2,1)S(1)} %bitcast.59, bf16[9216,128]{1,0:T(8,128)(2,1)S(1)} %bitcast.60, bf16[9216,128]{1,0:T(8,128)(2,1)S(1)} %bitcast.61, bf16[256,128,128]{2,1,0:T(8,128)(2,1)} %fusion.2.sa.sb.sc, bf16[256,128,128]{2,1,0:T(8,128)(2,1)} %fusion.2.sa.sb.sc, ...), custom_call_target="tpu_custom_call" | custom-call | flops 7361003520 | bytes 30000000 | tf_op jit(solution)/shard_map/score/pallas_call | solution.py:112
  116.0 3.2 %collective-permute-done.6.xb.xc = bf16[4608,128]{1,0:T(8,128)(2,1)S(1)} collective-permute-done((bf16[4608,128]{1,0:T(8,128)(2,1)}, bf16[4608,128]{1,0:T(8,128)(2,1)S(1)}, u32[]{:S(2)}, u32[]{:S(2)}) %collective-permute-start.6) | collective-permute-done | bytes 1179680 | tf_op jit(solution)/shard_map/ppermute | solution.py:156
  119.2 11.6 %score.7 = f32[4,128]{1,0:T(4,128)S(1)} custom-call(bf16[4608,128]{1,0:T(8,128)(2,1)} %collective-permute-done.3.xa, bf16[4608,128]{1,0:T(8,128)(2,1)S(1)} %collective-permute-done.6.xb.xc, bf16[4608,128]{1,0:T(8,128)(2,1)S(1)} %collective-permute-done.6.xb.xc, bf16[256,128,128]{2,1,0:T(8,128)(2,1)} %fusion.2.sa.sb.sc, ...), custom_call_target="tpu_custom_call" | custom-call | flops 7361003520 | bytes 30000000 | tf_op jit(solution)/shard_map/score/pallas_call | solution.py:112
  130.8 11.4 %score.5 = f32[4,128]{1,0:T(4,128)S(1)} custom-call(bf16[4608,128]{1,0:T(8,128)(2,1)S(1)} %collective-permute-done.1.xa, bf16[4608,128]{1,0:T(8,128)(2,1)S(1)} %collective-permute-done.2.xb.xc, bf16[4608,128]{1,0:T(8,128)(2,1)S(1)} %collective-permute-done.2.xb.xc, bf16[256,128,128]{2,1,0:T(8,128)(2,1)} %fusion.2.sa.sb.sc, ...), custom_call_target="tpu_custom_call" | custom-call | flops 7361003520 | bytes 30000000 | tf_op jit(solution)/shard_map/score/pallas_call | solution.py:112
  142.2 1.8 %collective-permute-done.5.xb.xc = bf16[4608,128]{1,0:T(8,128)(2,1)S(1)} collective-permute-done((bf16[4608,128]{1,0:T(8,128)(2,1)S(1)}, bf16[4608,128]{1,0:T(8,128)(2,1)S(1)}, u32[]{:S(2)}, u32[]{:S(2)}) %collective-permute-start.5) | collective-permute-done | bytes 1179680 | tf_op jit(solution)/shard_map/ppermute | solution.py:156
  144.0 11.4 %score.6 = f32[4,128]{1,0:T(4,128)S(1)} custom-call(bf16[4608,128]{1,0:T(8,128)(2,1)S(1)} %collective-permute-done.4.xa, bf16[4608,128]{1,0:T(8,128)(2,1)S(1)} %collective-permute-done.5.xb.xc, bf16[4608,128]{1,0:T(8,128)(2,1)S(1)} %collective-permute-done.5.xb.xc, bf16[256,128,128]{2,1,0:T(8,128)(2,1)} %fusion.2.sa.sb.sc, ...), custom_call_target="tpu_custom_call" | custom-call | flops 7361003520 | bytes 30000000 | tf_op jit(solution)/shard_map/score/pallas_call | solution.py:112
  155.4 0.1 slice.51
  155.6 0.8 fusion.18
  156.4 0.4 collective-permute-done.7
  156.7 0.6 copy.32
  (32 shorter events, 0.3 us)
Async XLA Ops:
  7.3 39.9 %all-to-all-start = ((bf16[32,8,16,128]{3,2,1,0:T(8,128)(2,1)}), bf16[32,8,16,128]{3,2,1,0:T(8,128)(2,1)S(1)}, u32[]{:S(2)}, u32[]{:S(2)}) async-start(bf16[32,8,16,128]{3,2,1,0:T(8,128)(2,1)} %bitcast.15), calls=%async_computation | async-start | bytes 2097152 | tf_op jit(solution)/shard_map/all_to_all | solution.py:195
  18.6 77.8 %collective-permute-start = (bf16[256,50,128]{2,0,1:T(8,128)(2,1)}, bf16[256,50,128]{2,0,1:T(8,128)(2,1)}, u32[]{:S(2)}, u32[]{:S(2)}) collective-permute-start(bf16[256,50,128]{2,0,1:T(8,128)(2,1)} %param.7), channel_id=1, source_target_pairs={{0,1},{1,0},{2,3},{3,2},{4,5},{5,4},{6,7},{7,6},{8,9},{9,8},{10,11... | collective-permute-start | bytes 9830408 | tf_op jit(solution)/shard_map/ppermute | solution.py:159
  49.3 2.4 %copy-start = (bf16[256,4,9,128]{3,1,2,0:T(4,128)(2,1)S(1)}, bf16[256,4,9,128]{3,1,2,0:T(4,128)(2,1)}, u32[]{:S(2)}) copy-start(bf16[256,4,9,128]{3,1,2,0:T(4,128)(2,1)} %param.6) | copy-start | bytes 7077892
  49.4 1.3 copy-start.2
  51.6 10.8 %collective-permute-start.8 = (f32[4,51,8,128]{3,2,1,0:T(8,128)}, f32[4,51,8,128]{3,2,1,0:T(8,128)}, u32[]{:S(2)}, u32[]{:S(2)}) collective-permute-start(f32[4,51,8,128]{3,2,1,0:T(8,128)} %dynamic-slice_bitcast_fusion), channel_id=1, source_target_pairs={{0,1},{1,0},{2,3},{3,2},{4,5},{5,4},{6,7},{7,6},{8,9},{9,8},{10,11... | collective-permute-start | bytes 2506760 | tf_op jit(solution)/shard_map/ppermute | solution.py:159
  53.9 29.2 %collective-permute-start.3 = (bf16[4608,128]{1,0:T(8,128)(2,1)}, bf16[4608,128]{1,0:T(8,128)(2,1)}, u32[]{:S(2)}, u32[]{:S(2)}) collective-permute-start(bf16[4608,128]{1,0:T(8,128)(2,1)} %bitcast.3), channel_id=1, source_target_pairs={{0,2},{1,3},{2,4},{3,5},{4,6},{5,7},{6,0},{7,1},{8,10},{9,11},{10,... | collective-permute-start | bytes 3538952 | tf_op jit(solution)/shard_map/ppermute | solution.py:156
  55.5 32.8 %collective-permute-start.2 = (bf16[4608,128]{1,0:T(8,128)(2,1)}, bf16[4608,128]{1,0:T(8,128)(2,1)S(1)}, u32[]{:S(2)}, u32[]{:S(2)}) collective-permute-start(bf16[4608,128]{1,0:T(8,128)(2,1)} %bitcast.4), channel_id=1, source_target_pairs={{0,6},{1,7},{2,0},{3,1},{4,2},{5,3},{6,4},{7,5},{8,14},{9,15},{10,... | collective-permute-start | bytes 3538952 | tf_op jit(solution)/shard_map/ppermute | solution.py:156
  64.0 24.4 %collective-permute-start.11 = (f32[51,8,128]{2,1,0:T(8,128)S(1)}, f32[51,8,128]{2,1,0:T(8,128)S(1)}, u32[]{:S(2)}, u32[]{:S(2)}) collective-permute-start(f32[51,8,128]{2,1,0:T(8,128)S(1)} %get-tuple-element.5), channel_id=1, source_target_pairs={{0,6},{1,7},{2,0},{3,1},{4,2},{5,3},{6,4},{7,5},{8,14},{9,15},{10,... | collective-permute-start | bytes 626696 | tf_op jit(solution)/shard_map/ppermute | solution.py:156
  65.7 28.5 %collective-permute-start.10 = (f32[51,8,128]{2,1,0:T(8,128)S(1)}, f32[51,8,128]{2,1,0:T(8,128)S(1)}, u32[]{:S(2)}, u32[]{:S(2)}) collective-permute-start(f32[51,8,128]{2,1,0:T(8,128)S(1)} %get-tuple-element.6), channel_id=1, source_target_pairs={{0,4},{1,5},{2,6},{3,7},{4,0},{5,1},{6,2},{7,3},{8,12},{9,13},{10,... | collective-permute-start | bytes 626696 | tf_op jit(solution)/shard_map/ppermute | solution.py:156
  83.1 11.2 %collective-permute-start.9 = (f32[51,8,128]{2,1,0:T(8,128)S(1)}, f32[51,8,128]{2,1,0:T(8,128)S(1)}, u32[]{:S(2)}, u32[]{:S(2)}) collective-permute-start(f32[51,8,128]{2,1,0:T(8,128)S(1)} %get-tuple-element.4), channel_id=1, source_target_pairs={{0,2},{1,3},{2,4},{3,5},{4,6},{5,7},{6,0},{7,1},{8,10},{9,11},{10,... | collective-permute-start | bytes 626696 | tf_op jit(solution)/shard_map/ppermute | solution.py:156
  88.3 30.9 %collective-permute-start.6 = (bf16[4608,128]{1,0:T(8,128)(2,1)}, bf16[4608,128]{1,0:T(8,128)(2,1)S(1)}, u32[]{:S(2)}, u32[]{:S(2)}) collective-permute-start(bf16[4608,128]{1,0:T(8,128)(2,1)} %bitcast.4), channel_id=1, source_target_pairs={{0,2},{1,3},{2,4},{3,5},{4,6},{5,7},{6,0},{7,1},{8,10},{9,11},{10,... | collective-permute-start | bytes 3538952 | tf_op jit(solution)/shard_map/ppermute | solution.py:156
  88.4 42.4 %collective-permute-start.1 = (bf16[4608,128]{1,0:T(8,128)(2,1)}, bf16[4608,128]{1,0:T(8,128)(2,1)S(1)}, u32[]{:S(2)}, u32[]{:S(2)}) collective-permute-start(bf16[4608,128]{1,0:T(8,128)(2,1)} %bitcast.3), channel_id=1, source_target_pairs={{0,6},{1,7},{2,0},{3,1},{4,2},{5,3},{6,4},{7,5},{8,14},{9,15},{10,... | collective-permute-start | bytes 3538952 | tf_op jit(solution)/shard_map/ppermute | solution.py:156
  94.2 48.0 %collective-permute-start.4 = (bf16[4608,128]{1,0:T(8,128)(2,1)}, bf16[4608,128]{1,0:T(8,128)(2,1)S(1)}, u32[]{:S(2)}, u32[]{:S(2)}) collective-permute-start(bf16[4608,128]{1,0:T(8,128)(2,1)} %collective-permute-done.3.xa), channel_id=1, source_target_pairs={{0,2},{1,3},{2,4},{3,5},{4,6},{5,7},{6,0},{7,1},{8,10},{9,11},{10,... | collective-permute-start | bytes 3538952 | tf_op jit(solution)/shard_map/ppermute | solution.py:156
  94.3 49.8 %collective-permute-start.5 = (bf16[4608,128]{1,0:T(8,128)(2,1)S(1)}, bf16[4608,128]{1,0:T(8,128)(2,1)S(1)}, u32[]{:S(2)}, u32[]{:S(2)}) collective-permute-start(bf16[4608,128]{1,0:T(8,128)(2,1)S(1)} %collective-permute-done.2.xb.xc), channel_id=1, source_target_pairs={{0,6},{1,7},{2,0},{3,1},{4,2},{5,3},{6,4},{7,5},{8,14},{9,15},{10,... | collective-permute-start | bytes 3538952 | tf_op jit(solution)/shard_map/ppermute | solution.py:156
  96.4 4.3 %copy-start.1 = (bf16[256,50,128]{2,1,0:T(8,128)(2,1)S(1)}, bf16[256,50,128]{2,1,0:T(8,128)(2,1)}, u32[]{:S(2)}) copy-start(bf16[256,50,128]{2,1,0:T(8,128)(2,1)} %copy.30) | copy-start | bytes 9830404
  155.5 1.2 collective-permute-start.7

commit v2 on v1

v2 whole, which is shorter than its diff:
```python
import functools
import math

import jax
import jax.numpy as jnp
from jax import lax
from jax.experimental import pallas as pl
from jax.experimental.pallas import tpu as pltpu
from jax.sharding import PartitionSpec as P


CHUNK = 16
LANES = 128
WHOLE = pl.BlockSpec(memory_space=pltpu.VMEM)


def folded_table(angles):
    half = angles // 2
    index = jnp.arange(half, dtype=jnp.int32)
    product = index[:, None] * index[None, :] % angles
    phase = product.astype(jnp.float32) * (2.0 * math.pi / angles)
    edge = (index[:, None] == 0) | (index[None, :] == 0)
    cosine = jnp.cos(phase)
    sine = jnp.where(edge, 0.0, -jnp.sin(phase))
    alternate = jnp.where(index % 2 == 0, 1.0, -1.0)
    nyquist = jnp.where(index[None, :] == 0, alternate[:, None], 0.0)
    last = jnp.concatenate([alternate, jnp.where(index == 0, 1.0, 0.0)])
    rows = [
        jnp.concatenate([cosine, nyquist], axis=1),
        jnp.concatenate([jnp.zeros_like(sine), sine], axis=1),
        jnp.broadcast_to(last[None, :], (8, angles)),
    ]
    return jnp.concatenate(rows, axis=0).astype(jnp.bfloat16)


def gather_kernel(sizes, starts, *refs):
    pieces, out_ref, work = refs[: len(sizes)], refs[len(sizes)], refs[len(sizes) + 1]
    total = out_ref.shape[1]
    work[...] = jnp.zeros(work.shape, jnp.float32)

    def chunk(j, carry):
        base = pl.multiple_of(j * CHUNK, CHUNK)
        for size, start, ref in zip(sizes, starts, pieces):
            block = ref[:, pl.ds(base, CHUNK), :].reshape(size * CHUNK, LANES)
            work[pl.ds(start * CHUNK, size * CHUNK), :] = block.astype(jnp.float32)
        for t in range(CHUNK):
            out_ref[base + t] = work[pl.ds(t, total, stride=CHUNK), :].astype(jnp.bfloat16)
        return carry

    lax.fori_loop(0, out_ref.shape[0] // CHUNK, chunk, 0)


def by_harmonic(pieces, starts):
    angles, cycle_parts = pieces[0].shape[1:]
    sizes = tuple(piece.shape[0] for piece in pieces)
    moved = 2 * angles * cycle_parts * (sum(sizes) + LANES)
    return pl.pallas_call(
        functools.partial(gather_kernel, sizes, tuple(starts)),
        in_specs=[WHOLE] * len(pieces),
        out_specs=WHOLE,
        out_shape=jax.ShapeDtypeStruct((angles, LANES, cycle_parts), jnp.bfloat16),
        scratch_shapes=[pltpu.VMEM((LANES * CHUNK, cycle_parts), jnp.float32)],
        compiler_params=pltpu.CompilerParams(vmem_limit_bytes=30 * 1024 * 1024),
        cost_estimate=pl.CostEstimate(flops=0, bytes_accessed=2 * moved, transcendentals=0),
        name="by_harmonic",
    )(*pieces)


def score_kernel(scale, rows, shifts, half, upper_offset, sets, *refs):
    lower, upper = refs[:2]
    stacked = refs[2 : 2 + sets]
    table_ref, out_ref, left_ref, fa, fb, folded = refs[2 + sets :]
    lanes = sets * LANES
    plane = half * 2 * rows
    cycles = LANES // 2
    lane = lax.broadcasted_iota(jnp.int32, (1, LANES), 1)
    sign = jnp.where(lane < cycles, 1.0, -1.0)
    block = CHUNK * rows

    def chunk(j, carry):
        back = upper_offset + half - CHUNK - j * CHUNK
        edge = jnp.where(j == 0, half, 2 * half - CHUNK * j)
        fa[...] = lower[pl.ds(pl.multiple_of(j * block, block), block), :].astype(jnp.float32)
        fb[pl.ds(0, block), :] = upper[pl.ds(pl.multiple_of(back * rows, block), block), :].astype(jnp.float32)
        edge_rows = pl.multiple_of((edge - half + upper_offset) * rows, block)
        fb[pl.ds(block, 2 * rows), :] = upper[pl.ds(edge_rows, 2 * rows), :].astype(jnp.float32)
        paired = jnp.where(j == 0, 0.0, 1.0)
        for t in range(CHUNK):
            a = fa[pl.ds(t * rows, rows), :]
            b = fb[pl.ds((CHUNK - t) * rows, rows), :]
            a_turned = pltpu.roll(a, cycles, 1) * sign
            b_turned = pltpu.roll(b, cycles, 1) * (-sign)
            if t == 0:
                b_turned = b_turned * paired + b * (1.0 - paired)
                a_turned = a_turned * paired
                b = b * paired
            slot = t % left_ref.shape[0]
            left_ref[slot, pl.ds(0, rows), pl.ds(0, LANES)] = a
            left_ref[slot, pl.ds(0, rows), pl.ds(LANES, LANES)] = b
            left_ref[slot, pl.ds(rows, rows), pl.ds(0, LANES)] = a_turned
            left_ref[slot, pl.ds(rows, rows), pl.ds(LANES, LANES)] = b_turned
            m = j * CHUNK + t
            mirror = edge if t == 0 else 2 * half - m
            right = jnp.concatenate(
                [
                    jnp.concatenate([ref[m] for ref in stacked], axis=0),
                    jnp.concatenate([ref[mirror] for ref in stacked], axis=0),
                ],
                axis=1,
            )
            products = lax.dot_general(
                left_ref[slot].astype(jnp.bfloat16),
                right,
                (((1,), (1,)), ((), ())),
                preferred_element_type=jnp.float32,
            )
            for part in range(sets):
                first = pl.multiple_of(part * plane + m * 2 * rows, 8)
                folded[pl.ds(first, 2 * rows), :] = products[:, part * LANES : (part + 1) * LANES]
        return carry

    lax.fori_loop(0, half // CHUNK, chunk, 0)
    table = table_ref[...]
    each = rows // shifts
    group = 2 // sets
    width = 2 * LANES

    def column(n, part):
        even = folded[pl.ds(part * plane + n, half, stride=2 * rows), :]
        odd = folded[pl.ds(part * plane + rows + n, half, stride=2 * rows), :]
        return jnp.concatenate([even, odd], axis=0).astype(jnp.bfloat16)

    def one_shift(s, best):
        better = []
        for q in range(each // group):
            columns = [
                column(s * each + i, part) for i in range(group * q, group * q + group) for part in range(sets)
            ]
            turned = jnp.dot(table, jnp.concatenate(columns, axis=1), preferred_element_type=jnp.float32)
            both = turned[:half] + jnp.abs(turned[half : 2 * half])
            top = jnp.max(both.reshape(half // 8, 8, width), axis=0)
            top = jnp.maximum(top, turned[2 * half :])
            better.append(jnp.maximum(best[q], top))
        return tuple(better)

    start = tuple(jnp.full((8, width), -jnp.inf, jnp.float32) for _ in range(each // group))
    best = lax.fori_loop(0, shifts, one_shift, start)
    for q in range(each // group):
        top = jnp.max(best[q], axis=0, keepdims=True) * scale
        for i in range(group):
            out_ref[group * q + i : group * q + i + 1, :] = top[:, i * lanes : (i + 1) * lanes]


def best_of_group(lower, upper, upper_offset, stacked, table, shifts, rows, scale):
    angles, _, cycle_parts = stacked[0].shape
    half = angles // 2
    each = rows // shifts
    sets = len(stacked)
    lanes = sets * LANES
    flops = 2 * half * 2 * rows * 2 * cycle_parts * lanes + 2 * rows * lanes * angles * (angles + 8)
    return pl.pallas_call(
        functools.partial(score_kernel, scale, rows, shifts, half, upper_offset, sets),
        in_specs=[WHOLE] * (3 + sets),
        out_specs=WHOLE,
        out_shape=jax.ShapeDtypeStruct((each, lanes), jnp.float32),
        scratch_shapes=[
            pltpu.VMEM((4, 2 * rows, 2 * cycle_parts), jnp.float32),
            pltpu.VMEM((CHUNK * rows, cycle_parts), jnp.float32),
            pltpu.VMEM(((CHUNK + 2) * rows, cycle_parts), jnp.float32),
            pltpu.VMEM((sets * 2 * rows * half, LANES), jnp.float32),
        ],
        compiler_params=pltpu.CompilerParams(vmem_limit_bytes=32 * 1024 * 1024),
        cost_estimate=pl.CostEstimate(flops=6 * flops, bytes_accessed=20_000_000, transcendentals=0),
        name="score",
    )(lower, upper, *stacked, table)


def on_device(particles, references, class_ids, counts, shift_ids, weights):
    cls_index = lax.axis_index("cls")
    core = cls_index % 2
    row = cls_index // 2
    angles, own, shifts, cycle_parts = particles.shape
    class_count = references.shape[1]
    list_length = class_ids.shape[1]
    half = angles // 2
    rows = shifts * own
    doms = 32
    chips = 4
    scale = 1.0 / math.sqrt(1.0 * cycle_parts * angles)

    def along(value, step):
        pairs = [(y * 2 + c, (y + step) % chips * 2 + c) for y in range(chips) for c in range(2)]
        return lax.ppermute(value, "cls", pairs)

    def across(value):
        return lax.ppermute(value, "cls", [(i, i ^ 1) for i in range(2 * chips)])

    native = jnp.transpose(particles, (0, 2, 1, 3))
    flat = native.reshape(angles * rows, cycle_parts)

    before = along(flat, 1)
    after = along(flat, -1)
    lower_far = along(before[: half * rows], 1)
    upper_far = along(after[half * rows :], -1)

    class_major = jnp.transpose(references, (1, 0, 2))
    mate = across(class_major)
    stacked = (by_harmonic([class_major, mate], [0, LANES // 2]),)
    table = folded_table(angles)
    score = functools.partial(best_of_group, stacked=stacked, table=table, shifts=shifts, rows=rows, scale=scale)

    listings = own * list_length
    padded = 16
    listed_shift = shift_ids.reshape(listings)
    listed_image = jnp.arange(listings, dtype=jnp.int32) // list_length
    pick = (listed_shift[:, None, None] == jnp.arange(shifts, dtype=jnp.int32)[None, :, None]) & (
        listed_image[:, None, None] == jnp.arange(own, dtype=jnp.int32)[None, None, :]
    )
    pick = jnp.pad(pick.astype(jnp.bfloat16), ((0, padded - listings), (0, 0), (0, 0)))
    listed = jnp.einsum("lsi,msic->mlc", pick, native, preferred_element_type=jnp.float32).astype(jnp.bfloat16)
    valid = jnp.arange(list_length, dtype=jnp.int32)[None, :] < counts[:, None]
    kept = jnp.where(valid, weights, jnp.zeros_like(weights)).reshape(1, listings)
    flat_ids = class_ids.reshape(1, listings)
    notes = jnp.concatenate(
        [(flat_ids // 16).astype(jnp.bfloat16), (flat_ids % 16).astype(jnp.bfloat16), kept], axis=0
    )
    notes = jnp.pad(notes, ((listings, padded - listings - 3), (0, cycle_parts - listings)))
    payload = (listed + notes[None]).reshape(doms, angles // doms, padded, cycle_parts)
    arrived = lax.all_to_all(payload, "dom", 0, 0, tiled=True)
    noted = arrived[:, 0, listings : listings + 3, :listings]
    ids = noted[:, 0].astype(jnp.int32) * 16 + noted[:, 1].astype(jnp.int32)
    classes = 2 * chips * class_count
    hit = ids[None] == jnp.arange(classes, dtype=jnp.int32)[:, None, None]
    mixing = jnp.where(hit, noted[:, 2][None], jnp.zeros((), jnp.bfloat16))
    totals = jnp.sum(mixing.astype(jnp.float32), axis=(1, 2))
    mixing = jnp.pad(mixing, ((0, 0), (0, 0), (0, padded - listings)))
    sums = jnp.einsum("ksl,smlc->kmc", mixing, arrived, preferred_element_type=jnp.float32)
    depth = angles // doms
    sums = sums.reshape(chips, 2, class_count, depth, cycle_parts)
    totals = jnp.pad(totals.reshape(chips, 2, 1, 1, class_count), ((0, 0), (0, 0), (0, 0), (0, depth - 1), (0, cycle_parts - class_count)))
    sums = jnp.concatenate([sums, totals], axis=2)
    mine = lax.dynamic_index_in_dim(sums, core, 1, keepdims=False)
    other = lax.dynamic_index_in_dim(sums, 1 - core, 1, keepdims=False)
    pair_sums = mine + across(other)
    total = lax.dynamic_index_in_dim(pair_sums, row, 0, keepdims=False)
    for step in range(1, chips):
        block = lax.dynamic_index_in_dim(pair_sums, (row + step) % chips, 0, keepdims=False)
        total = total + along(block, step)
    weight_sums = total[class_count, 0, :class_count]
    class_means = total[:class_count] / jnp.maximum(weight_sums, 1.0)[:, None, None]
    class_means = jnp.transpose(class_means, (1, 0, 2))

    own_best = score(flat, flat, half)
    after_best = score(after, after, half)
    before_best = score(before, before, half)
    far_best = score(lower_far, upper_far, 0)
    best = jnp.stack([own_best, after_best, far_best, before_best])
    kept_best = best[:, :, :class_count]
    sent_best = across(best[:, :, LANES // 2 : LANES // 2 + class_count])
    first = jnp.where(core == 0, kept_best, sent_best)
    second = jnp.where(core == 0, sent_best, kept_best)
    by_chip = jnp.stack([first, second], axis=1)
    by_chip = jnp.roll(by_chip, row, axis=0)
    best_scores = by_chip.reshape(2 * chips * own, class_count)
    return (best_scores, class_means)


def solution(mesh):
    return jax.shard_map(
        on_device,
        mesh=mesh,
        in_specs=(
            P(None, ("dom", "cls"), None, None),
            P(None, "cls", None),
            P(("dom", "cls"), None),
            P(("dom", "cls")),
            P(("dom", "cls"), None),
            P(("dom", "cls"), None),
        ),
        out_specs=(P("dom", "cls"), P("dom", "cls", None)),
        check_vma=False,
    )
```

time: 160 us -> 129 us (0.81); the launches traced: 157 us -> 128 us
  waiting for transfers between devices: 53.6 us -> 43.7 us
  local copies, waits for them, and re-layouts: 17.7 us -> 8.87 us
  Pallas kernels: 45.7 us -> 41.6 us
  other arithmetic: 8.48 us -> 4.49 us
  starting transfers between devices: 25.9 us -> 22.4 us
    ppermute x9 -> x7, waiting for transfers between devices: 24.8 us -> 14.8 us  [along(): return lax.ppermute(value, 'cls', pairs)]
    unnamed x8 -> x7, local copies, waits for them, and re-layouts: 7.23 us -> 1.37 us
    ppermute x1 -> x0, local copies, waits for them, and re-layouts: 4.23 us -> none  [across(): return lax.ppermute(value, 'cls', [(i, i ^ 1) for i in range(2 * chips)])]
    pallas_call x4 -> x5, Pallas kernels: 45.7 us -> 41.6 us  [the longest x4 33.2 us: best_of_group(): pl.pallas_call(functools.partial(score_kernel, scale, rows, shifts, half,...]
    concatenate x1 -> x0, other arithmetic: 3.99 us -> none  [on_device(): jnp.concatenate([jnp.pad(references, pad), jnp.pad(mate, pad)], axis=1)]
    ppermute x9 -> x7, starting transfers between devices: 14.5 us -> 10.9 us  [along(): return lax.ppermute(value, 'cls', pairs)]
    ppermute x3, waiting for transfers between devices: 0.36 us -> 2.41 us  [across(): return lax.ppermute(value, 'cls', [(i, i ^ 1) for i in range(2 * chips)])]
    all_to_all x1, waiting for transfers between devices: 28.5 us -> 26.5 us  [on_device(): arrived = lax.all_to_all(payload, 'dom', 0, 0, tiled=True)]
  transfers between devices with their start and end apart: 13 -> 11, of which waited for: 6 -> 5; matrix products, arithmetic and copies ran while one was open for 14% -> 9% of each run, Pallas kernels for 22% -> 27%
where the time goes in v2:
time: 129 us; the launch traced here: 128 us
  waiting for transfers between devices  43.7 us (34%)
  Pallas kernels  41.6 us (32%)
  starting transfers between devices  22.4 us (17%)
  local copies, waits for them, and re-layouts  8.87 us (7%)
  matrix products  6.31 us (5%)
  other arithmetic  4.49 us (3%)
    pallas_call x4, Pallas kernels, best_of_group(): pl.pallas_call(functools.partial(score_kernel, scale, rows, shifts, half,...  33.2 us
    all_to_all x1, waiting for transfers between devices, on_device(): arrived = lax.all_to_all(payload, 'dom', 0, 0, tiled=True)  26.5 us
    ppermute x7, waiting for transfers between devices, along(): return lax.ppermute(value, 'cls', pairs)  14.8 us
    all_to_all x1, starting transfers between devices, on_device(): arrived = lax.all_to_all(payload, 'dom', 0, 0, tiled=True)  11.4 us
    ppermute x7, starting transfers between devices, along(): return lax.ppermute(value, 'cls', pairs)  10.9 us
    pallas_call x1, Pallas kernels, by_harmonic(): pl.pallas_call(functools.partial(gather_kernel, sizes, tuple(starts)), in...  8.41 us
    dot_general x1, matrix products, on_device(): jnp.einsum('lsi,msic->mlc', pick, native, preferred_element_type=jnp.floa...  4.17 us
  transfers between devices with their start and end apart: 11, of which 5 were waited for; matrix products, arithmetic and copies ran while one was open for 9% of the time, Pallas kernels for 27%

profile of v2, /device:TPU:8, one launch (start us, length us, event | category | flops | bytes accessed | tf_op | source)
XLA Modules:
  0.0 128.3 jit_solution(11388226490049837194)
XLA Ops:
  0.6 0.8 fusion.34
  1.4 0.1 reshape.288
  1.5 0.8 reshape.287
  2.3 0.8 eq.102
  3.0 0.1 iota_compare_fusion.7
  3.1 0.1 broadcast_and_fusion
  3.2 0.0 copy-start
  3.2 4.2 %fusion.4 = bf16[16,256,128]{2,0,1:T(8,128)(2,1)} fusion(bf16[256,9,4,128]{3,2,1,0:T(4,128)(2,1)} %bitcast.62, bf16[16,128]{1,0:T(8,128)(2,1)S(1)} %select_maximum_fusion.1, pred[12,9,4]{1,0,2:T(8,128)(4,1)S(1)} %broadcast_and_fusion), kind=kOutput, calls=%fused_computation.6 | convolution fusion | flops 38797312 | bytes 3412400 | tf_op jit(solution)/shard_map/lsi,msic->mlc/dot_general | solution.py:220
  7.4 11.4 %all-to-all-start = ((bf16[32,8,16,128]{3,2,1,0:T(8,128)(2,1)}), bf16[32,8,16,128]{3,2,1,0:T(8,128)(2,1)}, u32[]{:S(2)}, u32[]{:S(2)}) async-start(bf16[32,8,16,128]{3,2,1,0:T(8,128)(2,1)} %bitcast.68), calls=%async_computation | async-start | bytes 2097152 | tf_op jit(solution)/shard_map/all_to_all | solution.py:229
  18.9 1.7 %collective-permute-start.2 = (bf16[9216,128]{1,0:T(8,128)(2,1)}, bf16[9216,128]{1,0:T(8,128)(2,1)}, u32[]{:S(2)}, u32[]{:S(2)}) collective-permute-start(bf16[9216,128]{1,0:T(8,128)(2,1)} %bitcast.63), channel_id=1, source_target_pairs={{0,2},{1,3},{2,4},{3,5},{4,6},{5,7},{6,0},{7,1},{8,10},{9,11},{10,... | collective-permute-start | bytes 7077896 | tf_op jit(solution)/shard_map/ppermute | solution.py:193
  20.5 0.4 collective-permute-start.1
  21.0 26.5 %all-to-all-done = bf16[32,8,16,128]{3,2,1,0:T(8,128)(2,1)} async-done(((bf16[32,8,16,128]{3,2,1,0:T(8,128)(2,1)}), bf16[32,8,16,128]{3,2,1,0:T(8,128)(2,1)}, u32[]{:S(2)}, u32[]{:S(2)}) %all-to-all-start) | async-done | bytes 1048608 | tf_op jit(solution)/shard_map/all_to_all | solution.py:229
  47.4 0.9 slice.44
  48.3 0.1 copy.31
  48.4 0.2 convert_reduce_fusion
  48.6 0.1 reshape.291
  48.7 0.2 fusion.8
  48.9 2.1 %convolution_bitcast_fusion = f32[400,8,128]{2,0,1:T(8,128)S(1)} fusion(bf16[32,8,16,128]{3,2,1,0:T(8,128)(2,1)} %all-to-all-done, bf16[400,32,12]{0,1,2:T(8,128)(2,1)S(1)} %fusion.8), kind=kOutput, calls=%fused_computation.5 | convolution fusion | flops 419430400 | bytes 2994176 | tf_op jit(solution)/shard_map/ksl,smlc->kmc/dot_general | solution.py:237
  51.0 0.5 copy.28
  51.6 0.1 select_maximum_fusion
  51.7 1.3 copy-done.2
  53.0 1.0 dynamic-slice_bitcast_fusion
  53.9 0.3 cosine_convert_fusion
  54.2 0.3 select_convert_fusion
  54.5 0.1 select_convert_fusion.1
  54.6 2.1 %collective-permute-done.6 = f32[4,51,8,128]{3,2,1,0:T(8,128)} collective-permute-done((f32[4,51,8,128]{3,2,1,0:T(8,128)}, f32[4,51,8,128]{3,2,1,0:T(8,128)}, u32[]{:S(2)}, u32[]{:S(2)}) %collective-permute-start.6) | collective-permute-done | bytes 835616 | tf_op jit(solution)/shard_map/ppermute | solution.py:196
  56.6 1.5 %bitcast_add_fusion = f32[4,51,8,128]{3,2,1,0:T(8,128)S(1)} fusion(f32[4,51,8,128]{3,2,1,0:T(8,128)} %collective-permute-done.6, f32[4,2,51,8,128]{4,3,2,1,0:T(8,128)} %copy-done.2, s32[]{:T(128)S(6)} %select_n.170), kind=kLoop, calls=%fused_computation.8 | loop fusion | flops 208896 | bytes 2506756 | tf_op jit(solution)/shard_map/add | solution.py:244
  58.1 0.1 dynamic-slice_bitcast_fusion.3
  58.2 0.5 collective-permute-start.9
  58.7 2.6 %collective-permute-start.8 = (f32[51,8,128]{2,1,0:T(8,128)S(1)}, f32[51,8,128]{2,1,0:T(8,128)S(1)}, u32[]{:S(2)}, u32[]{:S(2)}) collective-permute-start(f32[51,8,128]{2,1,0:T(8,128)S(1)} %get-tuple-element.4), channel_id=1, source_target_pairs={{0,4},{1,5},{2,6},{3,7},{4,0},{5,1},{6,2},{7,3},{8,12},{9,13},{10,... | collective-permute-start | bytes 626696 | tf_op jit(solution)/shard_map/ppermute | solution.py:193
  61.3 12.1 %collective-permute-done.2.refs_0_.refs_1_ = bf16[9216,128]{1,0:T(8,128)(2,1)} collective-permute-done((bf16[9216,128]{1,0:T(8,128)(2,1)}, bf16[9216,128]{1,0:T(8,128)(2,1)}, u32[]{:S(2)}, u32[]{:S(2)}) %collective-permute-start.2) | collective-permute-done | bytes 2359328 | tf_op jit(solution)/shard_map/ppermute | solution.py:193
  73.4 3.3 %collective-permute-start.7 = (f32[51,8,128]{2,1,0:T(8,128)S(1)}, f32[51,8,128]{2,1,0:T(8,128)S(1)}, u32[]{:S(2)}, u32[]{:S(2)}) collective-permute-start(f32[51,8,128]{2,1,0:T(8,128)S(1)} %get-tuple-element.2), channel_id=1, source_target_pairs={{0,2},{1,3},{2,4},{3,5},{4,6},{5,7},{6,0},{7,1},{8,10},{9,11},{10,... | collective-permute-start | bytes 626696 | tf_op jit(solution)/shard_map/ppermute | solution.py:193
  76.7 1.3 %slice.40 = bf16[4608,128]{1,0:T(8,128)(2,1)S(1)} slice(bf16[9216,128]{1,0:T(8,128)(2,1)} %collective-permute-done.2.refs_0_.refs_1_), slice={[0:4608], [0:128]} | slice | bytes 2359296 | tf_op jit(solution)/shard_map/slice | solution.py:203
  78.1 0.1 collective-permute-start.3
  78.2 1.3 %slice.41 = bf16[4608,128]{1,0:T(8,128)(2,1)S(1)} slice(bf16[9216,128]{1,0:T(8,128)(2,1)} %collective-permute-done.1.refs_0_.refs_1_), slice={[4608:9216], [0:128]} | slice | bytes 2359296 | tf_op jit(solution)/shard_map/slice | solution.py:204
  79.5 2.3 %collective-permute-start.4 = (bf16[4608,128]{1,0:T(8,128)(2,1)S(1)}, bf16[4608,128]{1,0:T(8,128)(2,1)S(1)}, u32[]{:S(2)}, u32[]{:S(2)}) collective-permute-start(bf16[4608,128]{1,0:T(8,128)(2,1)S(1)} %slice.41), channel_id=1, source_target_pairs={{0,6},{1,7},{2,0},{3,1},{4,2},{5,3},{6,4},{7,5},{8,14},{9,15},{10,... | collective-permute-start | bytes 3538952 | tf_op jit(solution)/shard_map/ppermute | solution.py:193
  81.8 2.8 %collective-permute-done.8 = f32[51,8,128]{2,1,0:T(8,128)S(1)} collective-permute-done((f32[51,8,128]{2,1,0:T(8,128)S(1)}, f32[51,8,128]{2,1,0:T(8,128)S(1)}, u32[]{:S(2)}, u32[]{:S(2)}) %collective-permute-start.8) | collective-permute-done | bytes 208928 | tf_op jit(solution)/shard_map/ppermute | solution.py:193
  84.6 0.1 fusion.14
  84.7 8.4 %by_harmonic.1.refs_2_ = bf16[256,128,128]{2,1,0:T(8,128)(2,1)S(1)} custom-call(bf16[50,256,128]{2,1,0:T(8,128)(2,1)S(1)} %bitcast.57, bf16[50,256,128]{2,1,0:T(8,128)(2,1)} %collective-permute-done.refs_1_), custom_call_target="tpu_custom_call" | custom-call | bytes 29884416 | tf_op jit(solution)/shard_map/by_harmonic/pallas_call | solution.py:57
  93.1 7.2 %score.4 = f32[4,128]{1,0:T(4,128)S(1)} custom-call(bf16[9216,128]{1,0:T(8,128)(2,1)S(1)} %bitcast.65, bf16[9216,128]{1,0:T(8,128)(2,1)S(1)} %bitcast.66, bf16[256,128,128]{2,1,0:T(8,128)(2,1)S(1)} %by_harmonic.1.refs_2_, bf16[264,256]{1,0:T(8,128)(2,1)S(1)} %fusion.17.refs_3_), custom_call_target="tpu_custom_call" | custom-call | flops 7361003520 | bytes 20000000 | tf_op jit(solution)/shard_map/score/pallas_call | solution.py:161
  100.3 9.5 %score.7 = f32[4,128]{1,0:T(4,128)S(1)} custom-call(bf16[9216,128]{1,0:T(8,128)(2,1)} %collective-permute-done.2.refs_0_.refs_1_, bf16[9216,128]{1,0:T(8,128)(2,1)} %collective-permute-done.2.refs_0_.refs_1_, bf16[256,128,128]{2,1,0:T(8,128)(2,1)S(1)} %by_harmonic.1.refs_2_, bf16[264,256]{1,0:T(8,128)(2,1)S(1)} %fusion.17.refs_3_), custom_call_target="tpu_custom_call" | custom-call | flops 7361003520 | bytes 20000000 | tf_op jit(solution)/shard_map/score/pallas_call | solution.py:161
  109.7 9.5 %score.5 = f32[4,128]{1,0:T(4,128)S(1)} custom-call(bf16[9216,128]{1,0:T(8,128)(2,1)} %collective-permute-done.1.refs_0_.refs_1_, bf16[9216,128]{1,0:T(8,128)(2,1)} %collective-permute-done.1.refs_0_.refs_1_, bf16[256,128,128]{2,1,0:T(8,128)(2,1)S(1)} %by_harmonic.1.refs_2_, bf16[264,256]{1,0:T(8,128)(2,1)S(1)} %fusion.17.refs_3_), custom_call_target="tpu_custom_call" | custom-call | flops 7361003520 | bytes 20000000 | tf_op jit(solution)/shard_map/score/pallas_call | solution.py:161
  119.2 7.1 %score.6 = f32[4,128]{1,0:T(4,128)S(1)} custom-call(bf16[4608,128]{1,0:T(8,128)(2,1)S(1)} %collective-permute-done.3.refs_0_, bf16[4608,128]{1,0:T(8,128)(2,1)S(1)} %collective-permute-done.4.refs_1_, bf16[256,128,128]{2,1,0:T(8,128)(2,1)S(1)} %by_harmonic.1.refs_2_, bf16[264,256]{1,0:T(8,128)(2,1)S(1)} %fusion.17.refs_3_), custom_call_target="tpu_custom_call" | custom-call | flops 7361003520 | bytes 20000000 | tf_op jit(solution)/shard_map/score/pallas_call | solution.py:161
  126.4 0.1 slice.43
  126.5 0.0 collective-permute-start.5
  126.5 0.8 fusion.15
  127.3 0.4 collective-permute-done.5
  127.7 0.6 copy.24
  (27 shorter events, 0.2 us)
Async XLA Ops:
  3.2 17.7 %copy-start = (bf16[256,50,128]{2,0,1:T(8,128)(2,1)S(1)}, bf16[256,50,128]{2,0,1:T(8,128)(2,1)}, u32[]{:S(2)}) copy-start(bf16[256,50,128]{2,0,1:T(8,128)(2,1)} %param.7) | copy-start | bytes 9830404
  7.4 40.0 %all-to-all-start = ((bf16[32,8,16,128]{3,2,1,0:T(8,128)(2,1)}), bf16[32,8,16,128]{3,2,1,0:T(8,128)(2,1)}, u32[]{:S(2)}, u32[]{:S(2)}) async-start(bf16[32,8,16,128]{3,2,1,0:T(8,128)(2,1)} %bitcast.68), calls=%async_computation | async-start | bytes 2097152 | tf_op jit(solution)/shard_map/all_to_all | solution.py:229
  18.9 54.5 %collective-permute-start.2 = (bf16[9216,128]{1,0:T(8,128)(2,1)}, bf16[9216,128]{1,0:T(8,128)(2,1)}, u32[]{:S(2)}, u32[]{:S(2)}) collective-permute-start(bf16[9216,128]{1,0:T(8,128)(2,1)} %bitcast.63), channel_id=1, source_target_pairs={{0,2},{1,3},{2,4},{3,5},{4,6},{5,7},{6,0},{7,1},{8,10},{9,11},{10,... | collective-permute-start | bytes 7077896 | tf_op jit(solution)/shard_map/ppermute | solution.py:193
  20.5 57.6 %collective-permute-start.1 = (bf16[9216,128]{1,0:T(8,128)(2,1)}, bf16[9216,128]{1,0:T(8,128)(2,1)}, u32[]{:S(2)}, u32[]{:S(2)}) collective-permute-start(bf16[9216,128]{1,0:T(8,128)(2,1)} %bitcast.64), channel_id=1, source_target_pairs={{0,6},{1,7},{2,0},{3,1},{4,2},{5,3},{6,4},{7,5},{8,14},{9,15},{10,... | collective-permute-start | bytes 7077896 | tf_op jit(solution)/shard_map/ppermute | solution.py:193
  21.0 63.7 %collective-permute-start = (bf16[50,256,128]{2,1,0:T(8,128)(2,1)S(1)}, bf16[50,256,128]{2,1,0:T(8,128)(2,1)}, u32[]{:S(2)}, u32[]{:S(2)}) collective-permute-start(bf16[50,256,128]{2,1,0:T(8,128)(2,1)S(1)} %bitcast.56), channel_id=1, source_target_pairs={{0,1},{1,0},{2,3},{3,2},{4,5},{5,4},{6,7},{7,6},{8,9},{9,8},{10,11... | collective-permute-start | bytes 9830408 | tf_op jit(solution)/shard_map/ppermute | solution.py:196
  51.7 1.3 copy-start.2
  53.9 2.7 %collective-permute-start.6 = (f32[4,51,8,128]{3,2,1,0:T(8,128)}, f32[4,51,8,128]{3,2,1,0:T(8,128)}, u32[]{:S(2)}, u32[]{:S(2)}) collective-permute-start(f32[4,51,8,128]{3,2,1,0:T(8,128)} %dynamic-slice_bitcast_fusion), channel_id=1, source_target_pairs={{0,1},{1,0},{2,3},{3,2},{4,5},{5,4},{6,7},{7,6},{8,9},{9,8},{10,11... | collective-permute-start | bytes 2506760 | tf_op jit(solution)/shard_map/ppermute | solution.py:196
  58.2 21.3 %collective-permute-start.9 = (f32[51,8,128]{2,1,0:T(8,128)S(1)}, f32[51,8,128]{2,1,0:T(8,128)S(1)}, u32[]{:S(2)}, u32[]{:S(2)}) collective-permute-start(f32[51,8,128]{2,1,0:T(8,128)S(1)} %get-tuple-element.3), channel_id=1, source_target_pairs={{0,6},{1,7},{2,0},{3,1},{4,2},{5,3},{6,4},{7,5},{8,14},{9,15},{10,... | collective-permute-start | bytes 626696 | tf_op jit(solution)/shard_map/ppermute | solution.py:193
  58.7 25.9 %collective-permute-start.8 = (f32[51,8,128]{2,1,0:T(8,128)S(1)}, f32[51,8,128]{2,1,0:T(8,128)S(1)}, u32[]{:S(2)}, u32[]{:S(2)}) collective-permute-start(f32[51,8,128]{2,1,0:T(8,128)S(1)} %get-tuple-element.4), channel_id=1, source_target_pairs={{0,4},{1,5},{2,6},{3,7},{4,0},{5,1},{6,2},{7,3},{8,12},{9,13},{10,... | collective-permute-start | bytes 626696 | tf_op jit(solution)/shard_map/ppermute | solution.py:193
  73.4 11.2 %collective-permute-start.7 = (f32[51,8,128]{2,1,0:T(8,128)S(1)}, f32[51,8,128]{2,1,0:T(8,128)S(1)}, u32[]{:S(2)}, u32[]{:S(2)}) collective-permute-start(f32[51,8,128]{2,1,0:T(8,128)S(1)} %get-tuple-element.2), channel_id=1, source_target_pairs={{0,2},{1,3},{2,4},{3,5},{4,6},{5,7},{6,0},{7,1},{8,10},{9,11},{10,... | collective-permute-start | bytes 626696 | tf_op jit(solution)/shard_map/ppermute | solution.py:193
  78.1 41.1 %collective-permute-start.3 = (bf16[4608,128]{1,0:T(8,128)(2,1)S(1)}, bf16[4608,128]{1,0:T(8,128)(2,1)S(1)}, u32[]{:S(2)}, u32[]{:S(2)}) collective-permute-start(bf16[4608,128]{1,0:T(8,128)(2,1)S(1)} %slice.40), channel_id=1, source_target_pairs={{0,2},{1,3},{2,4},{3,5},{4,6},{5,7},{6,0},{7,1},{8,10},{9,11},{10,... | collective-permute-start | bytes 3538952 | tf_op jit(solution)/shard_map/ppermute | solution.py:193
  79.5 39.7 %collective-permute-start.4 = (bf16[4608,128]{1,0:T(8,128)(2,1)S(1)}, bf16[4608,128]{1,0:T(8,128)(2,1)S(1)}, u32[]{:S(2)}, u32[]{:S(2)}) collective-permute-start(bf16[4608,128]{1,0:T(8,128)(2,1)S(1)} %slice.41), channel_id=1, source_target_pairs={{0,6},{1,7},{2,0},{3,1},{4,2},{5,3},{6,4},{7,5},{8,14},{9,15},{10,... | collective-permute-start | bytes 3538952 | tf_op jit(solution)/shard_map/ppermute | solution.py:193
  84.7 8.4 %copy-start.1 = (bf16[256,4,9,128]{3,1,2,0:T(4,128)(2,1)S(1)}, bf16[256,4,9,128]{3,1,2,0:T(4,128)(2,1)}, u32[]{:S(2)}) copy-start(bf16[256,4,9,128]{3,1,2,0:T(4,128)(2,1)} %param.6) | copy-start | bytes 7077892
  126.5 1.2 collective-permute-start.5

commit v3 on v2

v3 whole, which is shorter than its diff:
```python
import functools
import math

import jax
import jax.numpy as jnp
from jax import lax
from jax.experimental import pallas as pl
from jax.experimental.pallas import tpu as pltpu
from jax.sharding import PartitionSpec as P


CHUNK = 16
LANES = 128
WHOLE = pl.BlockSpec(memory_space=pltpu.VMEM)


def folded_table(angles):
    half = angles // 2
    index = jnp.arange(half, dtype=jnp.int32)
    product = index[:, None] * index[None, :] % angles
    phase = product.astype(jnp.float32) * (2.0 * math.pi / angles)
    edge = (index[:, None] == 0) | (index[None, :] == 0)
    cosine = jnp.cos(phase)
    sine = jnp.where(edge, 0.0, -jnp.sin(phase))
    alternate = jnp.where(index % 2 == 0, 1.0, -1.0)
    nyquist = jnp.where(index[None, :] == 0, alternate[:, None], 0.0)
    last = jnp.concatenate([alternate, jnp.where(index == 0, 1.0, 0.0)])
    rows = [
        jnp.concatenate([cosine, nyquist], axis=1),
        jnp.concatenate([jnp.zeros_like(sine), sine], axis=1),
        jnp.broadcast_to(last[None, :], (8, angles)),
    ]
    return jnp.concatenate(rows, axis=0).astype(jnp.bfloat16)


def gather_kernel(sizes, starts, *refs):
    pieces, out_ref, work = refs[: len(sizes)], refs[len(sizes)], refs[len(sizes) + 1]
    total = out_ref.shape[1]
    work[...] = jnp.zeros(work.shape, jnp.float32)

    def chunk(j, carry):
        base = pl.multiple_of(j * CHUNK, CHUNK)
        for size, start, ref in zip(sizes, starts, pieces):
            block = ref[:, pl.ds(base, CHUNK), :].reshape(size * CHUNK, LANES)
            work[pl.ds(start * CHUNK, size * CHUNK), :] = block.astype(jnp.float32)
        for t in range(CHUNK):
            out_ref[base + t] = work[pl.ds(t, total, stride=CHUNK), :].astype(jnp.bfloat16)
        return carry

    lax.fori_loop(0, out_ref.shape[0] // CHUNK, chunk, 0)


def by_harmonic(pieces, starts, total):
    angles, cycle_parts = pieces[0].shape[1:]
    sizes = tuple(piece.shape[0] for piece in pieces)
    moved = 2 * angles * cycle_parts * (sum(sizes) + total)
    return pl.pallas_call(
        functools.partial(gather_kernel, sizes, tuple(starts)),
        in_specs=[WHOLE] * len(pieces),
        out_specs=WHOLE,
        out_shape=jax.ShapeDtypeStruct((angles, total, cycle_parts), jnp.bfloat16),
        scratch_shapes=[pltpu.VMEM((total * CHUNK, cycle_parts), jnp.float32)],
        compiler_params=pltpu.CompilerParams(vmem_limit_bytes=30 * 1024 * 1024),
        cost_estimate=pl.CostEstimate(flops=0, bytes_accessed=2 * moved, transcendentals=0),
        name="by_harmonic",
    )(*pieces)


def score_kernel(scale, rows, shifts, groups, *refs):
    images, stacked = refs[:groups], refs[groups : groups + 2]
    table_ref, out_ref, left_ref, fa, fb, folded = refs[groups + 2 :]
    half = table_ref.shape[1] // 2
    all_rows = 2 * rows * groups
    cycles = LANES // 2
    lane = lax.broadcasted_iota(jnp.int32, (1, LANES), 1)
    sign = jnp.where(lane < cycles, 1.0, -1.0)
    block = CHUNK * rows

    def chunk(j, carry):
        back = 2 * half - CHUNK - j * CHUNK
        edge = jnp.where(j == 0, half, 2 * half - CHUNK * j)
        for g, image in enumerate(images):
            fa[g] = image[pl.ds(pl.multiple_of(j * block, block), block), :].astype(jnp.float32)
            fb[g, pl.ds(0, block), :] = image[pl.ds(pl.multiple_of(back * rows, block), block), :].astype(jnp.float32)
            edge_rows = pl.multiple_of(edge * rows, block)
            fb[g, pl.ds(block, 2 * rows), :] = image[pl.ds(edge_rows, 2 * rows), :].astype(jnp.float32)
        paired = jnp.where(j == 0, 0.0, 1.0)
        for t in range(CHUNK):
            slot = t % left_ref.shape[0]
            for g in range(groups):
                a = fa[g, pl.ds(t * rows, rows), :]
                b = fb[g, pl.ds((CHUNK - t) * rows, rows), :]
                a_turned = pltpu.roll(a, cycles, 1) * sign
                b_turned = pltpu.roll(b, cycles, 1) * (-sign)
                if t == 0:
                    b_turned = b_turned * paired + b * (1.0 - paired)
                    a_turned = a_turned * paired
                    b = b * paired
                top = 2 * rows * g
                left_ref[slot, pl.ds(top, rows), pl.ds(0, LANES)] = a
                left_ref[slot, pl.ds(top, rows), pl.ds(LANES, LANES)] = b
                left_ref[slot, pl.ds(top + rows, rows), pl.ds(0, LANES)] = a_turned
                left_ref[slot, pl.ds(top + rows, rows), pl.ds(LANES, LANES)] = b_turned
            m = j * CHUNK + t
            mirror = edge if t == 0 else 2 * half - m
            right = jnp.concatenate(
                [
                    jnp.concatenate([ref[m] for ref in stacked], axis=0),
                    jnp.concatenate([ref[mirror] for ref in stacked], axis=0),
                ],
                axis=1,
            )
            folded[pl.ds(pl.multiple_of(m * all_rows, 8), all_rows), :] = lax.dot_general(
                left_ref[slot].astype(jnp.bfloat16),
                right,
                (((1,), (1,)), ((), ())),
                preferred_element_type=jnp.float32,
            )
        return carry

    lax.fori_loop(0, half // CHUNK, chunk, 0)
    table = table_ref[...]
    each = rows // shifts
    width = 2 * LANES

    def column(g, n):
        even = folded[pl.ds(2 * rows * g + n, half, stride=all_rows), :]
        odd = folded[pl.ds(2 * rows * g + rows + n, half, stride=all_rows), :]
        return jnp.concatenate([even, odd], axis=0).astype(jnp.bfloat16)

    def one_shift(s, best):
        better = []
        for q in range(groups * each // 2):
            columns = [column(i // each, s * each + i % each) for i in (2 * q, 2 * q + 1)]
            turned = jnp.dot(table, jnp.concatenate(columns, axis=1), preferred_element_type=jnp.float32)
            both = turned[:half] + jnp.abs(turned[half : 2 * half])
            top = jnp.max(both.reshape(half // 8, 8, width), axis=0)
            top = jnp.maximum(top, turned[2 * half :])
            better.append(jnp.maximum(best[q], top))
        return tuple(better)

    start = tuple(jnp.full((8, width), -jnp.inf, jnp.float32) for _ in range(groups * each // 2))
    best = lax.fori_loop(0, shifts, one_shift, start)
    for q in range(groups * each // 2):
        top = jnp.max(best[q], axis=0, keepdims=True) * scale
        out_ref[2 * q : 2 * q + 1, :] = top[:, :LANES]
        out_ref[2 * q + 1 : 2 * q + 2, :] = top[:, LANES:]


def best_of_groups(images, stacked, table, shifts, rows, scale):
    angles, _, cycle_parts = stacked[0].shape
    half = angles // 2
    each = rows // shifts
    groups = len(images)
    flops = groups * (2 * half * 2 * rows * 2 * cycle_parts * LANES + 2 * rows * LANES * angles * (angles + 8))
    return pl.pallas_call(
        functools.partial(score_kernel, scale, rows, shifts, groups),
        in_specs=[WHOLE] * (groups + 3),
        out_specs=WHOLE,
        out_shape=jax.ShapeDtypeStruct((groups * each, LANES), jnp.float32),
        scratch_shapes=[
            pltpu.VMEM((4, 2 * rows * groups, 2 * cycle_parts), jnp.float32),
            pltpu.VMEM((groups, CHUNK * rows, cycle_parts), jnp.float32),
            pltpu.VMEM((groups, (CHUNK + 2) * rows, cycle_parts), jnp.float32),
            pltpu.VMEM((2 * rows * groups * half, LANES), jnp.float32),
        ],
        compiler_params=pltpu.CompilerParams(vmem_limit_bytes=34 * 1024 * 1024),
        cost_estimate=pl.CostEstimate(flops=6 * flops, bytes_accessed=20_000_000, transcendentals=0),
        name="score",
    )(*images, *stacked, table)


def on_device(particles, references, class_ids, counts, shift_ids, weights):
    cls_index = lax.axis_index("cls")
    core = cls_index % 2
    row = cls_index // 2
    angles, own, shifts, cycle_parts = particles.shape
    class_count = references.shape[1]
    list_length = class_ids.shape[1]
    rows = shifts * own
    doms = 32
    chips = 4
    ring = 4
    scale = 1.0 / math.sqrt(1.0 * cycle_parts * angles)

    def move(value, target):
        pairs = [(2 * y + c, 2 * t + e) for y in range(chips) for c in range(2) for t, e in [target(y, c)]]
        return lax.ppermute(value, "cls", pairs)

    def along(value, step):
        return move(value, lambda y, c: ((y + step) % chips, c))

    def across(value):
        return move(value, lambda y, c: (y, 1 - c))

    def facing(value):
        return move(value, lambda y, c: (chips - 1 - y, c))

    def around(value, step):
        length = doms // ring
        pairs = [(x * length + z, (x + step) % ring * length + z) for x in range(ring) for z in range(length)]
        return lax.ppermute(value, "dom", pairs)

    native = jnp.transpose(particles, (0, 2, 1, 3))
    flat = native.reshape(angles * rows, cycle_parts)
    class_major = jnp.transpose(references, (1, 0, 2))

    place = lax.axis_index("dom") // (doms // ring)
    straight = 20
    window = -(-(class_count - straight) // ring)
    first = jnp.minimum(straight + window * place, class_count - window)
    piece = facing(lax.dynamic_slice_in_dim(class_major, first, window, 0))
    direct = facing(class_major[:straight])
    from_left = around(piece, 1)
    from_right = around(piece, -1)
    far_upper = around(from_left[: window // 2], 1)
    far_lower = around(from_right[window // 2 :], -1)

    partner = move(flat, lambda y, c: (y ^ 1, c))
    mate = across(flat)
    partner_mate = across(partner)

    own_set = by_harmonic([class_major], [0], LANES // 2)
    starts = [0, straight, straight + window, straight + 2 * window, straight + 3 * window, straight + 3 * window + window // 2]
    facing_set = by_harmonic([direct, piece, from_left, from_right, far_upper, far_lower], starts, LANES // 2)
    stacked = [own_set, facing_set]
    table = folded_table(angles)
    score = functools.partial(best_of_groups, stacked=stacked, table=table, shifts=shifts, rows=rows, scale=scale)

    listings = own * list_length
    padded = 16
    listed_shift = shift_ids.reshape(listings)
    listed_image = jnp.arange(listings, dtype=jnp.int32) // list_length
    pick = (listed_shift[:, None, None] == jnp.arange(shifts, dtype=jnp.int32)[None, :, None]) & (
        listed_image[:, None, None] == jnp.arange(own, dtype=jnp.int32)[None, None, :]
    )
    pick = jnp.pad(pick.astype(jnp.bfloat16), ((0, padded - listings), (0, 0), (0, 0)))
    listed = jnp.einsum("lsi,msic->mlc", pick, native, preferred_element_type=jnp.float32).astype(jnp.bfloat16)
    valid = jnp.arange(list_length, dtype=jnp.int32)[None, :] < counts[:, None]
    kept = jnp.where(valid, weights, jnp.zeros_like(weights)).reshape(1, listings)
    flat_ids = class_ids.reshape(1, listings)
    notes = jnp.concatenate(
        [(flat_ids // 16).astype(jnp.bfloat16), (flat_ids % 16).astype(jnp.bfloat16), kept], axis=0
    )
    notes = jnp.pad(notes, ((listings, padded - listings - 3), (0, cycle_parts - listings)))
    payload = (listed + notes[None]).reshape(doms, angles // doms, padded, cycle_parts)
    arrived = lax.all_to_all(payload, "dom", 0, 0, tiled=True)
    noted = arrived[:, 0, listings : listings + 3, :listings]
    ids = noted[:, 0].astype(jnp.int32) * 16 + noted[:, 1].astype(jnp.int32)
    classes = 2 * chips * class_count
    hit = ids[None] == jnp.arange(classes, dtype=jnp.int32)[:, None, None]
    mixing = jnp.where(hit, noted[:, 2][None], jnp.zeros((), jnp.bfloat16))
    totals = jnp.sum(mixing.astype(jnp.float32), axis=(1, 2))
    mixing = jnp.pad(mixing, ((0, 0), (0, 0), (0, padded - listings)))
    sums = jnp.einsum("ksl,smlc->kmc", mixing, arrived, preferred_element_type=jnp.float32)
    depth = angles // doms
    sums = sums.reshape(chips, 2, class_count, depth, cycle_parts)
    totals = jnp.pad(totals.reshape(chips, 2, 1, 1, class_count), ((0, 0), (0, 0), (0, 0), (0, depth - 1), (0, cycle_parts - class_count)))
    sums = jnp.concatenate([sums, totals], axis=2)
    mine = lax.dynamic_index_in_dim(sums, core, 1, keepdims=False)
    other = lax.dynamic_index_in_dim(sums, 1 - core, 1, keepdims=False)
    pair_sums = mine + across(other)
    total = lax.dynamic_index_in_dim(pair_sums, row, 0, keepdims=False)
    for step in range(1, chips):
        block = lax.dynamic_index_in_dim(pair_sums, (row + step) % chips, 0, keepdims=False)
        total = total + along(block, step)
    weight_sums = total[class_count, 0, :class_count]
    class_means = total[:class_count] / jnp.maximum(weight_sums, 1.0)[:, None, None]
    class_means = jnp.transpose(class_means, (1, 0, 2))

    home = score([flat, mate])
    away = score([partner, partner_mate])
    best = jnp.concatenate([home, away], axis=0)
    lanes_of = LANES // 2
    sent = facing(best[:, lanes_of : lanes_of + straight + ring * window])
    by_step = [sent[:, straight + window * k : straight + window * (k + 1)] for k in (0, 2, 3, 1)]
    overlap = straight + ring * window - class_count
    ordered = []
    for x in range(ring):
        columns = [by_step[(k - x) % ring] for k in range(ring)]
        columns[-1] = columns[-1][:, overlap:]
        ordered.append(jnp.concatenate([sent[:, :straight]] + columns, axis=1))
    others = lax.select_n(place, *ordered)
    own_best = best[:, :class_count].reshape(2, 2, own, class_count)
    facing_best = others.reshape(2, 2, own, class_count)
    grid = jnp.stack([own_best, facing_best[::-1]])
    for axis, bit in ((0, row // 2), (1, row % 2), (2, core)):
        grid = jnp.where(bit == 1, jnp.flip(grid, axis), grid)
    best_scores = grid.reshape(2 * chips * own, class_count)
    return (best_scores, class_means)


def solution(mesh):
    return jax.shard_map(
        on_device,
        mesh=mesh,
        in_specs=(
            P(None, ("dom", "cls"), None, None),
            P(None, "cls", None),
            P(("dom", "cls"), None),
            P(("dom", "cls")),
            P(("dom", "cls"), None),
            P(("dom", "cls"), None),
        ),
        out_specs=(P("dom", "cls"), P("dom", "cls", None)),
        check_vma=False,
    )
```

time: 129 us -> 119 us (0.922)
  the two profiles are of different devices: /device:TPU:8 before, /device:TPU:32 now
where the time goes in v3:
time: 119 us; the launch traced here: 118 us
  waiting for transfers between devices  32.8 us (28%)
  Pallas kernels  31.2 us (26%)
  starting transfers between devices  25.7 us (22%)
  local copies, waits for them, and re-layouts  12.7 us (11%)
  other arithmetic  8.6 us (7%)
  matrix products  6.35 us (5%)
    pallas_call x2, Pallas kernels, best_of_groups(): pl.pallas_call(functools.partial(score_kernel, scale, rows, shifts, group...  23.2 us
    ppermute x10, waiting for transfers between devices, move(): return lax.ppermute(value, 'cls', pairs)  15.7 us
    all_to_all x1, starting transfers between devices, on_device(): arrived = lax.all_to_all(payload, 'dom', 0, 0, tiled=True)  11.2 us
    ppermute x10, starting transfers between devices, move(): return lax.ppermute(value, 'cls', pairs)  10.4 us
    ppermute x4, waiting for transfers between devices, around(): return lax.ppermute(value, 'dom', pairs)  8.97 us
    all_to_all x1, waiting for transfers between devices, on_device(): arrived = lax.all_to_all(payload, 'dom', 0, 0, tiled=True)  8.12 us
    pallas_call x2, Pallas kernels, by_harmonic(): pl.pallas_call(functools.partial(gather_kernel, sizes, tuple(starts)), in...  7.96 us
    dot_general x1, matrix products, on_device(): jnp.einsum('lsi,msic->mlc', pick, native, preferred_element_type=jnp.floa...  4.2 us
  transfers between devices with their start and end apart: 15, of which 5 were waited for; matrix products, arithmetic and copies ran while one was open for 15% of the time, Pallas kernels for 17%

profile of v3, /device:TPU:32, one launch (start us, length us, event | category | flops | bytes accessed | tf_op | source)
XLA Modules:
  0.0 118.3 jit_solution(18016540172680637504)
XLA Ops:
  0.6 0.8 reshape.305
  1.4 0.8 fusion.32
  2.3 0.8 eq.107
  3.2 4.2 %fusion.4 = bf16[16,256,128]{2,0,1:T(8,128)(2,1)} fusion(bf16[256,9,4,128]{3,2,1,0:T(4,128)(2,1)} %bitcast.68, bf16[16,128]{1,0:T(8,128)(2,1)S(1)} %select_maximum_fusion.1, pred[12,9,4]{1,0,2:T(8,128)(4,1)S(1)} %broadcast_and_fusion), kind=kOutput, calls=%fused_computation.6 | convolution fusion | flops 38797312 | bytes 3412400 | tf_op jit(solution)/shard_map/lsi,msic->mlc/dot_general | solution.py:238
  7.4 11.2 %all-to-all-start = ((bf16[32,8,16,128]{3,2,1,0:T(8,128)(2,1)}), bf16[32,8,16,128]{3,2,1,0:T(8,128)(2,1)}, u32[]{:S(2)}, u32[]{:S(2)}) async-start(bf16[32,8,16,128]{3,2,1,0:T(8,128)(2,1)} %bitcast.77), calls=%async_computation | async-start | bytes 2097152 | tf_op jit(solution)/shard_map/all_to_all | solution.py:247
  18.7 0.9 dynamic-slice_bitcast_fusion.1
  19.6 3.0 %collective-permute-start.2 = (bf16[8,256,128]{2,1,0:T(8,128)(2,1)}, bf16[8,256,128]{2,1,0:T(8,128)(2,1)}, u32[]{:S(2)}, u32[]{:S(2)}) collective-permute-start(bf16[8,256,128]{2,1,0:T(8,128)(2,1)} %dynamic-slice_bitcast_fusion.1), channel_id=1, source_target_pairs={{0,6},{1,7},{2,4},{3,5},{4,2},{5,3},{6,0},{7,1},{8,14},{9,15},{10,... | collective-permute-start | bytes 1572872 | tf_op jit(solution)/shard_map/ppermute | solution.py:188
  22.6 0.1 collective-permute-start.7
  22.7 1.3 %slice.96 = bf16[20,256,128]{2,1,0:T(8,128)(2,1)} slice(bf16[50,256,128]{2,1,0:T(8,128)(2,1)S(1)} %bitcast.66), slice={[0:20], [0:256], [0:128]} | slice | bytes 2621440 | tf_op jit(solution)/shard_map/slice | solution.py:213
  24.0 1.1 collective-permute-start.1
  25.1 10.8 %collective-permute-done.2.refs_1_ = bf16[8,256,128]{2,1,0:T(8,128)(2,1)} collective-permute-done((bf16[8,256,128]{2,1,0:T(8,128)(2,1)}, bf16[8,256,128]{2,1,0:T(8,128)(2,1)}, u32[]{:S(2)}, u32[]{:S(2)}) %collective-permute-start.2) | collective-permute-done | bytes 524320 | tf_op jit(solution)/shard_map/ppermute | solution.py:188
  35.9 1.5 %collective-permute-start.3 = (bf16[8,256,128]{2,1,0:T(8,128)(2,1)}, bf16[8,256,128]{2,1,0:T(8,128)(2,1)}, u32[]{:S(2)}, u32[]{:S(2)}) collective-permute-start(bf16[8,256,128]{2,1,0:T(8,128)(2,1)} %collective-permute-done.2.refs_1_), channel_id=1, source_target_pairs={{0,64},{8,72},{16,80},{24,88},{32,96},{40,104},{48,112},{56,120},{... | collective-permute-start | bytes 1572872 | tf_op jit(solution)/shard_map/ppermute | solution.py:202
  37.4 1.8 %collective-permute-start.4 = (bf16[8,256,128]{2,1,0:T(8,128)(2,1)}, bf16[8,256,128]{2,1,0:T(8,128)(2,1)}, u32[]{:S(2)}, u32[]{:S(2)}) collective-permute-start(bf16[8,256,128]{2,1,0:T(8,128)(2,1)} %collective-permute-done.2.refs_1_), channel_id=1, source_target_pairs={{0,192},{8,200},{16,208},{24,216},{32,224},{40,232},{48,240},{56,2... | collective-permute-start | bytes 1572872 | tf_op jit(solution)/shard_map/ppermute | solution.py:202
  39.1 8.1 %all-to-all-done = bf16[32,8,16,128]{3,2,1,0:T(8,128)(2,1)} async-done(((bf16[32,8,16,128]{3,2,1,0:T(8,128)(2,1)}), bf16[32,8,16,128]{3,2,1,0:T(8,128)(2,1)}, u32[]{:S(2)}, u32[]{:S(2)}) %all-to-all-start) | async-done | bytes 1048608 | tf_op jit(solution)/shard_map/all_to_all | solution.py:247
  47.3 0.9 slice.112
  48.1 0.1 copy.28
  48.2 0.2 fusion.8
  48.4 2.1 %convolution_bitcast_fusion = f32[400,8,128]{2,0,1:T(8,128)S(1)} fusion(bf16[32,8,16,128]{3,2,1,0:T(8,128)(2,1)} %all-to-all-done, bf16[400,32,12]{0,1,2:T(8,128)(2,1)S(1)} %fusion.8), kind=kOutput, calls=%fused_computation.5 | convolution fusion | flops 419430400 | bytes 2994176 | tf_op jit(solution)/shard_map/ksl,smlc->kmc/dot_general | solution.py:255
  50.6 0.2 convert_reduce_fusion
  50.8 1.7 %copy.25 = f32[400,8,128]{2,1,0:T(8,128)} copy(f32[400,8,128]{2,0,1:T(8,128)S(1)} %convolution_bitcast_fusion) | data formatting | bytes 3276800 | tf_op jit(solution)/shard_map/ksl,smlc->kmc/dot_general | solution.py:255
  52.5 1.5 %select_maximum_fusion = f32[4,2,51,8,128]{4,3,2,1,0:T(8,128)S(1)} fusion(f32[4,2,1,1,50]{4,3,2,1,0:T(1,128)S(1)} %reshape.309, f32[4,2,50,8,128]{4,3,2,1,0:T(8,128)} %bitcast.72), kind=kLoop, calls=%fused_computation.3 | loop fusion | flops 1253376 | bytes 3311168 | tf_op jit(solution)/shard_map/concatenate | solution.py:259
  54.1 1.1 dynamic-slice_bitcast_fusion
  55.2 0.9 select_convert_fusion
  56.1 1.0 slice.97
  57.1 0.7 collective-permute-start.5
  57.8 0.7 select_convert_fusion.1
  58.5 1.7 %slice.98 = bf16[4,256,128]{2,1,0:T(8,128)(2,1)} slice(bf16[8,256,128]{2,1,0:T(8,128)(2,1)} %collective-permute-done.4.refs_3_), slice={[4:8], [0:256], [0:128]} | slice | bytes 524288 | tf_op jit(solution)/shard_map/slice | solution.py:217
  60.2 6.9 %collective-permute-done.5.refs_4_ = bf16[4,256,128]{2,1,0:T(8,128)(2,1)S(1)} collective-permute-done((bf16[4,256,128]{2,1,0:T(8,128)(2,1)S(1)}, bf16[4,256,128]{2,1,0:T(8,128)(2,1)S(1)}, u32[]{:S(2)}, u32[]{:S(2)}) %collective-permute-start.5) | collective-permute-done | bytes 262176 | tf_op jit(solution)/shard_map/ppermute | solution.py:202
  67.1 0.1 collective-permute-start.6
  67.2 3.0 %by_harmonic.2.refs_2_ = bf16[256,64,128]{2,1,0:T(8,128)(2,1)S(1)} custom-call(bf16[50,256,128]{2,1,0:T(8,128)(2,1)S(1)} %bitcast.67), custom_call_target="tpu_custom_call" | custom-call | bytes 14942208 | tf_op jit(solution)/shard_map/by_harmonic/pallas_call | solution.py:57
  70.2 1.9 %copy-done.1 = bf16[256,64,128]{2,1,0:T(8,128)(2,1)} copy-done((bf16[256,64,128]{2,1,0:T(8,128)(2,1)}, bf16[256,64,128]{2,1,0:T(8,128)(2,1)S(1)}, u32[]{:S(2)}) %copy-start.1) | copy-done | bytes 4194328
  72.1 0.3 cosine_convert_fusion
  72.4 0.8 fusion.17.refs_4_
  73.2 2.1 %collective-permute-done.6.refs_5_ = bf16[4,256,128]{2,1,0:T(8,128)(2,1)} collective-permute-done((bf16[4,256,128]{2,1,0:T(8,128)(2,1)}, bf16[4,256,128]{2,1,0:T(8,128)(2,1)}, u32[]{:S(2)}, u32[]{:S(2)}) %collective-permute-start.6) | collective-permute-done | bytes 262176 | tf_op jit(solution)/shard_map/ppermute | solution.py:202
  75.2 5.0 %by_harmonic.3.refs_3_ = bf16[256,64,128]{2,1,0:T(8,128)(2,1)S(1)} custom-call(bf16[20,256,128]{2,1,0:T(8,128)(2,1)} %collective-permute-done.1.refs_0_, bf16[8,256,128]{2,1,0:T(8,128)(2,1)} %collective-permute-done.2.refs_1_, bf16[8,256,128]{2,1,0:T(8,128)(2,1)} %collective-permute-done.3.refs_2_, bf16[8,256,128]{2,1,0:T(8,128)(2,1)} %collective-permute-done.4.refs_3_, ...), custom_call_target="tpu_custom_call" | custom-call | bytes 15204352 | tf_op jit(solution)/shard_map/by_harmonic/pallas_call | solution.py:57
  80.3 0.1 collective-permute-start.8
  80.4 1.4 %bitcast_add_fusion = f32[4,51,8,128]{3,2,1,0:T(8,128)S(1)} fusion(f32[4,51,8,128]{3,2,1,0:T(8,128)} %collective-permute-done.10, f32[4,2,51,8,128]{4,3,2,1,0:T(8,128)S(1)} %copy-done.5, s32[]{:T(128)S(6)} %select_n.223), kind=kLoop, calls=%fused_computation.8 | loop fusion | flops 208896 | bytes 2506756 | tf_op jit(solution)/shard_map/add | solution.py:262
  81.8 1.8 %collective-permute-start.11 = (f32[51,8,128]{2,1,0:T(8,128)S(1)}, f32[51,8,128]{2,1,0:T(8,128)S(1)}, u32[]{:S(2)}, u32[]{:S(2)}) collective-permute-start(f32[51,8,128]{2,1,0:T(8,128)S(1)} %get-tuple-element.2), channel_id=1, source_target_pairs={{0,2},{1,3},{2,4},{3,5},{4,6},{5,7},{6,0},{7,1},{8,10},{9,11},{10,... | collective-permute-start | bytes 626696 | tf_op jit(solution)/shard_map/ppermute | solution.py:188
  83.7 2.9 %collective-permute-start.12 = (f32[51,8,128]{2,1,0:T(8,128)S(1)}, f32[51,8,128]{2,1,0:T(8,128)S(1)}, u32[]{:S(2)}, u32[]{:S(2)}) collective-permute-start(f32[51,8,128]{2,1,0:T(8,128)S(1)} %get-tuple-element.4), channel_id=1, source_target_pairs={{0,4},{1,5},{2,6},{3,7},{4,0},{5,1},{6,2},{7,3},{8,12},{9,13},{10,... | collective-permute-start | bytes 626696 | tf_op jit(solution)/shard_map/ppermute | solution.py:188
  86.6 1.3 %collective-permute-start.13 = (f32[51,8,128]{2,1,0:T(8,128)S(1)}, f32[51,8,128]{2,1,0:T(8,128)S(1)}, u32[]{:S(2)}, u32[]{:S(2)}) collective-permute-start(f32[51,8,128]{2,1,0:T(8,128)S(1)} %get-tuple-element.3), channel_id=1, source_target_pairs={{0,6},{1,7},{2,0},{3,1},{4,2},{5,3},{6,4},{7,5},{8,14},{9,15},{10,... | collective-permute-start | bytes 626696 | tf_op jit(solution)/shard_map/ppermute | solution.py:188
  87.9 11.6 %score.2 = f32[8,128]{1,0:T(8,128)S(1)} custom-call(bf16[9216,128]{1,0:T(8,128)(2,1)S(1)} %bitcast.71, bf16[9216,128]{1,0:T(8,128)(2,1)} %collective-permute-done.refs_1_, bf16[256,64,128]{2,1,0:T(8,128)(2,1)S(1)} %copy-done.2, bf16[256,64,128]{2,1,0:T(8,128)(2,1)S(1)} %by_harmonic.3.refs_3_, bf16[264,256]{1,0:T(8,128)(2,1)S(1)} %fusion.17.refs_4_), custom_call_target="tpu_custom_call" | custom-call | flops 14722007040 | bytes 20000000 | tf_op jit(solution)/shard_map/score/pallas_call | solution.py:156
  99.7 0.8 fusion.15
  100.5 11.6 %score.3 = f32[8,128]{1,0:T(8,128)S(1)} custom-call(bf16[9216,128]{1,0:T(8,128)(2,1)} %collective-permute-done.7.refs_0_, bf16[9216,128]{1,0:T(8,128)(2,1)S(1)} %collective-permute-done.8.refs_1_, bf16[256,64,128]{2,1,0:T(8,128)(2,1)S(1)} %copy-done.2, bf16[256,64,128]{2,1,0:T(8,128)(2,1)S(1)} %by_harmonic.3.refs_3_, bf16[264,256]{1,0:T(8,128)(2,1)S(1)} %fusion.17.refs_4_), custom_call_target="tpu_custom_call" | custom-call | flops 14722007040 | bytes 20000000 | tf_op jit(solution)/shard_map/score/pallas_call | solution.py:156
  112.2 4.8 %collective-permute-done.9 = f32[16,52]{1,0:T(8,128)S(1)} collective-permute-done((f32[16,52]{1,0:T(8,128)S(1)}, f32[16,52]{1,0:T(8,128)S(1)}, u32[]{:S(2)}, u32[]{:S(2)}) %collective-permute-start.9) | collective-permute-done | bytes 3360 | tf_op jit(solution)/shard_map/ppermute | solution.py:188
  117.2 0.1 concatenate.80
  117.3 0.1 concatenate.77
  117.5 0.1 fusion.26
  117.7 0.6 reverse_select_fusion
  (50 shorter events, 1.0 us)
Async XLA Ops:
  3.2 15.5 %copy-start = (bf16[256,50,128]{2,0,1:T(8,128)(2,1)S(1)}, bf16[256,50,128]{2,0,1:T(8,128)(2,1)}, u32[]{:S(2)}) copy-start(bf16[256,50,128]{2,0,1:T(8,128)(2,1)} %param.7) | copy-start | bytes 9830404
  7.4 39.8 %all-to-all-start = ((bf16[32,8,16,128]{3,2,1,0:T(8,128)(2,1)}), bf16[32,8,16,128]{3,2,1,0:T(8,128)(2,1)}, u32[]{:S(2)}, u32[]{:S(2)}) async-start(bf16[32,8,16,128]{3,2,1,0:T(8,128)(2,1)} %bitcast.77), calls=%async_computation | async-start | bytes 2097152 | tf_op jit(solution)/shard_map/all_to_all | solution.py:247
  19.6 16.3 %collective-permute-start.2 = (bf16[8,256,128]{2,1,0:T(8,128)(2,1)}, bf16[8,256,128]{2,1,0:T(8,128)(2,1)}, u32[]{:S(2)}, u32[]{:S(2)}) collective-permute-start(bf16[8,256,128]{2,1,0:T(8,128)(2,1)} %dynamic-slice_bitcast_fusion.1), channel_id=1, source_target_pairs={{0,6},{1,7},{2,4},{3,5},{4,2},{5,3},{6,0},{7,1},{8,14},{9,15},{10,... | collective-permute-start | bytes 1572872 | tf_op jit(solution)/shard_map/ppermute | solution.py:188
  22.6 65.3 %collective-permute-start = (bf16[9216,128]{1,0:T(8,128)(2,1)}, bf16[9216,128]{1,0:T(8,128)(2,1)}, u32[]{:S(2)}, u32[]{:S(2)}) collective-permute-start(bf16[9216,128]{1,0:T(8,128)(2,1)} %bitcast.69), channel_id=1, source_target_pairs={{0,1},{1,0},{2,3},{3,2},{4,5},{5,4},{6,7},{7,6},{8,9},{9,8},{10,11... | collective-permute-start | bytes 7077896 | tf_op jit(solution)/shard_map/ppermute | solution.py:188
  22.6 57.7 %collective-permute-start.7 = (bf16[9216,128]{1,0:T(8,128)(2,1)}, bf16[9216,128]{1,0:T(8,128)(2,1)}, u32[]{:S(2)}, u32[]{:S(2)}) collective-permute-start(bf16[9216,128]{1,0:T(8,128)(2,1)} %bitcast.70), channel_id=1, source_target_pairs={{0,2},{1,3},{2,0},{3,1},{4,6},{5,7},{6,4},{7,5},{8,10},{9,11},{10,... | collective-permute-start | bytes 7077896 | tf_op jit(solution)/shard_map/ppermute | solution.py:188
  24.0 51.3 %collective-permute-start.1 = (bf16[20,256,128]{2,1,0:T(8,128)(2,1)}, bf16[20,256,128]{2,1,0:T(8,128)(2,1)}, u32[]{:S(2)}, u32[]{:S(2)}) collective-permute-start(bf16[20,256,128]{2,1,0:T(8,128)(2,1)} %slice.96), channel_id=1, source_target_pairs={{0,6},{1,7},{2,4},{3,5},{4,2},{5,3},{6,0},{7,1},{8,14},{9,15},{10,... | collective-permute-start | bytes 3932168 | tf_op jit(solution)/shard_map/ppermute | solution.py:188
  35.9 19.3 %collective-permute-start.3 = (bf16[8,256,128]{2,1,0:T(8,128)(2,1)}, bf16[8,256,128]{2,1,0:T(8,128)(2,1)}, u32[]{:S(2)}, u32[]{:S(2)}) collective-permute-start(bf16[8,256,128]{2,1,0:T(8,128)(2,1)} %collective-permute-done.2.refs_1_), channel_id=1, source_target_pairs={{0,64},{8,72},{16,80},{24,88},{32,96},{40,104},{48,112},{56,120},{... | collective-permute-start | bytes 1572872 | tf_op jit(solution)/shard_map/ppermute | solution.py:202
  37.4 19.7 %collective-permute-start.4 = (bf16[8,256,128]{2,1,0:T(8,128)(2,1)}, bf16[8,256,128]{2,1,0:T(8,128)(2,1)}, u32[]{:S(2)}, u32[]{:S(2)}) collective-permute-start(bf16[8,256,128]{2,1,0:T(8,128)(2,1)} %collective-permute-done.2.refs_1_), channel_id=1, source_target_pairs={{0,192},{8,200},{16,208},{24,216},{32,224},{40,232},{48,240},{56,2... | collective-permute-start | bytes 1572872 | tf_op jit(solution)/shard_map/ppermute | solution.py:202
  54.1 13.0 %copy-start.4 = (f32[4,2,51,8,128]{4,3,2,1,0:T(8,128)}, f32[4,2,51,8,128]{4,3,2,1,0:T(8,128)S(1)}, u32[]{:S(2)}) copy-start(f32[4,2,51,8,128]{4,3,2,1,0:T(8,128)S(1)} %select_maximum_fusion) | copy-start | bytes 5013508
  55.2 25.2 %collective-permute-start.10 = (f32[4,51,8,128]{3,2,1,0:T(8,128)}, f32[4,51,8,128]{3,2,1,0:T(8,128)}, u32[]{:S(2)}, u32[]{:S(2)}) collective-permute-start(f32[4,51,8,128]{3,2,1,0:T(8,128)} %dynamic-slice_bitcast_fusion), channel_id=1, source_target_pairs={{0,1},{1,0},{2,3},{3,2},{4,5},{5,4},{6,7},{7,6},{8,9},{9,8},{10,11... | collective-permute-start | bytes 2506760 | tf_op jit(solution)/shard_map/ppermute | solution.py:188
  57.1 10.0 %collective-permute-start.5 = (bf16[4,256,128]{2,1,0:T(8,128)(2,1)S(1)}, bf16[4,256,128]{2,1,0:T(8,128)(2,1)S(1)}, u32[]{:S(2)}, u32[]{:S(2)}) collective-permute-start(bf16[4,256,128]{2,1,0:T(8,128)(2,1)S(1)} %slice.97), channel_id=1, source_target_pairs={{0,64},{8,72},{16,80},{24,88},{32,96},{40,104},{48,112},{56,120},{... | collective-permute-start | bytes 786440 | tf_op jit(solution)/shard_map/ppermute | solution.py:202
  67.1 8.2 %collective-permute-start.6 = (bf16[4,256,128]{2,1,0:T(8,128)(2,1)}, bf16[4,256,128]{2,1,0:T(8,128)(2,1)}, u32[]{:S(2)}, u32[]{:S(2)}) collective-permute-start(bf16[4,256,128]{2,1,0:T(8,128)(2,1)} %slice.98), channel_id=1, source_target_pairs={{0,192},{8,200},{16,208},{24,216},{32,224},{40,232},{48,240},{56,2... | collective-permute-start | bytes 786440 | tf_op jit(solution)/shard_map/ppermute | solution.py:202
  70.1 1.9 %copy-start.1 = (bf16[256,64,128]{2,1,0:T(8,128)(2,1)}, bf16[256,64,128]{2,1,0:T(8,128)(2,1)S(1)}, u32[]{:S(2)}) copy-start(bf16[256,64,128]{2,1,0:T(8,128)(2,1)S(1)} %by_harmonic.2.refs_2_) | copy-start | bytes 12582916
  73.2 7.2 %copy-start.5 = (f32[4,2,51,8,128]{4,3,2,1,0:T(8,128)S(1)}, f32[4,2,51,8,128]{4,3,2,1,0:T(8,128)}, u32[]{:S(2)}) copy-start(f32[4,2,51,8,128]{4,3,2,1,0:T(8,128)} %copy-done.4) | copy-start | bytes 5013508
  75.2 12.7 %copy-start.2 = (bf16[256,64,128]{2,1,0:T(8,128)(2,1)S(1)}, bf16[256,64,128]{2,1,0:T(8,128)(2,1)}, u32[]{:S(2)}) copy-start(bf16[256,64,128]{2,1,0:T(8,128)(2,1)} %copy-done.1) | copy-start | bytes 12582916
  80.3 7.7 %copy-start.3 = (bf16[256,4,9,128]{3,1,2,0:T(4,128)(2,1)S(1)}, bf16[256,4,9,128]{3,1,2,0:T(4,128)(2,1)}, u32[]{:S(2)}) copy-start(bf16[256,4,9,128]{3,1,2,0:T(4,128)(2,1)} %param.6) | copy-start | bytes 7077892
  80.3 20.2 %collective-permute-start.8 = (bf16[9216,128]{1,0:T(8,128)(2,1)}, bf16[9216,128]{1,0:T(8,128)(2,1)S(1)}, u32[]{:S(2)}, u32[]{:S(2)}) collective-permute-start(bf16[9216,128]{1,0:T(8,128)(2,1)} %collective-permute-done.7.refs_0_), channel_id=1, source_target_pairs={{0,1},{1,0},{2,3},{3,2},{4,5},{5,4},{6,7},{7,6},{8,9},{9,8},{10,11... | collective-permute-start | bytes 7077896 | tf_op jit(solution)/shard_map/ppermute | solution.py:188
  81.8 17.7 %collective-permute-start.11 = (f32[51,8,128]{2,1,0:T(8,128)S(1)}, f32[51,8,128]{2,1,0:T(8,128)S(1)}, u32[]{:S(2)}, u32[]{:S(2)}) collective-permute-start(f32[51,8,128]{2,1,0:T(8,128)S(1)} %get-tuple-element.2), channel_id=1, source_target_pairs={{0,2},{1,3},{2,4},{3,5},{4,6},{5,7},{6,0},{7,1},{8,10},{9,11},{10,... | collective-permute-start | bytes 626696 | tf_op jit(solution)/shard_map/ppermute | solution.py:188
  83.7 15.9 %collective-permute-start.12 = (f32[51,8,128]{2,1,0:T(8,128)S(1)}, f32[51,8,128]{2,1,0:T(8,128)S(1)}, u32[]{:S(2)}, u32[]{:S(2)}) collective-permute-start(f32[51,8,128]{2,1,0:T(8,128)S(1)} %get-tuple-element.4), channel_id=1, source_target_pairs={{0,4},{1,5},{2,6},{3,7},{4,0},{5,1},{6,2},{7,3},{8,12},{9,13},{10,... | collective-permute-start | bytes 626696 | tf_op jit(solution)/shard_map/ppermute | solution.py:188
  86.6 13.0 %collective-permute-start.13 = (f32[51,8,128]{2,1,0:T(8,128)S(1)}, f32[51,8,128]{2,1,0:T(8,128)S(1)}, u32[]{:S(2)}, u32[]{:S(2)}) collective-permute-start(f32[51,8,128]{2,1,0:T(8,128)S(1)} %get-tuple-element.3), channel_id=1, source_target_pairs={{0,6},{1,7},{2,0},{3,1},{4,2},{5,3},{6,4},{7,5},{8,14},{9,15},{10,... | collective-permute-start | bytes 626696 | tf_op jit(solution)/shard_map/ppermute | solution.py:188
  112.2 4.9 %collective-permute-start.9 = (f32[16,52]{1,0:T(8,128)S(1)}, f32[16,52]{1,0:T(8,128)S(1)}, u32[]{:S(2)}, u32[]{:S(2)}) collective-permute-start(f32[16,52]{1,0:T(8,128)S(1)} %pad_maximum_fusion.1), channel_id=1, source_target_pairs={{0,6},{1,7},{2,4},{3,5},{4,2},{5,3},{6,0},{7,1},{8,14},{9,15},{10,... | collective-permute-start | bytes 9992 | tf_op jit(solution)/shard_map/ppermute | solution.py:188

commit v4 on v3

--- a/solution.py
+++ b/solution.py
@@ -12,6 +12,7 @@
 CHUNK = 16
 LANES = 128
 WHOLE = pl.BlockSpec(memory_space=pltpu.VMEM)
+SCALARS = pl.BlockSpec(memory_space=pltpu.SMEM)
 
 
 def folded_table(angles):
@@ -33,16 +34,18 @@
     return jnp.concatenate(rows, axis=0).astype(jnp.bfloat16)
 
 
-def gather_kernel(sizes, starts, *refs):
+def gather_kernel(sizes, starts_ref, *refs):
     pieces, out_ref, work = refs[: len(sizes)], refs[len(sizes)], refs[len(sizes) + 1]
     total = out_ref.shape[1]
-    work[...] = jnp.zeros(work.shape, jnp.float32)
+    used = sum(sizes)
+    work[pl.ds(used * CHUNK, (total - used) * CHUNK), :] = jnp.zeros(((total - used) * CHUNK, LANES), jnp.float32)
 
     def chunk(j, carry):
         base = pl.multiple_of(j * CHUNK, CHUNK)
-        for size, start, ref in zip(sizes, starts, pieces):
+        for k, (size, ref) in enumerate(zip(sizes, pieces)):
             block = ref[:, pl.ds(base, CHUNK), :].reshape(size * CHUNK, LANES)
-            work[pl.ds(start * CHUNK, size * CHUNK), :] = block.astype(jnp.float32)
+            first = pl.multiple_of(starts_ref[k] * CHUNK, CHUNK)
+            work[pl.ds(first, size * CHUNK), :] = block.astype(jnp.float32)
         for t in range(CHUNK):
             out_ref[base + t] = work[pl.ds(t, total, stride=CHUNK), :].astype(jnp.bfloat16)
         return carry
@@ -55,22 +58,27 @@
     sizes = tuple(piece.shape[0] for piece in pieces)
     moved = 2 * angles * cycle_parts * (sum(sizes) + total)
     return pl.pallas_call(
-        functools.partial(gather_kernel, sizes, tuple(starts)),
-        in_specs=[WHOLE] * len(pieces),
+        functools.partial(gather_kernel, sizes),
+        in_specs=[SCALARS] + [WHOLE] * len(pieces),
         out_specs=WHOLE,
         out_shape=jax.ShapeDtypeStruct((angles, total, cycle_parts), jnp.bfloat16),
         scratch_shapes=[pltpu.VMEM((total * CHUNK, cycle_parts), jnp.float32)],
-        compiler_params=pltpu.CompilerParams(vmem_limit_bytes=30 * 1024 * 1024),
+        compiler_params=pltpu.CompilerParams(vmem_limit_bytes=14 * 1024 * 1024),
         cost_estimate=pl.CostEstimate(flops=0, bytes_accessed=2 * moved, transcendentals=0),
         name="by_harmonic",
-    )(*pieces)
-
-
-def score_kernel(scale, rows, shifts, groups, *refs):
-    images, stacked = refs[:groups], refs[groups : groups + 2]
-    table_ref, out_ref, left_ref, fa, fb, folded = refs[groups + 2 :]
+    )(jnp.asarray(starts, jnp.int32), *pieces)
+
+
+def score_kernel(scale, rows, shifts, counts, places_ref, *refs):
+    groups, pieces = len(counts), sum(counts)
+    firsts = [sum(counts[:g]) for g in range(groups)]
+    lowers = [refs[first] for first in firsts]
+    uppers = [refs[first + count - 1] for first, count in zip(firsts, counts)]
+    stacked = refs[pieces : pieces + 2]
+    table_ref, out_ref, left_ref, fa, fb, folded = refs[pieces + 2 :]
     half = table_ref.shape[1] // 2
     all_rows = 2 * rows * groups
+    pitch = all_rows + 1
     cycles = LANES // 2
     lane = lax.broadcasted_iota(jnp.int32, (1, LANES), 1)
     sign = jnp.where(lane < cycles, 1.0, -1.0)
@@ -79,11 +87,13 @@
     def chunk(j, carry):
         back = 2 * half - CHUNK - j * CHUNK
         edge = jnp.where(j == 0, half, 2 * half - CHUNK * j)
-        for g, image in enumerate(images):
-            fa[g] = image[pl.ds(pl.multiple_of(j * block, block), block), :].astype(jnp.float32)
-            fb[g, pl.ds(0, block), :] = image[pl.ds(pl.multiple_of(back * rows, block), block), :].astype(jnp.float32)
-            edge_rows = pl.multiple_of(edge * rows, block)
-            fb[g, pl.ds(block, 2 * rows), :] = image[pl.ds(edge_rows, 2 * rows), :].astype(jnp.float32)
+        for g, (lower, upper) in enumerate(zip(lowers, uppers)):
+            skip = upper.shape[0] // rows - 2 * half
+            fa[g] = lower[pl.ds(pl.multiple_of(j * block, block), block), :].astype(jnp.float32)
+            back_rows = pl.multiple_of((back + skip) * rows, block)
+            fb[g, pl.ds(0, block), :] = upper[pl.ds(back_rows, block), :].astype(jnp.float32)
+            edge_rows = pl.multiple_of((edge + skip) * rows, block)
+            fb[g, pl.ds(block, 2 * rows), :] = upper[pl.ds(edge_rows, 2 * rows), :].astype(jnp.float32)
         paired = jnp.where(j == 0, 0.0, 1.0)
         for t in range(CHUNK):
             slot = t % left_ref.shape[0]
@@ -110,7 +120,7 @@
                 ],
                 axis=1,
             )
-            folded[pl.ds(pl.multiple_of(m * all_rows, 8), all_rows), :] = lax.dot_general(
+            folded[pl.ds(m * pitch, all_rows), :] = lax.dot_general(
                 left_ref[slot].astype(jnp.bfloat16),
                 right,
                 (((1,), (1,)), ((), ())),
@@ -124,8 +134,8 @@
     width = 2 * LANES
 
     def column(g, n):
-        even = folded[pl.ds(2 * rows * g + n, half, stride=all_rows), :]
-        odd = folded[pl.ds(2 * rows * g + rows + n, half, stride=all_rows), :]
+        even = folded[pl.ds(2 * rows * g + n, half, stride=pitch), :]
+        odd = folded[pl.ds(2 * rows * g + rows + n, half, stride=pitch), :]
         return jnp.concatenate([even, odd], axis=0).astype(jnp.bfloat16)
 
     def one_shift(s, best):
@@ -143,31 +153,33 @@
     best = lax.fori_loop(0, shifts, one_shift, start)
     for q in range(groups * each // 2):
         top = jnp.max(best[q], axis=0, keepdims=True) * scale
-        out_ref[2 * q : 2 * q + 1, :] = top[:, :LANES]
-        out_ref[2 * q + 1 : 2 * q + 2, :] = top[:, LANES:]
-
-
-def best_of_groups(images, stacked, table, shifts, rows, scale):
+        first = places_ref[2 * q // each] * each + 2 * q % each
+        out_ref[pl.ds(first, 1), :] = top[:, :LANES]
+        out_ref[pl.ds(first + 1, 1), :] = top[:, LANES:]
+
+
+def best_of_groups(places, images, stacked, table, shifts, rows, scale):
     angles, _, cycle_parts = stacked[0].shape
     half = angles // 2
     each = rows // shifts
     groups = len(images)
+    counts = tuple(len(image) for image in images)
     flops = groups * (2 * half * 2 * rows * 2 * cycle_parts * LANES + 2 * rows * LANES * angles * (angles + 8))
     return pl.pallas_call(
-        functools.partial(score_kernel, scale, rows, shifts, groups),
-        in_specs=[WHOLE] * (groups + 3),
+        functools.partial(score_kernel, scale, rows, shifts, counts),
+        in_specs=[SCALARS] + [WHOLE] * (sum(counts) + 3),
         out_specs=WHOLE,
         out_shape=jax.ShapeDtypeStruct((groups * each, LANES), jnp.float32),
         scratch_shapes=[
             pltpu.VMEM((4, 2 * rows * groups, 2 * cycle_parts), jnp.float32),
             pltpu.VMEM((groups, CHUNK * rows, cycle_parts), jnp.float32),
             pltpu.VMEM((groups, (CHUNK + 2) * rows, cycle_parts), jnp.float32),
-            pltpu.VMEM((2 * rows * groups * half, LANES), jnp.float32),
+            pltpu.VMEM(((2 * rows * groups + 1) * half, LANES), jnp.float32),
         ],
-        compiler_params=pltpu.CompilerParams(vmem_limit_bytes=34 * 1024 * 1024),
+        compiler_params=pltpu.CompilerParams(vmem_limit_bytes=36 * 1024 * 1024),
         cost_estimate=pl.CostEstimate(flops=6 * flops, bytes_accessed=20_000_000, transcendentals=0),
         name="score",
-    )(*images, *stacked, table)
+    )(places, *[piece for image in images for piece in image], *stacked, table)
 
 
 def on_device(particles, references, class_ids, counts, shift_ids, weights):
@@ -177,6 +189,7 @@
     angles, own, shifts, cycle_parts = particles.shape
     class_count = references.shape[1]
     list_length = class_ids.shape[1]
+    half = angles // 2
     rows = shifts * own
     doms = 32
     chips = 4
@@ -205,24 +218,33 @@
     flat = native.reshape(angles * rows, cycle_parts)
     class_major = jnp.transpose(references, (1, 0, 2))
 
+    lower, again = lax.optimization_barrier((flat[: half * rows], flat))
+    upper = again[half * rows :]
+    lower_partner = move(lower, lambda y, c: (y ^ 1, c))
+    upper_partner = move(upper, lambda y, c: (y ^ 1, c))
+    mate = across(flat)
+    lower_both = across(lower_partner)
+    upper_both = across(upper_partner)
+
     place = lax.axis_index("dom") // (doms // ring)
-    straight = 20
-    window = -(-(class_count - straight) // ring)
-    first = jnp.minimum(straight + window * place, class_count - window)
-    piece = facing(lax.dynamic_slice_in_dim(class_major, first, window, 0))
-    direct = facing(class_major[:straight])
+    window = class_count // (ring + 1)
+    straight = class_count - ring * window
+
+    def window_of(x):
+        return lax.dynamic_slice_in_dim(class_major, straight + window * x, window, 0)
+
+    piece = facing(window_of(place))
+    far = facing(jnp.concatenate([class_major[:straight], window_of((place + 2) % ring)]))
     from_left = around(piece, 1)
     from_right = around(piece, -1)
-    far_upper = around(from_left[: window // 2], 1)
-    far_lower = around(from_right[window // 2 :], -1)
-
-    partner = move(flat, lambda y, c: (y ^ 1, c))
-    mate = across(flat)
-    partner_mate = across(partner)
 
     own_set = by_harmonic([class_major], [0], LANES // 2)
-    starts = [0, straight, straight + window, straight + 2 * window, straight + 3 * window, straight + 3 * window + window // 2]
-    facing_set = by_harmonic([direct, piece, from_left, from_right, far_upper, far_lower], starts, LANES // 2)
+    starts = [straight + window * ((place + step) % ring) for step in (0, 3, 1, 2)]
+    facing_set = by_harmonic(
+        [far[:straight], piece, from_left, from_right, far[straight:]],
+        jnp.stack([jnp.zeros_like(place)] + starts),
+        LANES // 2,
+    )
     stacked = [own_set, facing_set]
     table = folded_table(angles)
     score = functools.partial(best_of_groups, stacked=stacked, table=table, shifts=shifts, rows=rows, scale=scale)
@@ -268,25 +290,14 @@
     class_means = total[:class_count] / jnp.maximum(weight_sums, 1.0)[:, None, None]
     class_means = jnp.transpose(class_means, (1, 0, 2))
 
-    home = score([flat, mate])
-    away = score([partner, partner_mate])
-    best = jnp.concatenate([home, away], axis=0)
-    lanes_of = LANES // 2
-    sent = facing(best[:, lanes_of : lanes_of + straight + ring * window])
-    by_step = [sent[:, straight + window * k : straight + window * (k + 1)] for k in (0, 2, 3, 1)]
-    overlap = straight + ring * window - class_count
-    ordered = []
-    for x in range(ring):
-        columns = [by_step[(k - x) % ring] for k in range(ring)]
-        columns[-1] = columns[-1][:, overlap:]
-        ordered.append(jnp.concatenate([sent[:, :straight]] + columns, axis=1))
-    others = lax.select_n(place, *ordered)
-    own_best = best[:, :class_count].reshape(2, 2, own, class_count)
-    facing_best = others.reshape(2, 2, own, class_count)
-    grid = jnp.stack([own_best, facing_best[::-1]])
-    for axis, bit in ((0, row // 2), (1, row % 2), (2, core)):
-        grid = jnp.where(bit == 1, jnp.flip(grid, axis), grid)
-    best_scores = grid.reshape(2 * chips * own, class_count)
+    images = [(flat,), (mate,), (lower_partner, upper_partner), (lower_both, upper_both)]
+    places = jnp.stack([(row % 2 ^ chip) * 2 + (core ^ other) for chip in range(2) for other in range(2)])
+    best = score(places.astype(jnp.int32), images)
+    sent = facing(best)
+    mine, others = best[:, :class_count], sent[:, LANES // 2 : LANES // 2 + class_count]
+    low = jnp.where(row < chips // 2, mine, others)
+    high = jnp.where(row < chips // 2, others, mine)
+    best_scores = jnp.concatenate([low, high], axis=0)
     return (best_scores, class_means)
 
 

time: 119 us -> 137 us (1.15)
  the two profiles are of different devices: /device:TPU:32 before, /device:TPU:8 now
where the time goes in v4:
time: 137 us; the launch traced here: 136 us
  waiting for transfers between devices  56.4 us (41%)
  starting transfers between devices  25.9 us (19%)
  Pallas kernels  23.2 us (17%)
  local copies, waits for them, and re-layouts  18.1 us (13%)
  matrix products  6.34 us (5%)
  other arithmetic  5.09 us (4%)
    ppermute x12, waiting for transfers between devices, move(): return lax.ppermute(value, 'cls', pairs)  47.8 us
    pallas_call x1, Pallas kernels, best_of_groups(): pl.pallas_call(functools.partial(score_kernel, scale, rows, shifts, count...  15.7 us
    ppermute x12, starting transfers between devices, move(): return lax.ppermute(value, 'cls', pairs)  11.8 us
    all_to_all x1, starting transfers between devices, on_device(): arrived = lax.all_to_all(payload, 'dom', 0, 0, tiled=True)  11.4 us
    ppermute x2, waiting for transfers between devices, around(): return lax.ppermute(value, 'dom', pairs)  8.66 us
    pallas_call x2, Pallas kernels, by_harmonic(): pl.pallas_call(functools.partial(gather_kernel, sizes), in_specs=[SCALARS...  7.49 us
    unnamed x13, local copies, waits for them, and re-layouts  6.15 us
    dot_general x1, matrix products, on_device(): jnp.einsum('lsi,msic->mlc', pick, native, preferred_element_type=jnp.floa...  4.05 us
  transfers between devices with their start and end apart: 15, of which 5 were waited for; matrix products, arithmetic and copies ran while one was open for 12% of the time, Pallas kernels for 17%

profile of v4, /device:TPU:8, one launch (start us, length us, event | category | flops | bytes accessed | tf_op | source)
XLA Modules:
  0.0 136.0 jit_solution(9762286770255575865)
XLA Ops:
  0.6 0.8 reshape.284
  1.4 0.8 eq.103
  2.2 0.8 fusion.31
  3.2 4.0 %fusion.4 = bf16[16,256,128]{2,0,1:T(8,128)(2,1)} fusion(bf16[256,9,4,128]{3,2,1,0:T(4,128)(2,1)} %bitcast.4, bf16[16,128]{1,0:T(8,128)(2,1)S(1)} %select_maximum_fusion.1, pred[12,9,4]{1,0,2:T(8,128)(4,1)S(1)} %broadcast_and_fusion), kind=kOutput, calls=%fused_computation.7 | convolution fusion | flops 38797312 | bytes 3412400 | tf_op jit(solution)/shard_map/lsi,msic->mlc/dot_general | solution.py:260
  7.3 11.4 %all-to-all-start = ((bf16[32,8,16,128]{3,2,1,0:T(8,128)(2,1)}), bf16[32,8,16,128]{3,2,1,0:T(8,128)(2,1)}, u32[]{:S(2)}, u32[]{:S(2)}) async-start(bf16[32,8,16,128]{3,2,1,0:T(8,128)(2,1)} %bitcast.19), calls=%async_computation | async-start | bytes 2097152 | tf_op jit(solution)/shard_map/all_to_all | solution.py:269
  18.7 2.9 %slice.56 = bf16[128,9,4,128]{3,2,1,0:T(4,128)(2,1)} slice(bf16[256,9,4,128]{3,2,1,0:T(4,128)(2,1)} %bitcast.4), slice={[0:128], [0:9], [0:4], [0:128]} | slice | bytes 2359296 | tf_op jit(solution)/shard_map/slice | solution.py:221
  21.6 2.4 %slice.44 = bf16[4608,128]{1,0:T(8,128)(2,1)} slice(bf16[9216,128]{1,0:T(8,128)(2,1)} %bitcast.5.refs_0_), slice={[4608:9216], [0:128]} | slice | bytes 2359296 | tf_op jit(solution)/shard_map/slice | solution.py:222
  24.0 0.4 collective-permute-start.2
  24.4 0.9 slice.57
  25.4 1.0 dynamic-slice_bitcast_fusion.1
  26.4 0.3 copy-done.5
  26.6 1.2 pad_maximum_fusion
  27.9 2.4 %collective-permute-start.5 = (bf16[20,256,128]{2,1,0:T(8,128)(2,1)}, bf16[20,256,128]{2,1,0:T(8,128)(2,1)}, u32[]{:S(2)}, u32[]{:S(2)}) collective-permute-start(bf16[20,256,128]{2,1,0:T(8,128)(2,1)} %pad_maximum_fusion), channel_id=1, source_target_pairs={{0,6},{1,7},{2,4},{3,5},{4,2},{5,3},{6,0},{7,1},{8,14},{9,15},{10,... | collective-permute-start | bytes 3932168 | tf_op jit(solution)/shard_map/ppermute | solution.py:201
  30.3 1.3 collective-permute-start.1
  31.6 0.5 collective-permute-start.6
  32.1 0.3 cosine_convert_fusion
  32.5 40.4 %collective-permute-done.6.refs_1_ = bf16[10,256,128]{2,1,0:T(8,128)(2,1)} collective-permute-done((bf16[10,256,128]{2,1,0:T(8,128)(2,1)}, bf16[10,256,128]{2,1,0:T(8,128)(2,1)}, u32[]{:S(2)}, u32[]{:S(2)}) %collective-permute-start.6) | collective-permute-done | bytes 655392 | tf_op jit(solution)/shard_map/ppermute | solution.py:201
  72.9 2.7 %collective-permute-start.8 = (bf16[10,256,128]{2,1,0:T(8,128)(2,1)}, bf16[10,256,128]{2,1,0:T(8,128)(2,1)}, u32[]{:S(2)}, u32[]{:S(2)}) collective-permute-start(bf16[10,256,128]{2,1,0:T(8,128)(2,1)} %collective-permute-done.6.refs_1_), channel_id=1, source_target_pairs={{0,192},{8,200},{16,208},{24,216},{32,224},{40,232},{48,240},{56,2... | collective-permute-start | bytes 1966088 | tf_op jit(solution)/shard_map/ppermute | solution.py:215
  75.7 3.0 %by_harmonic.2.refs_6_ = bf16[256,64,128]{2,1,0:T(8,128)(2,1)S(1)} custom-call(s32[1]{0:T(128)} %constant.197.clone.starts_ref, bf16[50,256,128]{2,1,0:T(8,128)(2,1)S(1)} %bitcast.61), custom_call_target="tpu_custom_call" | custom-call | bytes 14942208 | tf_op jit(solution)/shard_map/by_harmonic/pallas_call | solution.py:60
  78.7 2.0 %copy-done.1 = bf16[256,64,128]{2,1,0:T(8,128)(2,1)} copy-done((bf16[256,64,128]{2,1,0:T(8,128)(2,1)}, bf16[256,64,128]{2,1,0:T(8,128)(2,1)S(1)}, u32[]{:S(2)}) %copy-start.1) | copy-done | bytes 4194328
  80.9 0.3 select_convert_fusion
  81.2 0.1 collective-permute-start.4
  81.3 0.5 collective-permute-start.3
  81.8 1.4 %fusion.37 = (bf16[10,256,128]{2,1,0:T(8,128)(2,1)S(1)}, bf16[10,256,128]{2,1,0:T(8,128)(2,1)S(1)}) fusion(bf16[20,256,128]{2,1,0:T(8,128)(2,1)} %collective-permute-done.5), kind=kLoop, calls=%fused_computation.87 | loop fusion | bytes 2621440 | tf_op jit(solution)/shard_map/slice | solution.py:244
  83.2 5.3 %collective-permute-done.8.refs_3_ = bf16[10,256,128]{2,1,0:T(8,128)(2,1)} collective-permute-done((bf16[10,256,128]{2,1,0:T(8,128)(2,1)}, bf16[10,256,128]{2,1,0:T(8,128)(2,1)}, u32[]{:S(2)}, u32[]{:S(2)}) %collective-permute-start.8) | collective-permute-done | bytes 655392 | tf_op jit(solution)/shard_map/ppermute | solution.py:215
  88.5 3.3 %collective-permute-done.7.refs_2_ = bf16[10,256,128]{2,1,0:T(8,128)(2,1)} collective-permute-done((bf16[10,256,128]{2,1,0:T(8,128)(2,1)}, bf16[10,256,128]{2,1,0:T(8,128)(2,1)}, u32[]{:S(2)}, u32[]{:S(2)}) %collective-permute-start.7) | collective-permute-done | bytes 655392 | tf_op jit(solution)/shard_map/ppermute | solution.py:215
  91.9 4.5 %by_harmonic.3.refs_7_ = bf16[256,64,128]{2,1,0:T(8,128)(2,1)S(1)} custom-call(s32[5]{0:T(128)S(1)} %stack.39.starts_ref, bf16[10,256,128]{2,1,0:T(8,128)(2,1)S(1)} %get-tuple-element.9.refs_0_, bf16[10,256,128]{2,1,0:T(8,128)(2,1)} %collective-permute-done.6.refs_1_, bf16[10,256,128]{2,1,0:T(8,128)(2,1)} %collective-permute-done.7.refs_2_, ...), custom_call_target="tpu_custom_call" | custom-call | bytes 14942208 | tf_op jit(solution)/shard_map/by_harmonic/pallas_call | solution.py:60
  96.3 2.1 %copy-done.3 = bf16[256,64,128]{2,1,0:T(8,128)(2,1)} copy-done((bf16[256,64,128]{2,1,0:T(8,128)(2,1)}, bf16[256,64,128]{2,1,0:T(8,128)(2,1)S(1)}, u32[]{:S(2)}) %copy-start.3) | copy-done | bytes 4194328
  98.4 0.9 slice.62
  99.3 0.1 copy.29
  99.4 0.2 convert_reduce_fusion
  99.6 0.1 reshape.288
  99.7 0.2 fusion.8
  99.9 2.3 %convolution_bitcast_fusion = f32[400,8,128]{2,0,1:T(8,128)S(1)} fusion(bf16[32,8,16,128]{3,2,1,0:T(8,128)(2,1)} %all-to-all-done, bf16[400,32,12]{0,1,2:T(8,128)(2,1)S(1)} %fusion.8), kind=kOutput, calls=%fused_computation.5 | convolution fusion | flops 419430400 | bytes 2994176 | tf_op jit(solution)/shard_map/ksl,smlc->kmc/dot_general | solution.py:277
  102.2 0.5 copy.26
  102.7 0.1 select_maximum_fusion
  102.9 0.3 collective-permute-start.10
  103.2 1.7 %copy-done.2 = bf16[256,64,128]{2,1,0:T(8,128)(2,1)S(1)} copy-done((bf16[256,64,128]{2,1,0:T(8,128)(2,1)S(1)}, bf16[256,64,128]{2,1,0:T(8,128)(2,1)}, u32[]{:S(2)}) %copy-start.2) | copy-done | bytes 4194328
  104.9 15.7 %score.1 = f32[16,128]{1,0:T(8,128)S(1)} custom-call(s32[4]{0:T(128)S(1)} %pad_add_fusion.places_ref, bf16[9216,128]{1,0:T(8,128)(2,1)} %bitcast.5.refs_0_, bf16[9216,128]{1,0:T(8,128)(2,1)} %collective-permute-done.refs_1_, bf16[4608,128]{1,0:T(8,128)(2,1)} %collective-permute-done.1.refs_2_, bf16[4608,128]{1,0:T(8,128)(2,1)} %collective-permute-done.2.refs_3_, ...), custom_call_target="tpu_custom_call" | custom-call | flops 29444014080 | bytes 20000000 | tf_op jit(solution)/shard_map/score/pallas_call | solution.py:168
  120.7 1.5 %collective-permute-start.9 = (f32[16,128]{1,0:T(8,128)S(1)}, f32[16,128]{1,0:T(8,128)S(1)}, u32[]{:S(2)}, u32[]{:S(2)}) collective-permute-start(f32[16,128]{1,0:T(8,128)S(1)} %score.1), channel_id=1, source_target_pairs={{0,6},{1,7},{2,4},{3,5},{4,2},{5,3},{6,0},{7,1},{8,14},{9,15},{10,... | collective-permute-start | bytes 24584 | tf_op jit(solution)/shard_map/ppermute | solution.py:201
  122.2 0.1 bitcast_add_fusion
  122.4 0.6 collective-permute-start.11
  123.1 2.1 %collective-permute-start.13 = (f32[51,8,128]{2,1,0:T(8,128)S(1)}, f32[51,8,128]{2,1,0:T(8,128)S(1)}, u32[]{:S(2)}, u32[]{:S(2)}) collective-permute-start(f32[51,8,128]{2,1,0:T(8,128)S(1)} %get-tuple-element.11), channel_id=1, source_target_pairs={{0,6},{1,7},{2,0},{3,1},{4,2},{5,3},{6,4},{7,5},{8,14},{9,15},{10,... | collective-permute-start | bytes 626696 | tf_op jit(solution)/shard_map/ppermute | solution.py:201
  125.1 2.0 %collective-permute-start.12 = (f32[51,8,128]{2,1,0:T(8,128)S(1)}, f32[51,8,128]{2,1,0:T(8,128)S(1)}, u32[]{:S(2)}, u32[]{:S(2)}) collective-permute-start(f32[51,8,128]{2,1,0:T(8,128)S(1)} %get-tuple-element.12), channel_id=1, source_target_pairs={{0,4},{1,5},{2,6},{3,7},{4,0},{5,1},{6,2},{7,3},{8,12},{9,13},{10,... | collective-permute-start | bytes 626696 | tf_op jit(solution)/shard_map/ppermute | solution.py:201
  127.2 0.6 pad_maximum_fusion.1
  127.8 2.9 %collective-permute-done.11 = f32[51,8,128]{2,1,0:T(8,128)S(1)} collective-permute-done((f32[51,8,128]{2,1,0:T(8,128)S(1)}, f32[51,8,128]{2,1,0:T(8,128)S(1)}, u32[]{:S(2)}, u32[]{:S(2)}) %collective-permute-start.11) | collective-permute-done | bytes 208928 | tf_op jit(solution)/shard_map/ppermute | solution.py:201
  130.7 4.5 %collective-permute-done.12 = f32[51,8,128]{2,1,0:T(8,128)S(1)} collective-permute-done((f32[51,8,128]{2,1,0:T(8,128)S(1)}, f32[51,8,128]{2,1,0:T(8,128)S(1)}, u32[]{:S(2)}, u32[]{:S(2)}) %collective-permute-start.12) | collective-permute-done | bytes 208928 | tf_op jit(solution)/shard_map/ppermute | solution.py:201
  135.2 0.8 fusion.15
  (42 shorter events, 0.9 us)
Async XLA Ops:
  7.3 91.2 %all-to-all-start = ((bf16[32,8,16,128]{3,2,1,0:T(8,128)(2,1)}), bf16[32,8,16,128]{3,2,1,0:T(8,128)(2,1)}, u32[]{:S(2)}, u32[]{:S(2)}) async-start(bf16[32,8,16,128]{3,2,1,0:T(8,128)(2,1)} %bitcast.19), calls=%async_computation | async-start | bytes 2097152 | tf_op jit(solution)/shard_map/all_to_all | solution.py:269
  18.7 5.7 %copy-start = (bf16[256,50,128]{2,0,1:T(8,128)(2,1)S(1)}, bf16[256,50,128]{2,0,1:T(8,128)(2,1)}, u32[]{:S(2)}) copy-start(bf16[256,50,128]{2,0,1:T(8,128)(2,1)} %param.8) | copy-start | bytes 9830404
  24.0 51.6 %collective-permute-start.2 = (bf16[4608,128]{1,0:T(8,128)(2,1)}, bf16[4608,128]{1,0:T(8,128)(2,1)}, u32[]{:S(2)}, u32[]{:S(2)}) collective-permute-start(bf16[4608,128]{1,0:T(8,128)(2,1)} %slice.44), channel_id=1, source_target_pairs={{0,2},{1,3},{2,0},{3,1},{4,6},{5,7},{6,4},{7,5},{8,10},{9,11},{10,... | collective-permute-start | bytes 3538952 | tf_op jit(solution)/shard_map/ppermute | solution.py:201
  25.4 1.3 copy-start.5
  27.9 53.4 %collective-permute-start.5 = (bf16[20,256,128]{2,1,0:T(8,128)(2,1)}, bf16[20,256,128]{2,1,0:T(8,128)(2,1)}, u32[]{:S(2)}, u32[]{:S(2)}) collective-permute-start(bf16[20,256,128]{2,1,0:T(8,128)(2,1)} %pad_maximum_fusion), channel_id=1, source_target_pairs={{0,6},{1,7},{2,4},{3,5},{4,2},{5,3},{6,0},{7,1},{8,14},{9,15},{10,... | collective-permute-start | bytes 3932168 | tf_op jit(solution)/shard_map/ppermute | solution.py:201
  30.3 50.9 %collective-permute-start.1 = (bf16[4608,128]{1,0:T(8,128)(2,1)}, bf16[4608,128]{1,0:T(8,128)(2,1)}, u32[]{:S(2)}, u32[]{:S(2)}) collective-permute-start(bf16[4608,128]{1,0:T(8,128)(2,1)} %bitcast.7), channel_id=1, source_target_pairs={{0,2},{1,3},{2,0},{3,1},{4,6},{5,7},{6,4},{7,5},{8,10},{9,11},{10,... | collective-permute-start | bytes 3538952 | tf_op jit(solution)/shard_map/ppermute | solution.py:201
  31.6 71.6 %collective-permute-start = (bf16[9216,128]{1,0:T(8,128)(2,1)}, bf16[9216,128]{1,0:T(8,128)(2,1)}, u32[]{:S(2)}, u32[]{:S(2)}) collective-permute-start(bf16[9216,128]{1,0:T(8,128)(2,1)} %bitcast.5.refs_0_), channel_id=1, source_target_pairs={{0,1},{1,0},{2,3},{3,2},{4,5},{5,4},{6,7},{7,6},{8,9},{9,8},{10,11... | collective-permute-start | bytes 7077896 | tf_op jit(solution)/shard_map/ppermute | solution.py:201
  31.6 41.2 %collective-permute-start.6 = (bf16[10,256,128]{2,1,0:T(8,128)(2,1)}, bf16[10,256,128]{2,1,0:T(8,128)(2,1)}, u32[]{:S(2)}, u32[]{:S(2)}) collective-permute-start(bf16[10,256,128]{2,1,0:T(8,128)(2,1)} %get-tuple-element.6), channel_id=1, source_target_pairs={{0,6},{1,7},{2,4},{3,5},{4,2},{5,3},{6,0},{7,1},{8,14},{9,15},{10,... | collective-permute-start | bytes 1966088 | tf_op jit(solution)/shard_map/ppermute | solution.py:201
  72.9 15.7 %collective-permute-start.8 = (bf16[10,256,128]{2,1,0:T(8,128)(2,1)}, bf16[10,256,128]{2,1,0:T(8,128)(2,1)}, u32[]{:S(2)}, u32[]{:S(2)}) collective-permute-start(bf16[10,256,128]{2,1,0:T(8,128)(2,1)} %collective-permute-done.6.refs_1_), channel_id=1, source_target_pairs={{0,192},{8,200},{16,208},{24,216},{32,224},{40,232},{48,240},{56,2... | collective-permute-start | bytes 1966088 | tf_op jit(solution)/shard_map/ppermute | solution.py:215
  75.6 16.3 %collective-permute-start.7 = (bf16[10,256,128]{2,1,0:T(8,128)(2,1)}, bf16[10,256,128]{2,1,0:T(8,128)(2,1)}, u32[]{:S(2)}, u32[]{:S(2)}) collective-permute-start(bf16[10,256,128]{2,1,0:T(8,128)(2,1)} %collective-permute-done.6.refs_1_), channel_id=1, source_target_pairs={{0,64},{8,72},{16,80},{24,88},{32,96},{40,104},{48,112},{56,120},{... | collective-permute-start | bytes 1966088 | tf_op jit(solution)/shard_map/ppermute | solution.py:215
  78.7 2.0 %copy-start.1 = (bf16[256,64,128]{2,1,0:T(8,128)(2,1)}, bf16[256,64,128]{2,1,0:T(8,128)(2,1)S(1)}, u32[]{:S(2)}) copy-start(bf16[256,64,128]{2,1,0:T(8,128)(2,1)S(1)} %by_harmonic.2.refs_6_) | copy-start | bytes 12582916
  81.2 22.0 %collective-permute-start.4 = (bf16[4608,128]{1,0:T(8,128)(2,1)}, bf16[4608,128]{1,0:T(8,128)(2,1)S(1)}, u32[]{:S(2)}, u32[]{:S(2)}) collective-permute-start(bf16[4608,128]{1,0:T(8,128)(2,1)} %collective-permute-done.2.refs_3_), channel_id=1, source_target_pairs={{0,1},{1,0},{2,3},{3,2},{4,5},{5,4},{6,7},{7,6},{8,9},{9,8},{10,11... | collective-permute-start | bytes 3538952 | tf_op jit(solution)/shard_map/ppermute | solution.py:201
  81.3 21.9 %collective-permute-start.3 = (bf16[4608,128]{1,0:T(8,128)(2,1)}, bf16[4608,128]{1,0:T(8,128)(2,1)S(1)}, u32[]{:S(2)}, u32[]{:S(2)}) collective-permute-start(bf16[4608,128]{1,0:T(8,128)(2,1)} %collective-permute-done.1.refs_2_), channel_id=1, source_target_pairs={{0,1},{1,0},{2,3},{3,2},{4,5},{5,4},{6,7},{7,6},{8,9},{9,8},{10,11... | collective-permute-start | bytes 3538952 | tf_op jit(solution)/shard_map/ppermute | solution.py:201
  96.3 2.1 %copy-start.3 = (bf16[256,64,128]{2,1,0:T(8,128)(2,1)}, bf16[256,64,128]{2,1,0:T(8,128)(2,1)S(1)}, u32[]{:S(2)}) copy-start(bf16[256,64,128]{2,1,0:T(8,128)(2,1)S(1)} %by_harmonic.3.refs_7_) | copy-start | bytes 12582916
  99.9 3.4 %copy-start.4 = (bf16[256,64,128]{2,1,0:T(8,128)(2,1)S(1)}, bf16[256,64,128]{2,1,0:T(8,128)(2,1)}, u32[]{:S(2)}) copy-start(bf16[256,64,128]{2,1,0:T(8,128)(2,1)} %copy-done.3) | copy-start | bytes 12582916
  102.7 2.2 %copy-start.2 = (bf16[256,64,128]{2,1,0:T(8,128)(2,1)S(1)}, bf16[256,64,128]{2,1,0:T(8,128)(2,1)}, u32[]{:S(2)}) copy-start(bf16[256,64,128]{2,1,0:T(8,128)(2,1)} %copy-done.1) | copy-start | bytes 12582916
  102.9 19.3 %collective-permute-start.10 = (f32[4,51,8,128]{3,2,1,0:T(8,128)S(1)}, f32[4,51,8,128]{3,2,1,0:T(8,128)S(1)}, u32[]{:S(2)}, u32[]{:S(2)}) collective-permute-start(f32[4,51,8,128]{3,2,1,0:T(8,128)S(1)} %dynamic-slice_bitcast_fusion), channel_id=1, source_target_pairs={{0,1},{1,0},{2,3},{3,2},{4,5},{5,4},{6,7},{7,6},{8,9},{9,8},{10,11... | collective-permute-start | bytes 2506760 | tf_op jit(solution)/shard_map/ppermute | solution.py:201
  120.7 6.5 %collective-permute-start.9 = (f32[16,128]{1,0:T(8,128)S(1)}, f32[16,128]{1,0:T(8,128)S(1)}, u32[]{:S(2)}, u32[]{:S(2)}) collective-permute-start(f32[16,128]{1,0:T(8,128)S(1)} %score.1), channel_id=1, source_target_pairs={{0,6},{1,7},{2,4},{3,5},{4,2},{5,3},{6,0},{7,1},{8,14},{9,15},{10,... | collective-permute-start | bytes 24584 | tf_op jit(solution)/shard_map/ppermute | solution.py:201
  122.4 8.3 %collective-permute-start.11 = (f32[51,8,128]{2,1,0:T(8,128)S(1)}, f32[51,8,128]{2,1,0:T(8,128)S(1)}, u32[]{:S(2)}, u32[]{:S(2)}) collective-permute-start(f32[51,8,128]{2,1,0:T(8,128)S(1)} %get-tuple-element.10), channel_id=1, source_target_pairs={{0,2},{1,3},{2,4},{3,5},{4,6},{5,7},{6,0},{7,1},{8,10},{9,11},{10,... | collective-permute-start | bytes 626696 | tf_op jit(solution)/shard_map/ppermute | solution.py:201
  123.1 7.6 %collective-permute-start.13 = (f32[51,8,128]{2,1,0:T(8,128)S(1)}, f32[51,8,128]{2,1,0:T(8,128)S(1)}, u32[]{:S(2)}, u32[]{:S(2)}) collective-permute-start(f32[51,8,128]{2,1,0:T(8,128)S(1)} %get-tuple-element.11), channel_id=1, source_target_pairs={{0,6},{1,7},{2,0},{3,1},{4,2},{5,3},{6,4},{7,5},{8,14},{9,15},{10,... | collective-permute-start | bytes 626696 | tf_op jit(solution)/shard_map/ppermute | solution.py:201
  125.1 10.0 %collective-permute-start.12 = (f32[51,8,128]{2,1,0:T(8,128)S(1)}, f32[51,8,128]{2,1,0:T(8,128)S(1)}, u32[]{:S(2)}, u32[]{:S(2)}) collective-permute-start(f32[51,8,128]{2,1,0:T(8,128)S(1)} %get-tuple-element.12), channel_id=1, source_target_pairs={{0,4},{1,5},{2,6},{3,7},{4,0},{5,1},{6,2},{7,3},{8,12},{9,13},{10,... | collective-permute-start | bytes 626696 | tf_op jit(solution)/shard_map/ppermute | solution.py:201

commit v5 on v4

--- a/solution.py
+++ b/solution.py
@@ -37,15 +37,20 @@
 def gather_kernel(sizes, starts_ref, *refs):
     pieces, out_ref, work = refs[: len(sizes)], refs[len(sizes)], refs[len(sizes) + 1]
     total = out_ref.shape[1]
-    used = sum(sizes)
+    used = sum(map(sum, sizes))
     work[pl.ds(used * CHUNK, (total - used) * CHUNK), :] = jnp.zeros(((total - used) * CHUNK, LANES), jnp.float32)
 
     def chunk(j, carry):
         base = pl.multiple_of(j * CHUNK, CHUNK)
-        for k, (size, ref) in enumerate(zip(sizes, pieces)):
-            block = ref[:, pl.ds(base, CHUNK), :].reshape(size * CHUNK, LANES)
-            first = pl.multiple_of(starts_ref[k] * CHUNK, CHUNK)
-            work[pl.ds(first, size * CHUNK), :] = block.astype(jnp.float32)
+        k = 0
+        for parts, ref in zip(sizes, pieces):
+            above = 0
+            for size in parts:
+                block = ref[above : above + size, pl.ds(base, CHUNK), :].reshape(size * CHUNK, LANES)
+                first = pl.multiple_of(starts_ref[k] * CHUNK, CHUNK)
+                work[pl.ds(first, size * CHUNK), :] = block.astype(jnp.float32)
+                above += size
+                k += 1
         for t in range(CHUNK):
             out_ref[base + t] = work[pl.ds(t, total, stride=CHUNK), :].astype(jnp.bfloat16)
         return carry
@@ -53,10 +58,9 @@
     lax.fori_loop(0, out_ref.shape[0] // CHUNK, chunk, 0)
 
 
-def by_harmonic(pieces, starts, total):
+def by_harmonic(pieces, sizes, starts, total):
     angles, cycle_parts = pieces[0].shape[1:]
-    sizes = tuple(piece.shape[0] for piece in pieces)
-    moved = 2 * angles * cycle_parts * (sum(sizes) + total)
+    moved = 2 * angles * cycle_parts * (sum(map(sum, sizes)) + total)
     return pl.pallas_call(
         functools.partial(gather_kernel, sizes),
         in_specs=[SCALARS] + [WHOLE] * len(pieces),
@@ -70,12 +74,10 @@
 
 
 def score_kernel(scale, rows, shifts, counts, places_ref, *refs):
-    groups, pieces = len(counts), sum(counts)
-    firsts = [sum(counts[:g]) for g in range(groups)]
-    lowers = [refs[first] for first in firsts]
-    uppers = [refs[first + count - 1] for first, count in zip(firsts, counts)]
+    groups = pieces = counts
     stacked = refs[pieces : pieces + 2]
     table_ref, out_ref, left_ref, fa, fb, folded = refs[pieces + 2 :]
+    images = refs[:groups]
     half = table_ref.shape[1] // 2
     all_rows = 2 * rows * groups
     pitch = all_rows + 1
@@ -83,17 +85,19 @@
     lane = lax.broadcasted_iota(jnp.int32, (1, LANES), 1)
     sign = jnp.where(lane < cycles, 1.0, -1.0)
     block = CHUNK * rows
+    steps = half // CHUNK
+
+    everyone = range(groups)
 
     def chunk(j, carry):
         back = 2 * half - CHUNK - j * CHUNK
         edge = jnp.where(j == 0, half, 2 * half - CHUNK * j)
-        for g, (lower, upper) in enumerate(zip(lowers, uppers)):
-            skip = upper.shape[0] // rows - 2 * half
-            fa[g] = lower[pl.ds(pl.multiple_of(j * block, block), block), :].astype(jnp.float32)
-            back_rows = pl.multiple_of((back + skip) * rows, block)
-            fb[g, pl.ds(0, block), :] = upper[pl.ds(back_rows, block), :].astype(jnp.float32)
-            edge_rows = pl.multiple_of((edge + skip) * rows, block)
-            fb[g, pl.ds(block, 2 * rows), :] = upper[pl.ds(edge_rows, 2 * rows), :].astype(jnp.float32)
+        for g in everyone:
+            fa[g] = images[g][pl.ds(pl.multiple_of(j * block, block), block), :].astype(jnp.float32)
+            back_rows = pl.multiple_of(back * rows, block)
+            fb[g, pl.ds(0, block), :] = images[g][pl.ds(back_rows, block), :].astype(jnp.float32)
+            edge_rows = pl.multiple_of(edge * rows, block)
+            fb[g, pl.ds(block, 2 * rows), :] = images[g][pl.ds(edge_rows, 2 * rows), :].astype(jnp.float32)
         paired = jnp.where(j == 0, 0.0, 1.0)
         for t in range(CHUNK):
             slot = t % left_ref.shape[0]
@@ -128,7 +132,7 @@
             )
         return carry
 
-    lax.fori_loop(0, half // CHUNK, chunk, 0)
+    lax.fori_loop(0, steps, chunk, 0)
     table = table_ref[...]
     each = rows // shifts
     width = 2 * LANES
@@ -163,11 +167,10 @@
     half = angles // 2
     each = rows // shifts
     groups = len(images)
-    counts = tuple(len(image) for image in images)
     flops = groups * (2 * half * 2 * rows * 2 * cycle_parts * LANES + 2 * rows * LANES * angles * (angles + 8))
     return pl.pallas_call(
-        functools.partial(score_kernel, scale, rows, shifts, counts),
-        in_specs=[SCALARS] + [WHOLE] * (sum(counts) + 3),
+        functools.partial(score_kernel, scale, rows, shifts, groups),
+        in_specs=[SCALARS] + [WHOLE] * (groups + 3),
         out_specs=WHOLE,
         out_shape=jax.ShapeDtypeStruct((groups * each, LANES), jnp.float32),
         scratch_shapes=[
@@ -179,7 +182,7 @@
         compiler_params=pltpu.CompilerParams(vmem_limit_bytes=36 * 1024 * 1024),
         cost_estimate=pl.CostEstimate(flops=6 * flops, bytes_accessed=20_000_000, transcendentals=0),
         name="score",
-    )(places, *[piece for image in images for piece in image], *stacked, table)
+    )(places, *images, *stacked, table)
 
 
 def on_device(particles, references, class_ids, counts, shift_ids, weights):
@@ -189,7 +192,6 @@
     angles, own, shifts, cycle_parts = particles.shape
     class_count = references.shape[1]
     list_length = class_ids.shape[1]
-    half = angles // 2
     rows = shifts * own
     doms = 32
     chips = 4
@@ -200,9 +202,6 @@
         pairs = [(2 * y + c, 2 * t + e) for y in range(chips) for c in range(2) for t, e in [target(y, c)]]
         return lax.ppermute(value, "cls", pairs)
 
-    def along(value, step):
-        return move(value, lambda y, c: ((y + step) % chips, c))
-
     def across(value):
         return move(value, lambda y, c: (y, 1 - c))
 
@@ -218,13 +217,9 @@
     flat = native.reshape(angles * rows, cycle_parts)
     class_major = jnp.transpose(references, (1, 0, 2))
 
-    lower, again = lax.optimization_barrier((flat[: half * rows], flat))
-    upper = again[half * rows :]
-    lower_partner = move(lower, lambda y, c: (y ^ 1, c))
-    upper_partner = move(upper, lambda y, c: (y ^ 1, c))
+    partner = move(flat, lambda y, c: (y ^ 1, c))
     mate = across(flat)
-    lower_both = across(lower_partner)
-    upper_both = across(upper_partner)
+    partner_mate = across(partner)
 
     place = lax.axis_index("dom") // (doms // ring)
     window = class_count // (ring + 1)
@@ -238,10 +233,11 @@
     from_left = around(piece, 1)
     from_right = around(piece, -1)
 
-    own_set = by_harmonic([class_major], [0], LANES // 2)
-    starts = [straight + window * ((place + step) % ring) for step in (0, 3, 1, 2)]
+    own_set = by_harmonic([class_major], [(class_count,)], [0], LANES // 2)
+    starts = [straight + window * ((place + step) % ring) for step in (2, 0, 3, 1)]
     facing_set = by_harmonic(
-        [far[:straight], piece, from_left, from_right, far[straight:]],
+        [far, piece, from_left, from_right],
+        [(straight, window)] + [(window,)] * 3,
         jnp.stack([jnp.zeros_like(place)] + starts),
         LANES // 2,
     )
@@ -276,21 +272,17 @@
     mixing = jnp.pad(mixing, ((0, 0), (0, 0), (0, padded - listings)))
     sums = jnp.einsum("ksl,smlc->kmc", mixing, arrived, preferred_element_type=jnp.float32)
     depth = angles // doms
-    sums = sums.reshape(chips, 2, class_count, depth, cycle_parts)
-    totals = jnp.pad(totals.reshape(chips, 2, 1, 1, class_count), ((0, 0), (0, 0), (0, 0), (0, depth - 1), (0, cycle_parts - class_count)))
-    sums = jnp.concatenate([sums, totals], axis=2)
-    mine = lax.dynamic_index_in_dim(sums, core, 1, keepdims=False)
-    other = lax.dynamic_index_in_dim(sums, 1 - core, 1, keepdims=False)
-    pair_sums = mine + across(other)
-    total = lax.dynamic_index_in_dim(pair_sums, row, 0, keepdims=False)
-    for step in range(1, chips):
-        block = lax.dynamic_index_in_dim(pair_sums, (row + step) % chips, 0, keepdims=False)
-        total = total + along(block, step)
+    sums = sums.reshape(2 * chips, class_count, depth, cycle_parts)
+    totals = totals.reshape(2 * chips, 1, 1, class_count)
+    totals = jnp.pad(totals, ((0, 0), (0, 0), (0, depth - 1), (0, cycle_parts - class_count)))
+    sums = jnp.concatenate([sums, totals], axis=1)
+    shares = lax.all_to_all(sums, "cls", 0, 0, tiled=True)
+    total = jnp.sum(shares, axis=0)
     weight_sums = total[class_count, 0, :class_count]
     class_means = total[:class_count] / jnp.maximum(weight_sums, 1.0)[:, None, None]
     class_means = jnp.transpose(class_means, (1, 0, 2))
 
-    images = [(flat,), (mate,), (lower_partner, upper_partner), (lower_both, upper_both)]
+    images = [flat, mate, partner, partner_mate]
     places = jnp.stack([(row % 2 ^ chip) * 2 + (core ^ other) for chip in range(2) for other in range(2)])
     best = score(places.astype(jnp.int32), images)
     sent = facing(best)

time: 137 us -> 179 us (1.31); the launches traced: 136 us -> 176 us
  waiting for transfers between devices: 56.4 us -> 104 us
  local copies, waits for them, and re-layouts: 18.1 us -> 11.8 us
  starting transfers between devices: 25.9 us -> 22.9 us
  other arithmetic: 5.09 us -> 7.33 us
    ppermute x12 -> x6, waiting for transfers between devices: 47.8 us -> 76.3 us  [move(): return lax.ppermute(value, 'cls', pairs)]
    all_to_all x1, waiting for transfers between devices: 0.01 us -> 28.1 us  [on_device(): arrived = lax.all_to_all(payload, 'dom', 0, 0, tiled=True)]
    ppermute x12 -> x6, starting transfers between devices: 11.8 us -> 3.04 us  [move(): return lax.ppermute(value, 'cls', pairs)]
    ppermute x2, waiting for transfers between devices: 8.66 us -> 0.01 us  [around(): return lax.ppermute(value, 'dom', pairs)]
    slice x3 -> x0, local copies, waits for them, and re-layouts: 6.64 us -> none  [the longest x1 2.85 us: on_device(): lower, again = lax.optimization_barrier((flat[:half * rows], flat))]
    all_to_all x0 -> x1, starting transfers between devices: none -> 5.29 us  [on_device(): shares = lax.all_to_all(sums, 'cls', 0, 0, tiled=True)]
    unnamed x13 -> x11, local copies, waits for them, and re-layouts: 6.15 us -> 8.4 us
  transfers between devices with their start and end apart: 15 -> 10, of which waited for: 5 -> 5; matrix products, arithmetic and copies ran while one was open for 12% -> 5% of each run, Pallas kernels for 17% -> 4%
where the time goes in v5:
time: 179 us; the launch traced here: 176 us
  waiting for transfers between devices  104 us (58%)
  Pallas kernels  24 us (13%)
  starting transfers between devices  22.9 us (13%)
  local copies, waits for them, and re-layouts  11.8 us (7%)
  other arithmetic  7.33 us (4%)
  matrix products  4.96 us (3%)
    ppermute x6, waiting for transfers between devices, move(): return lax.ppermute(value, 'cls', pairs)  76.3 us
    all_to_all x1, waiting for transfers between devices, on_device(): arrived = lax.all_to_all(payload, 'dom', 0, 0, tiled=True)  28.1 us
    pallas_call x1, Pallas kernels, best_of_groups(): pl.pallas_call(functools.partial(score_kernel, scale, rows, shifts, group...  16.5 us
    all_to_all x1, starting transfers between devices, on_device(): arrived = lax.all_to_all(payload, 'dom', 0, 0, tiled=True)  11.3 us
    unnamed x11, local copies, waits for them, and re-layouts  8.4 us
    pallas_call x2, Pallas kernels, by_harmonic(): pl.pallas_call(functools.partial(gather_kernel, sizes), in_specs=[SCALARS...  7.51 us
    all_to_all x1, starting transfers between devices, on_device(): shares = lax.all_to_all(sums, 'cls', 0, 0, tiled=True)  5.29 us
    dot_general x1, matrix products, on_device(): jnp.einsum('lsi,msic->mlc', pick, native, preferred_element_type=jnp.floa...  4.04 us
  transfers between devices with their start and end apart: 10, of which 5 were waited for; matrix products, arithmetic and copies ran while one was open for 5% of the time, Pallas kernels for 4%

profile of v5, /device:TPU:8, one launch (start us, length us, event | category | flops | bytes accessed | tf_op | source)
XLA Modules:
  0.0 176.2 jit_solution(126748516054518812)
XLA Ops:
  0.6 0.8 reshape.283
  1.4 0.8 fusion.29
  2.2 0.1 reshape.284
  2.3 0.8 eq.100
  3.0 0.1 iota_compare_fusion.7
  3.1 0.1 broadcast_and_fusion
  3.2 4.0 %fusion.4 = bf16[16,256,128]{2,0,1:T(8,128)(2,1)} fusion(bf16[256,9,4,128]{3,2,1,0:T(4,128)(2,1)} %bitcast.4, bf16[16,128]{1,0:T(8,128)(2,1)S(1)} %select_maximum_fusion.1, pred[12,9,4]{1,0,2:T(8,128)(4,1)S(1)} %broadcast_and_fusion), kind=kOutput, calls=%fused_computation.7 | convolution fusion | flops 38797312 | bytes 3412400 | tf_op jit(solution)/shard_map/lsi,msic->mlc/dot_general | solution.py:256
  7.2 11.3 %all-to-all-start = ((bf16[32,8,16,128]{3,2,1,0:T(8,128)(2,1)}), bf16[32,8,16,128]{3,2,1,0:T(8,128)(2,1)S(1)}, u32[]{:S(2)}, u32[]{:S(2)}) async-start(bf16[32,8,16,128]{3,2,1,0:T(8,128)(2,1)} %bitcast.18), calls=%async_computation | async-start | bytes 2097152 | tf_op jit(solution)/shard_map/all_to_all | solution.py:265
  18.6 0.5 collective-permute-start.1
  19.1 0.0 collective-permute-start
  19.1 28.1 %all-to-all-done = bf16[32,8,16,128]{3,2,1,0:T(8,128)(2,1)S(1)} async-done(((bf16[32,8,16,128]{3,2,1,0:T(8,128)(2,1)}), bf16[32,8,16,128]{3,2,1,0:T(8,128)(2,1)S(1)}, u32[]{:S(2)}, u32[]{:S(2)}) %all-to-all-start) | async-done | bytes 1048608 | tf_op jit(solution)/shard_map/all_to_all | solution.py:265
  47.2 0.1 copy.29
  47.3 0.2 fusion.8
  47.5 24.2 %collective-permute-done.1.refs_2_ = bf16[9216,128]{1,0:T(8,128)(2,1)} collective-permute-done((bf16[9216,128]{1,0:T(8,128)(2,1)}, bf16[9216,128]{1,0:T(8,128)(2,1)}, u32[]{:S(2)}, u32[]{:S(2)}) %collective-permute-start.1) | collective-permute-done | bytes 2359328 | tf_op jit(solution)/shard_map/ppermute | solution.py:203
  71.7 0.0 collective-permute-start.2
  71.7 0.9 convolution_bitcast_fusion
  72.6 0.5 copy.26
  73.2 0.2 convert_reduce_fusion
  73.3 0.1 reshape.287
  73.4 1.3 select_maximum_fusion
  74.7 5.3 %all-to-all-start.1 = ((f32[8,51,8,128]{3,2,1,0:T(8,128)}), f32[8,51,8,128]{3,2,1,0:T(8,128)}, u32[]{:S(2)}, u32[]{:S(2)}) async-start(f32[8,51,8,128]{3,2,1,0:T(8,128)} %select_maximum_fusion), calls=%async_computation.1 | async-start | bytes 3342336 | tf_op jit(solution)/shard_map/all_to_all | solution.py:279
  80.0 1.0 dynamic-slice_bitcast_fusion
  81.0 1.5 collective-permute-start.4
  82.5 1.2 pad_maximum_fusion
  83.7 0.6 collective-permute-start.3
  84.3 3.0 %by_harmonic.2.refs_4_ = bf16[256,64,128]{2,1,0:T(8,128)(2,1)S(1)} custom-call(s32[1]{0:T(128)} %constant.168.clone.starts_ref, bf16[50,256,128]{2,1,0:T(8,128)(2,1)S(1)} %bitcast.44), custom_call_target="tpu_custom_call" | custom-call | bytes 14942208 | tf_op jit(solution)/shard_map/by_harmonic/pallas_call | solution.py:64
  87.3 2.0 %copy-done.1 = bf16[256,64,128]{2,1,0:T(8,128)(2,1)} copy-done((bf16[256,64,128]{2,1,0:T(8,128)(2,1)}, bf16[256,64,128]{2,1,0:T(8,128)(2,1)S(1)}, u32[]{:S(2)}) %copy-start.1) | copy-done | bytes 4194328
  89.2 0.1 stack.39.starts_ref
  89.4 25.9 %collective-permute-done.4.refs_1_ = bf16[10,256,128]{2,1,0:T(8,128)(2,1)} collective-permute-done((bf16[10,256,128]{2,1,0:T(8,128)(2,1)}, bf16[10,256,128]{2,1,0:T(8,128)(2,1)}, u32[]{:S(2)}, u32[]{:S(2)}) %collective-permute-start.4) | collective-permute-done | bytes 655392 | tf_op jit(solution)/shard_map/ppermute | solution.py:203
  115.3 1.5 collective-permute-start.5
  116.8 1.7 collective-permute-start.6
  118.5 0.1 pad_add_fusion.places_ref
  118.6 0.1 select_convert_fusion.1
  118.7 0.3 select_convert_fusion
  119.0 23.8 %collective-permute-done.3.refs_0_ = bf16[20,256,128]{2,1,0:T(8,128)(2,1)} collective-permute-done((bf16[20,256,128]{2,1,0:T(8,128)(2,1)}, bf16[20,256,128]{2,1,0:T(8,128)(2,1)}, u32[]{:S(2)}, u32[]{:S(2)}) %collective-permute-start.3) | collective-permute-done | bytes 1310752 | tf_op jit(solution)/shard_map/ppermute | solution.py:203
  142.8 0.0 collective-permute-done.5.refs_2_
  142.8 0.0 collective-permute-done.6.refs_3_
  142.8 4.5 %by_harmonic.3.refs_5_ = bf16[256,64,128]{2,1,0:T(8,128)(2,1)S(1)} custom-call(s32[5]{0:T(128)S(1)} %stack.39.starts_ref, bf16[20,256,128]{2,1,0:T(8,128)(2,1)} %collective-permute-done.3.refs_0_, bf16[10,256,128]{2,1,0:T(8,128)(2,1)} %collective-permute-done.4.refs_1_, bf16[10,256,128]{2,1,0:T(8,128)(2,1)S(1)} %collective-permute-done.5.refs_2_, ...), custom_call_target="tpu_custom_call" | custom-call | bytes 14942208 | tf_op jit(solution)/shard_map/by_harmonic/pallas_call | solution.py:64
  147.3 2.0 %copy-done.3 = bf16[256,64,128]{2,1,0:T(8,128)(2,1)} copy-done((bf16[256,64,128]{2,1,0:T(8,128)(2,1)}, bf16[256,64,128]{2,1,0:T(8,128)(2,1)S(1)}, u32[]{:S(2)}) %copy-start.3) | copy-done | bytes 4194328
  149.3 1.5 reduce_sum.19
  150.9 2.2 %copy-done.2 = bf16[256,64,128]{2,1,0:T(8,128)(2,1)S(1)} copy-done((bf16[256,64,128]{2,1,0:T(8,128)(2,1)S(1)}, bf16[256,64,128]{2,1,0:T(8,128)(2,1)}, u32[]{:S(2)}) %copy-start.2) | copy-done | bytes 4194328
  153.1 2.2 %copy-done.4 = bf16[256,64,128]{2,1,0:T(8,128)(2,1)S(1)} copy-done((bf16[256,64,128]{2,1,0:T(8,128)(2,1)S(1)}, bf16[256,64,128]{2,1,0:T(8,128)(2,1)}, u32[]{:S(2)}) %copy-start.4) | copy-done | bytes 4194328
  155.3 16.5 %score.1 = f32[16,128]{1,0:T(8,128)S(1)} custom-call(s32[4]{0:T(128)S(1)} %pad_add_fusion.places_ref, bf16[9216,128]{1,0:T(8,128)(2,1)} %bitcast.5.refs_0_, bf16[9216,128]{1,0:T(8,128)(2,1)} %collective-permute-done.refs_1_, bf16[9216,128]{1,0:T(8,128)(2,1)} %collective-permute-done.1.refs_2_, bf16[9216,128]{1,0:T(8,128)(2,1)} %collective-permute-done.2.refs_3_, ...), custom_call_target="tpu_custom_call" | custom-call | flops 29444014080 | bytes 20000000 | tf_op jit(solution)/shard_map/score/pallas_call | solution.py:171
  171.8 0.5 collective-permute-start.7
  172.3 0.8 fusion.13
  173.1 2.5 %collective-permute-done.7 = f32[16,128]{1,0:T(8,128)S(1)} collective-permute-done((f32[16,128]{1,0:T(8,128)S(1)}, f32[16,128]{1,0:T(8,128)S(1)}, u32[]{:S(2)}, u32[]{:S(2)}) %collective-permute-start.7) | collective-permute-done | bytes 8224 | tf_op jit(solution)/shard_map/ppermute | solution.py:203
  175.5 0.1 slice_select_fusion.1
  175.6 0.6 pad_maximum_fusion.1
  (23 shorter events, 0.2 us)
Async XLA Ops:
  7.2 39.9 %all-to-all-start = ((bf16[32,8,16,128]{3,2,1,0:T(8,128)(2,1)}), bf16[32,8,16,128]{3,2,1,0:T(8,128)(2,1)S(1)}, u32[]{:S(2)}, u32[]{:S(2)}) async-start(bf16[32,8,16,128]{3,2,1,0:T(8,128)(2,1)} %bitcast.18), calls=%async_computation | async-start | bytes 2097152 | tf_op jit(solution)/shard_map/all_to_all | solution.py:265
  18.6 53.1 %collective-permute-start.1 = (bf16[9216,128]{1,0:T(8,128)(2,1)}, bf16[9216,128]{1,0:T(8,128)(2,1)}, u32[]{:S(2)}, u32[]{:S(2)}) collective-permute-start(bf16[9216,128]{1,0:T(8,128)(2,1)} %bitcast.5.refs_0_), channel_id=1, source_target_pairs={{0,2},{1,3},{2,0},{3,1},{4,6},{5,7},{6,4},{7,5},{8,10},{9,11},{10,... | collective-permute-start | bytes 7077896 | tf_op jit(solution)/shard_map/ppermute | solution.py:203
  19.1 131.8 %collective-permute-start = (bf16[9216,128]{1,0:T(8,128)(2,1)}, bf16[9216,128]{1,0:T(8,128)(2,1)}, u32[]{:S(2)}, u32[]{:S(2)}) collective-permute-start(bf16[9216,128]{1,0:T(8,128)(2,1)} %bitcast.5.refs_0_), channel_id=1, source_target_pairs={{0,1},{1,0},{2,3},{3,2},{4,5},{5,4},{6,7},{7,6},{8,9},{9,8},{10,11... | collective-permute-start | bytes 7077896 | tf_op jit(solution)/shard_map/ppermute | solution.py:203
  71.7 79.2 %collective-permute-start.2 = (bf16[9216,128]{1,0:T(8,128)(2,1)}, bf16[9216,128]{1,0:T(8,128)(2,1)}, u32[]{:S(2)}, u32[]{:S(2)}) collective-permute-start(bf16[9216,128]{1,0:T(8,128)(2,1)} %collective-permute-done.1.refs_2_), channel_id=1, source_target_pairs={{0,1},{1,0},{2,3},{3,2},{4,5},{5,4},{6,7},{7,6},{8,9},{9,8},{10,11... | collective-permute-start | bytes 7077896 | tf_op jit(solution)/shard_map/ppermute | solution.py:203
  74.7 5.3 %copy-start = (bf16[256,50,128]{2,0,1:T(8,128)(2,1)S(1)}, bf16[256,50,128]{2,0,1:T(8,128)(2,1)}, u32[]{:S(2)}) copy-start(bf16[256,50,128]{2,0,1:T(8,128)(2,1)} %param.8) | copy-start | bytes 9830404
  74.7 74.6 %all-to-all-start.1 = ((f32[8,51,8,128]{3,2,1,0:T(8,128)}), f32[8,51,8,128]{3,2,1,0:T(8,128)}, u32[]{:S(2)}, u32[]{:S(2)}) async-start(f32[8,51,8,128]{3,2,1,0:T(8,128)} %select_maximum_fusion), calls=%async_computation.1 | async-start | bytes 3342336 | tf_op jit(solution)/shard_map/all_to_all | solution.py:279
  81.0 34.3 %collective-permute-start.4 = (bf16[10,256,128]{2,1,0:T(8,128)(2,1)}, bf16[10,256,128]{2,1,0:T(8,128)(2,1)}, u32[]{:S(2)}, u32[]{:S(2)}) collective-permute-start(bf16[10,256,128]{2,1,0:T(8,128)(2,1)} %get-tuple-element.2), channel_id=1, source_target_pairs={{0,6},{1,7},{2,4},{3,5},{4,2},{5,3},{6,0},{7,1},{8,14},{9,15},{10,... | collective-permute-start | bytes 1966088 | tf_op jit(solution)/shard_map/ppermute | solution.py:203
  83.7 59.1 %collective-permute-start.3 = (bf16[20,256,128]{2,1,0:T(8,128)(2,1)}, bf16[20,256,128]{2,1,0:T(8,128)(2,1)}, u32[]{:S(2)}, u32[]{:S(2)}) collective-permute-start(bf16[20,256,128]{2,1,0:T(8,128)(2,1)} %pad_maximum_fusion), channel_id=1, source_target_pairs={{0,6},{1,7},{2,4},{3,5},{4,2},{5,3},{6,0},{7,1},{8,14},{9,15},{10,... | collective-permute-start | bytes 3932168 | tf_op jit(solution)/shard_map/ppermute | solution.py:203
  87.3 2.0 %copy-start.1 = (bf16[256,64,128]{2,1,0:T(8,128)(2,1)}, bf16[256,64,128]{2,1,0:T(8,128)(2,1)S(1)}, u32[]{:S(2)}) copy-start(bf16[256,64,128]{2,1,0:T(8,128)(2,1)S(1)} %by_harmonic.2.refs_4_) | copy-start | bytes 12582916
  115.3 27.5 %collective-permute-start.5 = (bf16[10,256,128]{2,1,0:T(8,128)(2,1)}, bf16[10,256,128]{2,1,0:T(8,128)(2,1)S(1)}, u32[]{:S(2)}, u32[]{:S(2)}) collective-permute-start(bf16[10,256,128]{2,1,0:T(8,128)(2,1)} %collective-permute-done.4.refs_1_), channel_id=1, source_target_pairs={{0,64},{8,72},{16,80},{24,88},{32,96},{40,104},{48,112},{56,120},{... | collective-permute-start | bytes 1966088 | tf_op jit(solution)/shard_map/ppermute | solution.py:214
  116.8 26.0 %collective-permute-start.6 = (bf16[10,256,128]{2,1,0:T(8,128)(2,1)}, bf16[10,256,128]{2,1,0:T(8,128)(2,1)S(1)}, u32[]{:S(2)}, u32[]{:S(2)}) collective-permute-start(bf16[10,256,128]{2,1,0:T(8,128)(2,1)} %collective-permute-done.4.refs_1_), channel_id=1, source_target_pairs={{0,192},{8,200},{16,208},{24,216},{32,224},{40,232},{48,240},{56,2... | collective-permute-start | bytes 1966088 | tf_op jit(solution)/shard_map/ppermute | solution.py:214
  147.3 2.0 %copy-start.3 = (bf16[256,64,128]{2,1,0:T(8,128)(2,1)}, bf16[256,64,128]{2,1,0:T(8,128)(2,1)S(1)}, u32[]{:S(2)}) copy-start(bf16[256,64,128]{2,1,0:T(8,128)(2,1)S(1)} %by_harmonic.3.refs_5_) | copy-start | bytes 12582916
  150.9 2.2 %copy-start.2 = (bf16[256,64,128]{2,1,0:T(8,128)(2,1)S(1)}, bf16[256,64,128]{2,1,0:T(8,128)(2,1)}, u32[]{:S(2)}) copy-start(bf16[256,64,128]{2,1,0:T(8,128)(2,1)} %copy-done.1) | copy-start | bytes 12582916
  153.1 2.2 %copy-start.4 = (bf16[256,64,128]{2,1,0:T(8,128)(2,1)S(1)}, bf16[256,64,128]{2,1,0:T(8,128)(2,1)}, u32[]{:S(2)}) copy-start(bf16[256,64,128]{2,1,0:T(8,128)(2,1)} %copy-done.3) | copy-start | bytes 12582916
  171.8 3.7 %collective-permute-start.7 = (f32[16,128]{1,0:T(8,128)S(1)}, f32[16,128]{1,0:T(8,128)S(1)}, u32[]{:S(2)}, u32[]{:S(2)}) collective-permute-start(f32[16,128]{1,0:T(8,128)S(1)} %score.1), channel_id=1, source_target_pairs={{0,6},{1,7},{2,4},{3,5},{4,2},{5,3},{6,0},{7,1},{8,14},{9,15},{10,... | collective-permute-start | bytes 24584 | tf_op jit(solution)/shard_map/ppermute | solution.py:203

commit v6 on v5

--- a/solution.py
+++ b/solution.py
@@ -179,10 +179,134 @@
             pltpu.VMEM((groups, (CHUNK + 2) * rows, cycle_parts), jnp.float32),
             pltpu.VMEM(((2 * rows * groups + 1) * half, LANES), jnp.float32),
         ],
-        compiler_params=pltpu.CompilerParams(vmem_limit_bytes=36 * 1024 * 1024),
+        compiler_params=pltpu.CompilerParams(vmem_limit_bytes=26 * 1024 * 1024),
         cost_estimate=pl.CostEstimate(flops=6 * flops, bytes_accessed=20_000_000, transcendentals=0),
         name="score",
     )(places, *images, *stacked, table)
+
+
+def listing_kernel(shift_ref, id_ref, count_ref, weight_ref, images_ref, out_ref, work):
+    own, length = id_ref.shape
+    owners, tiles, depth, cycle_parts = out_ref.shape
+    angles = owners * depth
+    rows = images_ref.shape[0] // angles
+    block = CHUNK * rows
+
+    def widen(j, carry):
+        part = pl.ds(pl.multiple_of(j * block, block), block)
+        work[part, :] = images_ref[part, :].astype(jnp.float32)
+        return carry
+
+    lax.fori_loop(0, angles // CHUNK, widen, 0)
+    lane = lax.broadcasted_iota(jnp.int32, (depth, cycle_parts), 1)
+    digit = lax.broadcasted_iota(jnp.int32, (depth, cycle_parts), 0)
+    notes = jnp.zeros((depth, cycle_parts), jnp.float32)
+    for i in range(own):
+        for j in range(length):
+            place = i * length + j
+            column = work[pl.ds(shift_ref[i, j] * own + i, angles, stride=rows), :]
+            out_ref[:, place] = column.reshape(owners, depth, cycle_parts).astype(jnp.bfloat16)
+            name = id_ref[i, j]
+            kept = jnp.where(j < count_ref[i], weight_ref[i, j], 0.0)
+            upper = (name >> 4).astype(jnp.float32)
+            lower = (name & 15).astype(jnp.float32)
+            value = jnp.where(digit == 0, upper, jnp.where(digit == 1, lower, jnp.where(digit == 2, kept, 0.0)))
+            notes = jnp.where(lane == place, value, notes)
+    out_ref[:, tiles - 1] = jnp.broadcast_to(notes.astype(jnp.bfloat16)[None], (owners, depth, cycle_parts))
+
+
+def listings_by_owner(shift_ids, class_ids, counts, weights, images, owners):
+    own, length = class_ids.shape
+    cycle_parts = images.shape[1]
+    rows = images.shape[0]
+    angles = rows // (9 * own)
+    shape = (owners, own * length + 1, angles // owners, cycle_parts)
+    return pl.pallas_call(
+        listing_kernel,
+        in_specs=[SCALARS] * 4 + [WHOLE],
+        out_specs=WHOLE,
+        out_shape=jax.ShapeDtypeStruct(shape, jnp.bfloat16),
+        scratch_shapes=[pltpu.VMEM((rows, cycle_parts), jnp.float32)],
+        compiler_params=pltpu.CompilerParams(vmem_limit_bytes=14 * 1024 * 1024),
+        cost_estimate=pl.CostEstimate(flops=0, bytes_accessed=8_000_000, transcendentals=0),
+        name="listings",
+    )(shift_ids, class_ids, counts, weights, images)
+
+
+def sums_kernel(class_count, sets, arrived_ref, out_ref, work):
+    sources, tiles, depth, cycle_parts = arrived_ref.shape
+    listings = tiles - 1
+    each = tiles * depth
+    places = work.shape[0] // depth
+    used = sources * each
+    padded = -(-class_count // 8) * 8
+
+    def widen(j, carry):
+        first = pl.multiple_of(j * each, each)
+        work[pl.ds(first, each), :] = arrived_ref[j].reshape(each, cycle_parts).astype(jnp.float32)
+        return carry
+
+    lax.fori_loop(0, sources, widen, 0)
+    work[pl.ds(used, work.shape[0] - used), :] = jnp.zeros((work.shape[0] - used, cycle_parts), jnp.float32)
+    lane = lax.broadcasted_iota(jnp.int32, (1, LANES), 1)
+    names = [jnp.zeros((1, LANES), jnp.float32) for _ in range(places // LANES)]
+    kept = [jnp.zeros((1, LANES), jnp.float32) for _ in range(places // LANES)]
+    for source in range(sources):
+        first = source * each + listings * depth
+        name = work[pl.ds(first, 1), :] * 16.0 + work[pl.ds(first + 1, 1), :]
+        weight = work[pl.ds(first + 2, 1), :]
+        column, offset = divmod(source * tiles, LANES)
+        if offset:
+            name, weight = pltpu.roll(name, offset, 1), pltpu.roll(weight, offset, 1)
+        here = lane >= offset
+        names[column] = names[column] + jnp.where(here, name, 0.0)
+        kept[column] = kept[column] + jnp.where(here, weight, 0.0)
+        if offset + listings > LANES:
+            names[column + 1] = names[column + 1] + jnp.where(here, 0.0, name)
+            kept[column + 1] = kept[column + 1] + jnp.where(here, 0.0, weight)
+    names = jnp.concatenate(names, axis=1)
+    kept = jnp.concatenate(kept, axis=1)
+
+    def mixing_of(block, rows):
+        row = lax.broadcasted_iota(jnp.int32, (rows, places), 0)
+        wanted = (row + block * class_count).astype(jnp.float32)
+        return jnp.where((wanted == names) & (row < class_count), kept, 0.0).astype(jnp.bfloat16)
+
+    mixing = jnp.concatenate([mixing_of(block, padded) for block in range(sets)], axis=0)
+    ones = jnp.ones((8, places), jnp.bfloat16)
+    for block in range(sets):
+        total = lax.dot_general(
+            ones, mixing_of(block, LANES), (((1,), (1,)), ((), ())), preferred_element_type=jnp.float32
+        )
+        out_ref[pl.ds((block * (class_count + 1) + class_count) * depth, depth), :] = total
+    for m in range(0, depth, 2):
+        pair = [work[pl.ds(m + k, places, stride=depth), :].astype(jnp.bfloat16) for k in range(2)]
+        result = jnp.dot(mixing, jnp.concatenate(pair, axis=1), preferred_element_type=jnp.float32)
+        for k in range(2):
+            for block in range(sets):
+                for first in range(0, class_count, 8):
+                    n = min(8, class_count - first)
+                    start = (block * (class_count + 1) + first) * depth + m + k
+                    row = block * padded + first
+                    out_ref[pl.ds(start, n, stride=depth), :] = result[
+                        row : row + n, k * cycle_parts : (k + 1) * cycle_parts
+                    ]
+
+
+def class_shares(arrived, class_count, sets):
+    sources, tiles, depth, cycle_parts = arrived.shape
+    places = -(-sources * tiles // LANES) * LANES
+    rows = sets * (class_count + 1) * depth
+    return pl.pallas_call(
+        functools.partial(sums_kernel, class_count, sets),
+        in_specs=[WHOLE],
+        out_specs=WHOLE,
+        out_shape=jax.ShapeDtypeStruct((rows, cycle_parts), jnp.float32),
+        scratch_shapes=[pltpu.VMEM((places * depth, cycle_parts), jnp.float32)],
+        compiler_params=pltpu.CompilerParams(vmem_limit_bytes=14 * 1024 * 1024),
+        cost_estimate=pl.CostEstimate(flops=4_000_000_000, bytes_accessed=8_000_000, transcendentals=0),
+        name="shares",
+    )(arrived)
 
 
 def on_device(particles, references, class_ids, counts, shift_ids, weights):
@@ -191,7 +315,6 @@
     row = cls_index // 2
     angles, own, shifts, cycle_parts = particles.shape
     class_count = references.shape[1]
-    list_length = class_ids.shape[1]
     rows = shifts * own
     doms = 32
     chips = 4
@@ -245,37 +368,12 @@
     table = folded_table(angles)
     score = functools.partial(best_of_groups, stacked=stacked, table=table, shifts=shifts, rows=rows, scale=scale)
 
-    listings = own * list_length
-    padded = 16
-    listed_shift = shift_ids.reshape(listings)
-    listed_image = jnp.arange(listings, dtype=jnp.int32) // list_length
-    pick = (listed_shift[:, None, None] == jnp.arange(shifts, dtype=jnp.int32)[None, :, None]) & (
-        listed_image[:, None, None] == jnp.arange(own, dtype=jnp.int32)[None, None, :]
-    )
-    pick = jnp.pad(pick.astype(jnp.bfloat16), ((0, padded - listings), (0, 0), (0, 0)))
-    listed = jnp.einsum("lsi,msic->mlc", pick, native, preferred_element_type=jnp.float32).astype(jnp.bfloat16)
-    valid = jnp.arange(list_length, dtype=jnp.int32)[None, :] < counts[:, None]
-    kept = jnp.where(valid, weights, jnp.zeros_like(weights)).reshape(1, listings)
-    flat_ids = class_ids.reshape(1, listings)
-    notes = jnp.concatenate(
-        [(flat_ids // 16).astype(jnp.bfloat16), (flat_ids % 16).astype(jnp.bfloat16), kept], axis=0
-    )
-    notes = jnp.pad(notes, ((listings, padded - listings - 3), (0, cycle_parts - listings)))
-    payload = (listed + notes[None]).reshape(doms, angles // doms, padded, cycle_parts)
-    arrived = lax.all_to_all(payload, "dom", 0, 0, tiled=True)
-    noted = arrived[:, 0, listings : listings + 3, :listings]
-    ids = noted[:, 0].astype(jnp.int32) * 16 + noted[:, 1].astype(jnp.int32)
-    classes = 2 * chips * class_count
-    hit = ids[None] == jnp.arange(classes, dtype=jnp.int32)[:, None, None]
-    mixing = jnp.where(hit, noted[:, 2][None], jnp.zeros((), jnp.bfloat16))
-    totals = jnp.sum(mixing.astype(jnp.float32), axis=(1, 2))
-    mixing = jnp.pad(mixing, ((0, 0), (0, 0), (0, padded - listings)))
-    sums = jnp.einsum("ksl,smlc->kmc", mixing, arrived, preferred_element_type=jnp.float32)
     depth = angles // doms
-    sums = sums.reshape(2 * chips, class_count, depth, cycle_parts)
-    totals = totals.reshape(2 * chips, 1, 1, class_count)
-    totals = jnp.pad(totals, ((0, 0), (0, 0), (0, depth - 1), (0, cycle_parts - class_count)))
-    sums = jnp.concatenate([sums, totals], axis=1)
+    payload = listings_by_owner(shift_ids, class_ids, counts, weights.astype(jnp.float32), flat, doms)
+    tiles = payload.shape[1]
+    arrived = lax.all_to_all(payload.reshape(doms, tiles * depth, cycle_parts), "dom", 0, 0, tiled=True)
+    sums = class_shares(arrived.reshape(doms, tiles, depth, cycle_parts), class_count, 2 * chips)
+    sums = sums.reshape(2 * chips, class_count + 1, depth, cycle_parts)
     shares = lax.all_to_all(sums, "cls", 0, 0, tiled=True)
     total = jnp.sum(shares, axis=0)
     weight_sums = total[class_count, 0, :class_count]
@@ -284,7 +382,11 @@
 
     images = [flat, mate, partner, partner_mate]
     places = jnp.stack([(row % 2 ^ chip) * 2 + (core ^ other) for chip in range(2) for other in range(2)])
-    best = score(places.astype(jnp.int32), images)
+    places = places.astype(jnp.int32)
+    home = score(places[:2] % 2, images[:2])
+    away = score(places[2:] % 2, images[2:])
+    even = row % 2 == 0
+    best = jnp.concatenate([jnp.where(even, home, away), jnp.where(even, away, home)], axis=0)
     sent = facing(best)
     mine, others = best[:, :class_count], sent[:, LANES // 2 : LANES // 2 + class_count]
     low = jnp.where(row < chips // 2, mine, others)

time: 179 us -> 131 us (0.73)
  waiting for transfers between devices: 104 us -> 50.2 us
  Pallas kernels: 24 us -> 33.4 us
  matrix products: 4.96 us -> 0 us
  local copies, waits for them, and re-layouts: 11.8 us -> 15 us
  other arithmetic: 7.33 us -> 5.41 us
    ppermute x6, waiting for transfers between devices: 76.3 us -> 45.9 us  [move(): return lax.ppermute(value, 'cls', pairs)]
    all_to_all x1, waiting for transfers between devices: 28.1 us -> 0.01 us  [on_device(): lax.all_to_all(payload.reshape(doms, tiles * depth, cycle_parts), 'dom',...]
    unnamed x11 -> x26, local copies, waits for them, and re-layouts: 8.4 us -> 13.9 us
    dot_general x2 -> x0, matrix products: 4.96 us -> none  [the longest x1 4.04 us: on_device(): jnp.einsum('lsi,msic->mlc', pick, native, preferred_element_type=jnp.floa...]
    pallas_call x0 -> x2, Pallas kernels: none -> 4.9 us  [the longest x1 3.7 us: class_shares(): pl.pallas_call(functools.partial(sums_kernel, class_count, sets), in_spec...]
    all_to_all x1, waiting for transfers between devices: 0.01 us -> 4.22 us  [on_device(): shares = lax.all_to_all(sums, 'cls', 0, 0, tiled=True)]
    pallas_call x1 -> x2, Pallas kernels: 16.5 us -> 20.4 us  [best_of_groups(): pl.pallas_call(functools.partial(score_kernel, scale, rows, shifts, group...]
  transfers between devices with their start and end apart: 10 -> 10, of which waited for: 5 -> 4; matrix products, arithmetic and copies ran while one was open for 5% -> 4% of each run, Pallas kernels for 4% -> 18%
where the time goes in v6:
time: 131 us; the launch traced here: 129 us
  waiting for transfers between devices  50.2 us (38%)
  Pallas kernels  33.4 us (25%)
  starting transfers between devices  24 us (18%)
  local copies, waits for them, and re-layouts  15 us (11%)
  other arithmetic  5.41 us (4%)
    ppermute x6, waiting for transfers between devices, move(): return lax.ppermute(value, 'cls', pairs)  45.9 us
    pallas_call x2, Pallas kernels, best_of_groups(): pl.pallas_call(functools.partial(score_kernel, scale, rows, shifts, group...  20.4 us
    unnamed x26, local copies, waits for them, and re-layouts  13.9 us
    all_to_all x1, starting transfers between devices, on_device(): lax.all_to_all(payload.reshape(doms, tiles * depth, cycle_parts), 'dom',...  9.72 us
    pallas_call x2, Pallas kernels, by_harmonic(): pl.pallas_call(functools.partial(gather_kernel, sizes), in_specs=[SCALARS...  8.05 us
    all_to_all x1, starting transfers between devices, on_device(): shares = lax.all_to_all(sums, 'cls', 0, 0, tiled=True)  6.32 us
    ppermute x6, starting transfers between devices, move(): return lax.ppermute(value, 'cls', pairs)  4.78 us
    all_to_all x1, waiting for transfers between devices, on_device(): shares = lax.all_to_all(sums, 'cls', 0, 0, tiled=True)  4.22 us
  transfers between devices with their start and end apart: 10, of which 4 were waited for; matrix products, arithmetic and copies ran while one was open for 4% of the time, Pallas kernels for 18%

profile of v6, /device:TPU:8, one launch (start us, length us, event | category | flops | bytes accessed | tf_op | source)
XLA Modules:
  0.0 128.9 jit_solution(4295371259302091545)
XLA Ops:
  0.6 2.2 %collective-permute-start.5 = (bf16[9216,128]{1,0:T(8,128)(2,1)}, bf16[9216,128]{1,0:T(8,128)(2,1)}, u32[]{:S(2)}, u32[]{:S(2)}) collective-permute-start(bf16[9216,128]{1,0:T(8,128)(2,1)} %bitcast.26), channel_id=1, source_target_pairs={{0,2},{1,3},{2,0},{3,1},{4,6},{5,7},{6,4},{7,5},{8,10},{9,11},{10,... | collective-permute-start | bytes 7077896 | tf_op jit(solution)/shard_map/ppermute | solution.py:326
  2.9 0.0 collective-permute-start
  2.9 0.7 convert_element_type.10.weight_ref
  3.6 1.7 %copy-done.7 = bf16[256,4,9,128]{3,1,2,0:T(4,128)(2,1)S(1)} copy-done((bf16[256,4,9,128]{3,1,2,0:T(4,128)(2,1)S(1)}, bf16[256,4,9,128]{3,1,2,0:T(4,128)(2,1)}, u32[]{:S(2)}) %copy-start.7) | copy-done | bytes 2359320
  5.2 0.7 copy-done.9
  5.9 0.7 copy-done.10
  6.6 0.7 copy-done.11
  7.2 1.2 listings.1
  8.5 0.9 copy-done.6
  9.4 9.7 %all-to-all-start = ((bf16[32,104,128]{2,1,0:T(8,128)(2,1)}), bf16[32,104,128]{2,1,0:T(8,128)(2,1)}, u32[]{:S(2)}, u32[]{:S(2)}) async-start(bf16[32,104,128]{2,1,0:T(8,128)(2,1)} %bitcast.25), calls=%async_computation | async-start | bytes 1703936 | tf_op jit(solution)/shard_map/all_to_all | solution.py:374
  19.1 0.9 slice.24
  20.0 0.1 dynamic-slice_bitcast_fusion
  20.1 1.0 copy-done.12
  21.1 1.2 pad_maximum_fusion
  22.3 2.4 %collective-permute-start.1 = (bf16[20,256,128]{2,1,0:T(8,128)(2,1)}, bf16[20,256,128]{2,1,0:T(8,128)(2,1)}, u32[]{:S(2)}, u32[]{:S(2)}) collective-permute-start(bf16[20,256,128]{2,1,0:T(8,128)(2,1)} %pad_maximum_fusion), channel_id=1, source_target_pairs={{0,6},{1,7},{2,4},{3,5},{4,2},{5,3},{6,0},{7,1},{8,14},{9,15},{10,... | collective-permute-start | bytes 3932168 | tf_op jit(solution)/shard_map/ppermute | solution.py:326
  24.7 0.0 collective-permute-start.2
  24.8 0.3 select_convert_fusion
  25.1 29.0 %collective-permute-done.5.refs_0_ = bf16[9216,128]{1,0:T(8,128)(2,1)} collective-permute-done((bf16[9216,128]{1,0:T(8,128)(2,1)}, bf16[9216,128]{1,0:T(8,128)(2,1)}, u32[]{:S(2)}, u32[]{:S(2)}) %collective-permute-start.5) | collective-permute-done | bytes 2359328 | tf_op jit(solution)/shard_map/ppermute | solution.py:326
  54.0 0.0 collective-permute-start.6
  54.0 0.1 select_convert_fusion.1
  54.1 14.2 %collective-permute-done.2.refs_1_ = bf16[10,256,128]{2,1,0:T(8,128)(2,1)} collective-permute-done((bf16[10,256,128]{2,1,0:T(8,128)(2,1)S(1)}, bf16[10,256,128]{2,1,0:T(8,128)(2,1)}, u32[]{:S(2)}, u32[]{:S(2)}) %collective-permute-start.2) | collective-permute-done | bytes 655392 | tf_op jit(solution)/shard_map/ppermute | solution.py:326
  68.3 1.4 %collective-permute-start.3 = (bf16[10,256,128]{2,1,0:T(8,128)(2,1)}, bf16[10,256,128]{2,1,0:T(8,128)(2,1)}, u32[]{:S(2)}, u32[]{:S(2)}) collective-permute-start(bf16[10,256,128]{2,1,0:T(8,128)(2,1)} %collective-permute-done.2.refs_1_), channel_id=1, source_target_pairs={{0,64},{8,72},{16,80},{24,88},{32,96},{40,104},{48,112},{56,120},{... | collective-permute-start | bytes 1966088 | tf_op jit(solution)/shard_map/ppermute | solution.py:337
  69.7 1.8 %collective-permute-start.4 = (bf16[10,256,128]{2,1,0:T(8,128)(2,1)}, bf16[10,256,128]{2,1,0:T(8,128)(2,1)}, u32[]{:S(2)}, u32[]{:S(2)}) collective-permute-start(bf16[10,256,128]{2,1,0:T(8,128)(2,1)} %collective-permute-done.2.refs_1_), channel_id=1, source_target_pairs={{0,192},{8,200},{16,208},{24,216},{32,224},{40,232},{48,240},{56,2... | collective-permute-start | bytes 1966088 | tf_op jit(solution)/shard_map/ppermute | solution.py:337
  71.5 3.0 %by_harmonic.2.refs_2_ = bf16[256,64,128]{2,1,0:T(8,128)(2,1)S(1)} custom-call(s32[1]{0:T(128)} %constant.146.clone.starts_ref, bf16[50,256,128]{2,1,0:T(8,128)(2,1)S(1)} %bitcast.24), custom_call_target="tpu_custom_call" | custom-call | bytes 14942208 | tf_op jit(solution)/shard_map/by_harmonic/pallas_call | solution.py:64
  74.5 1.9 %copy-done.1 = bf16[256,64,128]{2,1,0:T(8,128)(2,1)} copy-done((bf16[256,64,128]{2,1,0:T(8,128)(2,1)}, bf16[256,64,128]{2,1,0:T(8,128)(2,1)S(1)}, u32[]{:S(2)}) %copy-start.1) | copy-done | bytes 4194328
  76.5 0.1 stack.39.starts_ref
  76.6 0.0 all-to-all-done
  76.6 3.7 %shares.1 = f32[3264,128]{1,0:T(8,128)} custom-call(bf16[32,13,8,128]{3,2,1,0:T(8,128)(2,1)} %bitcast.15.arrived_ref), custom_call_target="tpu_custom_call" | custom-call | flops 4000000000 | bytes 8000000 | tf_op jit(solution)/shard_map/shares/pallas_call | solution.py:300
  80.3 6.3 %all-to-all-start.1 = ((f32[8,51,8,128]{3,2,1,0:T(8,128)}), f32[8,51,8,128]{3,2,1,0:T(8,128)}, u32[]{:S(2)}, u32[]{:S(2)}) async-start(f32[8,51,8,128]{3,2,1,0:T(8,128)} %bitcast.16), calls=%async_computation.1 | async-start | bytes 3342336 | tf_op jit(solution)/shard_map/all_to_all | solution.py:377
  86.6 0.1 and_select_fusion
  86.7 0.0 copy-start.8
  86.7 0.0 collective-permute-done.1.refs_0_
  86.7 0.0 collective-permute-done.3.refs_2_
  86.7 5.0 %by_harmonic.3.refs_3_ = bf16[256,64,128]{2,1,0:T(8,128)(2,1)S(1)} custom-call(s32[5]{0:T(128)S(1)} %stack.39.starts_ref, bf16[20,256,128]{2,1,0:T(8,128)(2,1)} %collective-permute-done.1.refs_0_, bf16[10,256,128]{2,1,0:T(8,128)(2,1)} %collective-permute-done.2.refs_1_, bf16[10,256,128]{2,1,0:T(8,128)(2,1)} %collective-permute-done.3.refs_2_, ...), custom_call_target="tpu_custom_call" | custom-call | bytes 14942208 | tf_op jit(solution)/shard_map/by_harmonic/pallas_call | solution.py:64
  91.8 0.0 collective-permute-done.refs_1_
  91.8 9.8 %score.2 = f32[8,128]{1,0:T(8,128)S(1)} custom-call(s32[2]{0:T(128)S(1)} %get-tuple-element.9.places_ref, bf16[9216,128]{1,0:T(8,128)(2,1)S(1)} %bitcast.29, bf16[9216,128]{1,0:T(8,128)(2,1)} %collective-permute-done.refs_1_, bf16[256,64,128]{2,1,0:T(8,128)(2,1)S(1)} %copy-done.2, bf16[256,64,128]{2,1,0:T(8,128)(2,1)S(1)} %by_harmonic.3.refs_3_, ...), custom_call_target="tpu_custom_call" | custom-call | flops 14722007040 | bytes 20000000 | tf_op jit(solution)/shard_map/score/pallas_call | solution.py:171
  101.7 2.0 %copy-done.4 = bf16[256,64,128]{2,1,0:T(8,128)(2,1)} copy-done((bf16[256,64,128]{2,1,0:T(8,128)(2,1)}, bf16[256,64,128]{2,1,0:T(8,128)(2,1)S(1)}, u32[]{:S(2)}) %copy-start.4) | copy-done | bytes 4194328
  103.7 4.2 %all-to-all-done.1 = f32[8,51,8,128]{3,2,1,0:T(8,128)} async-done(((f32[8,51,8,128]{3,2,1,0:T(8,128)}), f32[8,51,8,128]{3,2,1,0:T(8,128)}, u32[]{:S(2)}, u32[]{:S(2)}) %all-to-all-start.1) | async-done | bytes 1671200 | tf_op jit(solution)/shard_map/all_to_all | solution.py:377
  107.9 1.5 %reduce_sum.9 = f32[51,8,128]{2,1,0:T(8,128)S(1)} reduce(f32[8,51,8,128]{3,2,1,0:T(8,128)} %all-to-all-done.1, f32[]{:T(128)} %constant.144.clone.1), dimensions={0}, to_apply=%region_0.1 | reduce | flops 365568 | bytes 1880068 | tf_op jit(solution)/shard_map/reduce_sum | solution.py:378
  109.5 0.0 collective-permute-done.6.refs_1_
  109.5 2.2 %copy-done.3 = bf16[256,64,128]{2,1,0:T(8,128)(2,1)S(1)} copy-done((bf16[256,64,128]{2,1,0:T(8,128)(2,1)S(1)}, bf16[256,64,128]{2,1,0:T(8,128)(2,1)}, u32[]{:S(2)}) %copy-start.3) | copy-done | bytes 4194328
  111.7 2.2 %copy-done.5 = bf16[256,64,128]{2,1,0:T(8,128)(2,1)S(1)} copy-done((bf16[256,64,128]{2,1,0:T(8,128)(2,1)S(1)}, bf16[256,64,128]{2,1,0:T(8,128)(2,1)}, u32[]{:S(2)}) %copy-start.5) | copy-done | bytes 4194328
  113.8 10.6 %score.3 = f32[8,128]{1,0:T(8,128)S(1)} custom-call(s32[2]{0:T(128)S(1)} %get-tuple-element.8.places_ref, bf16[9216,128]{1,0:T(8,128)(2,1)} %collective-permute-done.5.refs_0_, bf16[9216,128]{1,0:T(8,128)(2,1)} %collective-permute-done.6.refs_1_, bf16[256,64,128]{2,1,0:T(8,128)(2,1)S(1)} %copy-done.3, bf16[256,64,128]{2,1,0:T(8,128)(2,1)S(1)} %copy-done.5, ...), custom_call_target="tpu_custom_call" | custom-call | flops 14722007040 | bytes 20000000 | tf_op jit(solution)/shard_map/score/pallas_call | solution.py:171
  124.5 0.1 collective-permute-start.7
  124.6 0.8 fusion.2
  125.4 2.8 %collective-permute-done.7 = f32[16,128]{1,0:T(8,128)S(1)} collective-permute-done((f32[16,128]{1,0:T(8,128)S(1)}, f32[16,128]{1,0:T(8,128)S(1)}, u32[]{:S(2)}, u32[]{:S(2)}) %collective-permute-start.7) | collective-permute-done | bytes 8224 | tf_op jit(solution)/shard_map/ppermute | solution.py:326
  128.2 0.1 slice_select_fusion.1
  128.3 0.6 pad_maximum_fusion.1
  (24 shorter events, 0.1 us)
Async XLA Ops:
  0.6 53.4 %collective-permute-start.5 = (bf16[9216,128]{1,0:T(8,128)(2,1)}, bf16[9216,128]{1,0:T(8,128)(2,1)}, u32[]{:S(2)}, u32[]{:S(2)}) collective-permute-start(bf16[9216,128]{1,0:T(8,128)(2,1)} %bitcast.26), channel_id=1, source_target_pairs={{0,2},{1,3},{2,0},{3,1},{4,6},{5,7},{6,4},{7,5},{8,10},{9,11},{10,... | collective-permute-start | bytes 7077896 | tf_op jit(solution)/shard_map/ppermute | solution.py:326
  2.9 88.9 %collective-permute-start = (bf16[9216,128]{1,0:T(8,128)(2,1)}, bf16[9216,128]{1,0:T(8,128)(2,1)}, u32[]{:S(2)}, u32[]{:S(2)}) collective-permute-start(bf16[9216,128]{1,0:T(8,128)(2,1)} %bitcast.27), channel_id=1, source_target_pairs={{0,1},{1,0},{2,3},{3,2},{4,5},{5,4},{6,7},{7,6},{8,9},{9,8},{10,11... | collective-permute-start | bytes 7077896 | tf_op jit(solution)/shard_map/ppermute | solution.py:326
  3.6 1.7 %copy-start.7 = (bf16[256,4,9,128]{3,1,2,0:T(4,128)(2,1)S(1)}, bf16[256,4,9,128]{3,1,2,0:T(4,128)(2,1)}, u32[]{:S(2)}) copy-start(bf16[256,4,9,128]{3,1,2,0:T(4,128)(2,1)} %param.7) | copy-start | bytes 7077892
  5.2 0.7 copy-start.9
  5.9 0.7 copy-start.10
  6.6 0.7 copy-start.11
  7.2 11.9 %copy-start = (bf16[256,50,128]{2,0,1:T(8,128)(2,1)S(1)}, bf16[256,50,128]{2,0,1:T(8,128)(2,1)}, u32[]{:S(2)}) copy-start(bf16[256,50,128]{2,0,1:T(8,128)(2,1)} %param.8) | copy-start | bytes 9830404
  8.4 0.9 copy-start.6
  9.4 67.2 %all-to-all-start = ((bf16[32,104,128]{2,1,0:T(8,128)(2,1)}), bf16[32,104,128]{2,1,0:T(8,128)(2,1)}, u32[]{:S(2)}, u32[]{:S(2)}) async-start(bf16[32,104,128]{2,1,0:T(8,128)(2,1)} %bitcast.25), calls=%async_computation | async-start | bytes 1703936 | tf_op jit(solution)/shard_map/all_to_all | solution.py:374
  20.0 1.1 copy-start.12
  22.3 64.4 %collective-permute-start.1 = (bf16[20,256,128]{2,1,0:T(8,128)(2,1)}, bf16[20,256,128]{2,1,0:T(8,128)(2,1)}, u32[]{:S(2)}, u32[]{:S(2)}) collective-permute-start(bf16[20,256,128]{2,1,0:T(8,128)(2,1)} %pad_maximum_fusion), channel_id=1, source_target_pairs={{0,6},{1,7},{2,4},{3,5},{4,2},{5,3},{6,0},{7,1},{8,14},{9,15},{10,... | collective-permute-start | bytes 3932168 | tf_op jit(solution)/shard_map/ppermute | solution.py:326
  24.7 43.5 %collective-permute-start.2 = (bf16[10,256,128]{2,1,0:T(8,128)(2,1)S(1)}, bf16[10,256,128]{2,1,0:T(8,128)(2,1)}, u32[]{:S(2)}, u32[]{:S(2)}) collective-permute-start(bf16[10,256,128]{2,1,0:T(8,128)(2,1)S(1)} %get-tuple-element.2), channel_id=1, source_target_pairs={{0,6},{1,7},{2,4},{3,5},{4,2},{5,3},{6,0},{7,1},{8,14},{9,15},{10,... | collective-permute-start | bytes 1966088 | tf_op jit(solution)/shard_map/ppermute | solution.py:326
  54.0 55.4 %collective-permute-start.6 = (bf16[9216,128]{1,0:T(8,128)(2,1)}, bf16[9216,128]{1,0:T(8,128)(2,1)}, u32[]{:S(2)}, u32[]{:S(2)}) collective-permute-start(bf16[9216,128]{1,0:T(8,128)(2,1)} %collective-permute-done.5.refs_0_), channel_id=1, source_target_pairs={{0,1},{1,0},{2,3},{3,2},{4,5},{5,4},{6,7},{7,6},{8,9},{9,8},{10,11... | collective-permute-start | bytes 7077896 | tf_op jit(solution)/shard_map/ppermute | solution.py:326
  68.3 18.5 %collective-permute-start.3 = (bf16[10,256,128]{2,1,0:T(8,128)(2,1)}, bf16[10,256,128]{2,1,0:T(8,128)(2,1)}, u32[]{:S(2)}, u32[]{:S(2)}) collective-permute-start(bf16[10,256,128]{2,1,0:T(8,128)(2,1)} %collective-permute-done.2.refs_1_), channel_id=1, source_target_pairs={{0,64},{8,72},{16,80},{24,88},{32,96},{40,104},{48,112},{56,120},{... | collective-permute-start | bytes 1966088 | tf_op jit(solution)/shard_map/ppermute | solution.py:337
  69.7 17.0 %collective-permute-start.4 = (bf16[10,256,128]{2,1,0:T(8,128)(2,1)}, bf16[10,256,128]{2,1,0:T(8,128)(2,1)}, u32[]{:S(2)}, u32[]{:S(2)}) collective-permute-start(bf16[10,256,128]{2,1,0:T(8,128)(2,1)} %collective-permute-done.2.refs_1_), channel_id=1, source_target_pairs={{0,192},{8,200},{16,208},{24,216},{32,224},{40,232},{48,240},{56,2... | collective-permute-start | bytes 1966088 | tf_op jit(solution)/shard_map/ppermute | solution.py:337
  74.5 1.9 %copy-start.1 = (bf16[256,64,128]{2,1,0:T(8,128)(2,1)}, bf16[256,64,128]{2,1,0:T(8,128)(2,1)S(1)}, u32[]{:S(2)}) copy-start(bf16[256,64,128]{2,1,0:T(8,128)(2,1)S(1)} %by_harmonic.2.refs_2_) | copy-start | bytes 12582916
  80.3 27.6 %all-to-all-start.1 = ((f32[8,51,8,128]{3,2,1,0:T(8,128)}), f32[8,51,8,128]{3,2,1,0:T(8,128)}, u32[]{:S(2)}, u32[]{:S(2)}) async-start(f32[8,51,8,128]{3,2,1,0:T(8,128)} %bitcast.16), calls=%async_computation.1 | async-start | bytes 3342336 | tf_op jit(solution)/shard_map/all_to_all | solution.py:377
  86.7 5.1 %copy-start.2 = (bf16[256,64,128]{2,1,0:T(8,128)(2,1)S(1)}, bf16[256,64,128]{2,1,0:T(8,128)(2,1)}, u32[]{:S(2)}) copy-start(bf16[256,64,128]{2,1,0:T(8,128)(2,1)} %copy-done.1) | copy-start | bytes 12582916
  86.7 5.1 %copy-start.8 = (bf16[256,4,9,128]{3,1,2,0:T(4,128)(2,1)S(1)}, bf16[256,4,9,128]{3,1,2,0:T(4,128)(2,1)}, u32[]{:S(2)}) copy-start(bf16[256,4,9,128]{3,1,2,0:T(4,128)(2,1)} %param.7) | copy-start | bytes 7077892
  101.6 2.0 %copy-start.4 = (bf16[256,64,128]{2,1,0:T(8,128)(2,1)}, bf16[256,64,128]{2,1,0:T(8,128)(2,1)S(1)}, u32[]{:S(2)}) copy-start(bf16[256,64,128]{2,1,0:T(8,128)(2,1)S(1)} %by_harmonic.3.refs_3_) | copy-start | bytes 12582916
  109.5 2.2 %copy-start.3 = (bf16[256,64,128]{2,1,0:T(8,128)(2,1)S(1)}, bf16[256,64,128]{2,1,0:T(8,128)(2,1)}, u32[]{:S(2)}) copy-start(bf16[256,64,128]{2,1,0:T(8,128)(2,1)} %copy-done.1) | copy-start | bytes 12582916
  111.7 2.2 %copy-start.5 = (bf16[256,64,128]{2,1,0:T(8,128)(2,1)S(1)}, bf16[256,64,128]{2,1,0:T(8,128)(2,1)}, u32[]{:S(2)}) copy-start(bf16[256,64,128]{2,1,0:T(8,128)(2,1)} %copy-done.4) | copy-start | bytes 12582916
  124.5 3.7 %collective-permute-start.7 = (f32[16,128]{1,0:T(8,128)S(1)}, f32[16,128]{1,0:T(8,128)S(1)}, u32[]{:S(2)}, u32[]{:S(2)}) collective-permute-start(f32[16,128]{1,0:T(8,128)S(1)} %pad_maximum_fusion.2), channel_id=1, source_target_pairs={{0,6},{1,7},{2,4},{3,5},{4,2},{5,3},{6,0},{7,1},{8,14},{9,15},{10,... | collective-permute-start | bytes 24584 | tf_op jit(solution)/shard_map/ppermute | solution.py:326

commit v7 on v6

--- a/solution.py
+++ b/solution.py
@@ -345,14 +345,15 @@
     partner_mate = across(partner)
 
     place = lax.axis_index("dom") // (doms // ring)
-    window = class_count // (ring + 1)
+    window = class_count // ring
     straight = class_count - ring * window
 
-    def window_of(x):
-        return lax.dynamic_slice_in_dim(class_major, straight + window * x, window, 0)
-
-    piece = facing(window_of(place))
-    far = facing(jnp.concatenate([class_major[:straight], window_of((place + 2) % ring)]))
+    def window_of(classes, x):
+        return lax.dynamic_slice_in_dim(classes, straight + window * x, window, 0)
+
+    nearest, again = lax.optimization_barrier((window_of(class_major, place), class_major))
+    piece = facing(nearest)
+    far = facing(jnp.concatenate([again[:straight], window_of(again, (place + 2) % ring)]))
     from_left = around(piece, 1)
     from_right = around(piece, -1)
 

time: 131 us -> 113 us (0.86)
  the two profiles are of different devices: /device:TPU:8 before, /device:TPU:100 now
where the time goes in v7:
time: 113 us
  waiting for transfers between devices  35.7 us (32%)
  Pallas kernels  33.4 us (30%)
  starting transfers between devices  23.1 us (20%)
  local copies, waits for them, and re-layouts  14 us (12%)
  other arithmetic  5.34 us (5%)
    ppermute x6, waiting for transfers between devices, move(): return lax.ppermute(value, 'cls', pairs)  30.1 us
    pallas_call x2, Pallas kernels, best_of_groups(): pl.pallas_call(functools.partial(score_kernel, scale, rows, shifts, group...  20.4 us
    unnamed x24, local copies, waits for them, and re-layouts  12.9 us
    all_to_all x1, starting transfers between devices, on_device(): lax.all_to_all(payload.reshape(doms, tiles * depth, cycle_parts), 'dom',...  10.3 us
    pallas_call x2, Pallas kernels, by_harmonic(): pl.pallas_call(functools.partial(gather_kernel, sizes), in_specs=[SCALARS...  8.06 us
    ppermute x6, starting transfers between devices, move(): return lax.ppermute(value, 'cls', pairs)  6.15 us
    all_to_all x1, waiting for transfers between devices, on_device(): shares = lax.all_to_all(sums, 'cls', 0, 0, tiled=True)  5.64 us
    all_to_all x1, starting transfers between devices, on_device(): shares = lax.all_to_all(sums, 'cls', 0, 0, tiled=True)  4.59 us
  transfers between devices with their start and end apart: 10, of which 4 were waited for; matrix products, arithmetic and copies ran while one was open for 5% of the time, Pallas kernels for 20%

profile of v7, /device:TPU:100, one launch (start us, length us, event | category | flops | bytes accessed | tf_op | source)
XLA Modules:
  0.0 112.5 jit_solution(5786916928372225196)
XLA Ops:
  0.6 1.7 %collective-permute-start.5 = (bf16[9216,128]{1,0:T(8,128)(2,1)}, bf16[9216,128]{1,0:T(8,128)(2,1)}, u32[]{:S(2)}, u32[]{:S(2)}) collective-permute-start(bf16[9216,128]{1,0:T(8,128)(2,1)} %bitcast.25), channel_id=1, source_target_pairs={{0,2},{1,3},{2,0},{3,1},{4,6},{5,7},{6,4},{7,5},{8,10},{9,11},{10,... | collective-permute-start | bytes 7077896 | tf_op jit(solution)/shard_map/ppermute | solution.py:326
  2.3 0.0 collective-permute-start
  2.3 0.7 convert_element_type.10.weight_ref
  3.0 1.7 %copy-done.7 = bf16[256,4,9,128]{3,1,2,0:T(4,128)(2,1)S(1)} copy-done((bf16[256,4,9,128]{3,1,2,0:T(4,128)(2,1)S(1)}, bf16[256,4,9,128]{3,1,2,0:T(4,128)(2,1)}, u32[]{:S(2)}) %copy-start.7) | copy-done | bytes 2359320
  4.6 0.7 copy-done.9
  5.3 0.7 copy-done.10
  6.0 0.7 copy-done.11
  6.7 1.2 %listings.1 = bf16[32,13,8,128]{3,2,1,0:T(8,128)(2,1)S(1)} custom-call(s32[4,3]{1,0:T(4,128)S(1)} %copy-done.9, s32[4,3]{1,0:T(4,128)S(1)} %copy-done.10, s32[4]{0:T(128)S(1)} %copy-done.11, f32[4,3]{1,0:T(4,128)S(1)} %convert_element_type.10.weight_ref, bf16[9216,128]{1,0:T(8,128)(2,1)S(1)} %bitcast.27), custom_call_target="tpu_custom_call" | custom-call | bytes 8000000 | tf_op jit(solution)/shard_map/listings/pallas_call | solution.py:224
  7.9 0.9 copy-done.6
  8.8 10.3 %all-to-all-start = ((bf16[32,104,128]{2,1,0:T(8,128)(2,1)}), bf16[32,104,128]{2,1,0:T(8,128)(2,1)}, u32[]{:S(2)}, u32[]{:S(2)}) async-start(bf16[32,104,128]{2,1,0:T(8,128)(2,1)} %bitcast.24), calls=%async_computation | async-start | bytes 1703936 | tf_op jit(solution)/shard_map/all_to_all | solution.py:375
  19.1 1.0 dynamic-slice_bitcast_fusion
  20.1 2.2 %collective-permute-start.2 = (bf16[12,256,128]{2,1,0:T(8,128)(2,1)}, bf16[12,256,128]{2,1,0:T(8,128)(2,1)}, u32[]{:S(2)}, u32[]{:S(2)}) collective-permute-start(bf16[12,256,128]{2,1,0:T(8,128)(2,1)} %dynamic-slice_bitcast_fusion), channel_id=1, source_target_pairs={{0,6},{1,7},{2,4},{3,5},{4,2},{5,3},{6,0},{7,1},{8,14},{9,15},{10,... | collective-permute-start | bytes 2359304 | tf_op jit(solution)/shard_map/ppermute | solution.py:326
  22.3 0.1 constant_dynamic-slice_fusion
  22.3 1.1 pad_maximum_fusion
  23.5 1.1 collective-permute-start.1
  24.5 0.3 select_convert_fusion
  24.8 17.2 %collective-permute-done.2.refs_1_ = bf16[12,256,128]{2,1,0:T(8,128)(2,1)} collective-permute-done((bf16[12,256,128]{2,1,0:T(8,128)(2,1)}, bf16[12,256,128]{2,1,0:T(8,128)(2,1)}, u32[]{:S(2)}, u32[]{:S(2)}) %collective-permute-start.2) | collective-permute-done | bytes 786464 | tf_op jit(solution)/shard_map/ppermute | solution.py:326
  42.0 1.2 %collective-permute-start.3 = (bf16[12,256,128]{2,1,0:T(8,128)(2,1)}, bf16[12,256,128]{2,1,0:T(8,128)(2,1)}, u32[]{:S(2)}, u32[]{:S(2)}) collective-permute-start(bf16[12,256,128]{2,1,0:T(8,128)(2,1)} %collective-permute-done.2.refs_1_), channel_id=1, source_target_pairs={{0,64},{8,72},{16,80},{24,88},{32,96},{40,104},{48,112},{56,120},{... | collective-permute-start | bytes 2359304 | tf_op jit(solution)/shard_map/ppermute | solution.py:337
  43.2 0.8 collective-permute-start.4
  44.0 10.0 %collective-permute-done.5.refs_0_ = bf16[9216,128]{1,0:T(8,128)(2,1)} collective-permute-done((bf16[9216,128]{1,0:T(8,128)(2,1)}, bf16[9216,128]{1,0:T(8,128)(2,1)}, u32[]{:S(2)}, u32[]{:S(2)}) %collective-permute-start.5) | collective-permute-done | bytes 2359328 | tf_op jit(solution)/shard_map/ppermute | solution.py:326
  54.0 0.0 collective-permute-start.6
  54.0 0.1 select_convert_fusion.1
  54.2 3.0 %by_harmonic.2.refs_2_ = bf16[256,64,128]{2,1,0:T(8,128)(2,1)S(1)} custom-call(s32[1]{0:T(128)} %constant.146.clone.starts_ref, bf16[50,256,128]{2,1,0:T(8,128)(2,1)S(1)} %bitcast.23), custom_call_target="tpu_custom_call" | custom-call | bytes 14942208 | tf_op jit(solution)/shard_map/by_harmonic/pallas_call | solution.py:64
  57.2 1.9 %copy-done.1 = bf16[256,64,128]{2,1,0:T(8,128)(2,1)} copy-done((bf16[256,64,128]{2,1,0:T(8,128)(2,1)}, bf16[256,64,128]{2,1,0:T(8,128)(2,1)S(1)}, u32[]{:S(2)}) %copy-start.1) | copy-done | bytes 4194328
  59.2 0.1 stack.39.starts_ref
  59.3 0.0 all-to-all-done
  59.3 3.7 %shares.1 = f32[3264,128]{1,0:T(8,128)} custom-call(bf16[32,13,8,128]{3,2,1,0:T(8,128)(2,1)} %bitcast.14.arrived_ref), custom_call_target="tpu_custom_call" | custom-call | flops 4000000000 | bytes 8000000 | tf_op jit(solution)/shard_map/shares/pallas_call | solution.py:300
  63.0 4.6 %all-to-all-start.1 = ((f32[8,51,8,128]{3,2,1,0:T(8,128)}), f32[8,51,8,128]{3,2,1,0:T(8,128)}, u32[]{:S(2)}, u32[]{:S(2)}) async-start(f32[8,51,8,128]{3,2,1,0:T(8,128)} %bitcast.15), calls=%async_computation.1 | async-start | bytes 3342336 | tf_op jit(solution)/shard_map/all_to_all | solution.py:378
  67.6 0.1 and_select_fusion
  67.7 0.0 copy-start.8
  67.7 0.0 collective-permute-done.1.refs_0_
  67.7 0.0 collective-permute-done.3.refs_2_
  67.7 0.0 collective-permute-done.4.refs_3_
  67.7 5.0 %by_harmonic.3.refs_3_ = bf16[256,64,128]{2,1,0:T(8,128)(2,1)S(1)} custom-call(s32[5]{0:T(128)S(1)} %stack.39.starts_ref, bf16[14,256,128]{2,1,0:T(8,128)(2,1)} %collective-permute-done.1.refs_0_, bf16[12,256,128]{2,1,0:T(8,128)(2,1)} %collective-permute-done.2.refs_1_, bf16[12,256,128]{2,1,0:T(8,128)(2,1)} %collective-permute-done.3.refs_2_, ...), custom_call_target="tpu_custom_call" | custom-call | bytes 14942208 | tf_op jit(solution)/shard_map/by_harmonic/pallas_call | solution.py:64
  72.8 0.0 collective-permute-done.refs_1_
  72.8 9.8 %score.2 = f32[8,128]{1,0:T(8,128)S(1)} custom-call(s32[2]{0:T(128)S(1)} %get-tuple-element.11.places_ref, bf16[9216,128]{1,0:T(8,128)(2,1)S(1)} %bitcast.28, bf16[9216,128]{1,0:T(8,128)(2,1)} %collective-permute-done.refs_1_, bf16[256,64,128]{2,1,0:T(8,128)(2,1)S(1)} %copy-done.2, bf16[256,64,128]{2,1,0:T(8,128)(2,1)S(1)} %by_harmonic.3.refs_3_, ...), custom_call_target="tpu_custom_call" | custom-call | flops 14722007040 | bytes 20000000 | tf_op jit(solution)/shard_map/score/pallas_call | solution.py:171
  82.6 2.0 %copy-done.4 = bf16[256,64,128]{2,1,0:T(8,128)(2,1)} copy-done((bf16[256,64,128]{2,1,0:T(8,128)(2,1)}, bf16[256,64,128]{2,1,0:T(8,128)(2,1)S(1)}, u32[]{:S(2)}) %copy-start.4) | copy-done | bytes 4194328
  84.7 5.6 %all-to-all-done.1 = f32[8,51,8,128]{3,2,1,0:T(8,128)} async-done(((f32[8,51,8,128]{3,2,1,0:T(8,128)}), f32[8,51,8,128]{3,2,1,0:T(8,128)}, u32[]{:S(2)}, u32[]{:S(2)}) %all-to-all-start.1) | async-done | bytes 1671200 | tf_op jit(solution)/shard_map/all_to_all | solution.py:378
  90.3 1.5 %reduce_sum.9 = f32[51,8,128]{2,1,0:T(8,128)S(1)} reduce(f32[8,51,8,128]{3,2,1,0:T(8,128)} %all-to-all-done.1, f32[]{:T(128)} %constant.144.clone.1), dimensions={0}, to_apply=%region_0.1 | reduce | flops 365568 | bytes 1880068 | tf_op jit(solution)/shard_map/reduce_sum | solution.py:379
  91.9 0.0 collective-permute-done.6.refs_1_
  91.9 2.2 %copy-done.3 = bf16[256,64,128]{2,1,0:T(8,128)(2,1)S(1)} copy-done((bf16[256,64,128]{2,1,0:T(8,128)(2,1)S(1)}, bf16[256,64,128]{2,1,0:T(8,128)(2,1)}, u32[]{:S(2)}) %copy-start.3) | copy-done | bytes 4194328
  94.1 2.2 %copy-done.5 = bf16[256,64,128]{2,1,0:T(8,128)(2,1)S(1)} copy-done((bf16[256,64,128]{2,1,0:T(8,128)(2,1)S(1)}, bf16[256,64,128]{2,1,0:T(8,128)(2,1)}, u32[]{:S(2)}) %copy-start.5) | copy-done | bytes 4194328
  96.3 10.6 %score.3 = f32[8,128]{1,0:T(8,128)S(1)} custom-call(s32[2]{0:T(128)S(1)} %get-tuple-element.10.places_ref, bf16[9216,128]{1,0:T(8,128)(2,1)} %collective-permute-done.5.refs_0_, bf16[9216,128]{1,0:T(8,128)(2,1)} %collective-permute-done.6.refs_1_, bf16[256,64,128]{2,1,0:T(8,128)(2,1)S(1)} %copy-done.3, bf16[256,64,128]{2,1,0:T(8,128)(2,1)S(1)} %copy-done.5, ...), custom_call_target="tpu_custom_call" | custom-call | flops 14722007040 | bytes 20000000 | tf_op jit(solution)/shard_map/score/pallas_call | solution.py:171
  106.9 1.2 %collective-permute-start.7 = (f32[16,128]{1,0:T(8,128)S(1)}, f32[16,128]{1,0:T(8,128)S(1)}, u32[]{:S(2)}, u32[]{:S(2)}) collective-permute-start(f32[16,128]{1,0:T(8,128)S(1)} %pad_maximum_fusion.2), channel_id=1, source_target_pairs={{0,6},{1,7},{2,4},{3,5},{4,2},{5,3},{6,0},{7,1},{8,14},{9,15},{10,... | collective-permute-start | bytes 24584 | tf_op jit(solution)/shard_map/ppermute | solution.py:326
  108.1 0.8 fusion.2
  108.9 2.9 %collective-permute-done.7 = f32[16,128]{1,0:T(8,128)S(1)} collective-permute-done((f32[16,128]{1,0:T(8,128)S(1)}, f32[16,128]{1,0:T(8,128)S(1)}, u32[]{:S(2)}, u32[]{:S(2)}) %collective-permute-start.7) | collective-permute-done | bytes 8224 | tf_op jit(solution)/shard_map/ppermute | solution.py:326
  111.8 0.1 slice_select_fusion.1
  111.9 0.6 pad_maximum_fusion.1
  (23 shorter events, 0.1 us)
Async XLA Ops:
  0.6 53.4 %collective-permute-start.5 = (bf16[9216,128]{1,0:T(8,128)(2,1)}, bf16[9216,128]{1,0:T(8,128)(2,1)}, u32[]{:S(2)}, u32[]{:S(2)}) collective-permute-start(bf16[9216,128]{1,0:T(8,128)(2,1)} %bitcast.25), channel_id=1, source_target_pairs={{0,2},{1,3},{2,0},{3,1},{4,6},{5,7},{6,4},{7,5},{8,10},{9,11},{10,... | collective-permute-start | bytes 7077896 | tf_op jit(solution)/shard_map/ppermute | solution.py:326
  2.3 70.5 %collective-permute-start = (bf16[9216,128]{1,0:T(8,128)(2,1)}, bf16[9216,128]{1,0:T(8,128)(2,1)}, u32[]{:S(2)}, u32[]{:S(2)}) collective-permute-start(bf16[9216,128]{1,0:T(8,128)(2,1)} %bitcast.26), channel_id=1, source_target_pairs={{0,1},{1,0},{2,3},{3,2},{4,5},{5,4},{6,7},{7,6},{8,9},{9,8},{10,11... | collective-permute-start | bytes 7077896 | tf_op jit(solution)/shard_map/ppermute | solution.py:326
  3.0 1.7 %copy-start.7 = (bf16[256,4,9,128]{3,1,2,0:T(4,128)(2,1)S(1)}, bf16[256,4,9,128]{3,1,2,0:T(4,128)(2,1)}, u32[]{:S(2)}) copy-start(bf16[256,4,9,128]{3,1,2,0:T(4,128)(2,1)} %param.7) | copy-start | bytes 7077892
  4.6 0.7 copy-start.9
  5.3 0.7 copy-start.10
  6.0 0.7 copy-start.11
  6.7 12.4 %copy-start = (bf16[256,50,128]{2,0,1:T(8,128)(2,1)S(1)}, bf16[256,50,128]{2,0,1:T(8,128)(2,1)}, u32[]{:S(2)}) copy-start(bf16[256,50,128]{2,0,1:T(8,128)(2,1)} %param.8) | copy-start | bytes 9830404
  7.9 0.9 copy-start.6
  8.8 50.5 %all-to-all-start = ((bf16[32,104,128]{2,1,0:T(8,128)(2,1)}), bf16[32,104,128]{2,1,0:T(8,128)(2,1)}, u32[]{:S(2)}, u32[]{:S(2)}) async-start(bf16[32,104,128]{2,1,0:T(8,128)(2,1)} %bitcast.24), calls=%async_computation | async-start | bytes 1703936 | tf_op jit(solution)/shard_map/all_to_all | solution.py:375
  20.1 21.9 %collective-permute-start.2 = (bf16[12,256,128]{2,1,0:T(8,128)(2,1)}, bf16[12,256,128]{2,1,0:T(8,128)(2,1)}, u32[]{:S(2)}, u32[]{:S(2)}) collective-permute-start(bf16[12,256,128]{2,1,0:T(8,128)(2,1)} %dynamic-slice_bitcast_fusion), channel_id=1, source_target_pairs={{0,6},{1,7},{2,4},{3,5},{4,2},{5,3},{6,0},{7,1},{8,14},{9,15},{10,... | collective-permute-start | bytes 2359304 | tf_op jit(solution)/shard_map/ppermute | solution.py:326
  23.5 44.2 %collective-permute-start.1 = (bf16[14,256,128]{2,1,0:T(8,128)(2,1)}, bf16[14,256,128]{2,1,0:T(8,128)(2,1)}, u32[]{:S(2)}, u32[]{:S(2)}) collective-permute-start(bf16[14,256,128]{2,1,0:T(8,128)(2,1)} %pad_maximum_fusion), channel_id=1, source_target_pairs={{0,6},{1,7},{2,4},{3,5},{4,2},{5,3},{6,0},{7,1},{8,14},{9,15},{10,... | collective-permute-start | bytes 2752520 | tf_op jit(solution)/shard_map/ppermute | solution.py:326
  42.0 25.7 %collective-permute-start.3 = (bf16[12,256,128]{2,1,0:T(8,128)(2,1)}, bf16[12,256,128]{2,1,0:T(8,128)(2,1)}, u32[]{:S(2)}, u32[]{:S(2)}) collective-permute-start(bf16[12,256,128]{2,1,0:T(8,128)(2,1)} %collective-permute-done.2.refs_1_), channel_id=1, source_target_pairs={{0,64},{8,72},{16,80},{24,88},{32,96},{40,104},{48,112},{56,120},{... | collective-permute-start | bytes 2359304 | tf_op jit(solution)/shard_map/ppermute | solution.py:337
  43.2 24.5 %collective-permute-start.4 = (bf16[12,256,128]{2,1,0:T(8,128)(2,1)}, bf16[12,256,128]{2,1,0:T(8,128)(2,1)}, u32[]{:S(2)}, u32[]{:S(2)}) collective-permute-start(bf16[12,256,128]{2,1,0:T(8,128)(2,1)} %collective-permute-done.2.refs_1_), channel_id=1, source_target_pairs={{0,192},{8,200},{16,208},{24,216},{32,224},{40,232},{48,240},{56,2... | collective-permute-start | bytes 2359304 | tf_op jit(solution)/shard_map/ppermute | solution.py:337
  54.0 37.8 %collective-permute-start.6 = (bf16[9216,128]{1,0:T(8,128)(2,1)}, bf16[9216,128]{1,0:T(8,128)(2,1)}, u32[]{:S(2)}, u32[]{:S(2)}) collective-permute-start(bf16[9216,128]{1,0:T(8,128)(2,1)} %collective-permute-done.5.refs_0_), channel_id=1, source_target_pairs={{0,1},{1,0},{2,3},{3,2},{4,5},{5,4},{6,7},{7,6},{8,9},{9,8},{10,11... | collective-permute-start | bytes 7077896 | tf_op jit(solution)/shard_map/ppermute | solution.py:326
  57.2 1.9 %copy-start.1 = (bf16[256,64,128]{2,1,0:T(8,128)(2,1)}, bf16[256,64,128]{2,1,0:T(8,128)(2,1)S(1)}, u32[]{:S(2)}) copy-start(bf16[256,64,128]{2,1,0:T(8,128)(2,1)S(1)} %by_harmonic.2.refs_2_) | copy-start | bytes 12582916
  63.0 27.3 %all-to-all-start.1 = ((f32[8,51,8,128]{3,2,1,0:T(8,128)}), f32[8,51,8,128]{3,2,1,0:T(8,128)}, u32[]{:S(2)}, u32[]{:S(2)}) async-start(f32[8,51,8,128]{3,2,1,0:T(8,128)} %bitcast.15), calls=%async_computation.1 | async-start | bytes 3342336 | tf_op jit(solution)/shard_map/all_to_all | solution.py:378
  67.7 5.1 %copy-start.2 = (bf16[256,64,128]{2,1,0:T(8,128)(2,1)S(1)}, bf16[256,64,128]{2,1,0:T(8,128)(2,1)}, u32[]{:S(2)}) copy-start(bf16[256,64,128]{2,1,0:T(8,128)(2,1)} %copy-done.1) | copy-start | bytes 12582916
  67.7 5.1 %copy-start.8 = (bf16[256,4,9,128]{3,1,2,0:T(4,128)(2,1)S(1)}, bf16[256,4,9,128]{3,1,2,0:T(4,128)(2,1)}, u32[]{:S(2)}) copy-start(bf16[256,4,9,128]{3,1,2,0:T(4,128)(2,1)} %param.7) | copy-start | bytes 7077892
  82.6 2.0 %copy-start.4 = (bf16[256,64,128]{2,1,0:T(8,128)(2,1)}, bf16[256,64,128]{2,1,0:T(8,128)(2,1)S(1)}, u32[]{:S(2)}) copy-start(bf16[256,64,128]{2,1,0:T(8,128)(2,1)S(1)} %by_harmonic.3.refs_3_) | copy-start | bytes 12582916
  91.9 2.2 %copy-start.3 = (bf16[256,64,128]{2,1,0:T(8,128)(2,1)S(1)}, bf16[256,64,128]{2,1,0:T(8,128)(2,1)}, u32[]{:S(2)}) copy-start(bf16[256,64,128]{2,1,0:T(8,128)(2,1)} %copy-done.1) | copy-start | bytes 12582916
  94.1 2.2 %copy-start.5 = (bf16[256,64,128]{2,1,0:T(8,128)(2,1)S(1)}, bf16[256,64,128]{2,1,0:T(8,128)(2,1)}, u32[]{:S(2)}) copy-start(bf16[256,64,128]{2,1,0:T(8,128)(2,1)} %copy-done.4) | copy-start | bytes 12582916
  106.9 4.9 %collective-permute-start.7 = (f32[16,128]{1,0:T(8,128)S(1)}, f32[16,128]{1,0:T(8,128)S(1)}, u32[]{:S(2)}, u32[]{:S(2)}) collective-permute-start(f32[16,128]{1,0:T(8,128)S(1)} %pad_maximum_fusion.2), channel_id=1, source_target_pairs={{0,6},{1,7},{2,4},{3,5},{4,2},{5,3},{6,0},{7,1},{8,14},{9,15},{10,... | collective-permute-start | bytes 24584 | tf_op jit(solution)/shard_map/ppermute | solution.py:326

commit v8 on v6

--- a/solution.py
+++ b/solution.py
@@ -179,7 +179,7 @@
             pltpu.VMEM((groups, (CHUNK + 2) * rows, cycle_parts), jnp.float32),
             pltpu.VMEM(((2 * rows * groups + 1) * half, LANES), jnp.float32),
         ],
-        compiler_params=pltpu.CompilerParams(vmem_limit_bytes=26 * 1024 * 1024),
+        compiler_params=pltpu.CompilerParams(vmem_limit_bytes=36 * 1024 * 1024),
         cost_estimate=pl.CostEstimate(flops=6 * flops, bytes_accessed=20_000_000, transcendentals=0),
         name="score",
     )(places, *images, *stacked, table)
@@ -345,7 +345,7 @@
     partner_mate = across(partner)
 
     place = lax.axis_index("dom") // (doms // ring)
-    window = class_count // (ring + 1)
+    window = class_count // ring
     straight = class_count - ring * window
 
     def window_of(x):
@@ -382,11 +382,7 @@
 
     images = [flat, mate, partner, partner_mate]
     places = jnp.stack([(row % 2 ^ chip) * 2 + (core ^ other) for chip in range(2) for other in range(2)])
-    places = places.astype(jnp.int32)
-    home = score(places[:2] % 2, images[:2])
-    away = score(places[2:] % 2, images[2:])
-    even = row % 2 == 0
-    best = jnp.concatenate([jnp.where(even, home, away), jnp.where(even, away, home)], axis=0)
+    best = score(places.astype(jnp.int32), images)
     sent = facing(best)
     mine, others = best[:, :class_count], sent[:, LANES // 2 : LANES // 2 + class_count]
     low = jnp.where(row < chips // 2, mine, others)

time: 131 us -> 151 us (1.15)
  the two profiles are of different devices: /device:TPU:8 before, /device:TPU:198 now
where the time goes in v8:
time: 151 us; the launch traced here: 150 us
  waiting for transfers between devices  72.4 us (48%)
  Pallas kernels  26.9 us (18%)
  starting transfers between devices  26.2 us (17%)
  local copies, waits for them, and re-layouts  17.3 us (11%)
  other arithmetic  6.36 us (4%)
    ppermute x6, waiting for transfers between devices, move(): return lax.ppermute(value, 'cls', pairs)  72.4 us
    unnamed x24, local copies, waits for them, and re-layouts  15.8 us
    pallas_call x1, Pallas kernels, best_of_groups(): pl.pallas_call(functools.partial(score_kernel, scale, rows, shifts, group...  15.7 us
    ppermute x6, starting transfers between devices, move(): return lax.ppermute(value, 'cls', pairs)  10.9 us
    all_to_all x1, starting transfers between devices, on_device(): lax.all_to_all(payload.reshape(doms, tiles * depth, cycle_parts), 'dom',...  8.97 us
    pallas_call x2, Pallas kernels, by_harmonic(): pl.pallas_call(functools.partial(gather_kernel, sizes), in_specs=[SCALARS...  7.44 us
    all_to_all x1, starting transfers between devices, on_device(): shares = lax.all_to_all(sums, 'cls', 0, 0, tiled=True)  4.3 us
  transfers between devices with their start and end apart: 10, of which 4 were waited for; matrix products, arithmetic and copies ran while one was open for 5% of the time, Pallas kernels for 7%

profile of v8, /device:TPU:198, one launch (start us, length us, event | category | flops | bytes accessed | tf_op | source)
XLA Modules:
  0.0 150.0 jit_solution(8521926585873409444)
XLA Ops:
  0.6 1.7 %collective-permute-start.1 = (bf16[9216,128]{1,0:T(8,128)(2,1)}, bf16[9216,128]{1,0:T(8,128)(2,1)}, u32[]{:S(2)}, u32[]{:S(2)}) collective-permute-start(bf16[9216,128]{1,0:T(8,128)(2,1)} %bitcast.26), channel_id=1, source_target_pairs={{0,2},{1,3},{2,0},{3,1},{4,6},{5,7},{6,4},{7,5},{8,10},{9,11},{10,... | collective-permute-start | bytes 7077896 | tf_op jit(solution)/shard_map/ppermute | solution.py:326
  2.3 0.7 convert_element_type.10.weight_ref
  3.0 1.7 %copy-done.6 = bf16[256,4,9,128]{3,1,2,0:T(4,128)(2,1)S(1)} copy-done((bf16[256,4,9,128]{3,1,2,0:T(4,128)(2,1)S(1)}, bf16[256,4,9,128]{3,1,2,0:T(4,128)(2,1)}, u32[]{:S(2)}) %copy-start.6) | copy-done | bytes 2359320
  4.6 0.7 copy-done.9
  5.3 0.7 copy-done.10
  6.0 0.7 copy-done.11
  6.7 1.2 listings.1
  7.9 0.9 copy-done.5
  8.8 9.0 %all-to-all-start = ((bf16[32,104,128]{2,1,0:T(8,128)(2,1)}), bf16[32,104,128]{2,1,0:T(8,128)(2,1)}, u32[]{:S(2)}, u32[]{:S(2)}) async-start(bf16[32,104,128]{2,1,0:T(8,128)(2,1)} %bitcast.25), calls=%async_computation | async-start | bytes 1703936 | tf_op jit(solution)/shard_map/all_to_all | solution.py:374
  17.8 0.1 collective-permute-start
  17.9 36.1 %collective-permute-done.1.refs_2_ = bf16[9216,128]{1,0:T(8,128)(2,1)} collective-permute-done((bf16[9216,128]{1,0:T(8,128)(2,1)}, bf16[9216,128]{1,0:T(8,128)(2,1)}, u32[]{:S(2)}, u32[]{:S(2)}) %collective-permute-start.1) | collective-permute-done | bytes 2359328 | tf_op jit(solution)/shard_map/ppermute | solution.py:326
  54.0 0.0 collective-permute-start.2
  54.0 1.4 dynamic-slice_bitcast_fusion
  55.4 3.0 %collective-permute-start.4 = (bf16[12,256,128]{2,1,0:T(8,128)(2,1)}, bf16[12,256,128]{2,1,0:T(8,128)(2,1)}, u32[]{:S(2)}, u32[]{:S(2)}) collective-permute-start(bf16[12,256,128]{2,1,0:T(8,128)(2,1)} %get-tuple-element.2), channel_id=1, source_target_pairs={{0,6},{1,7},{2,4},{3,5},{4,2},{5,3},{6,0},{7,1},{8,14},{9,15},{10,... | collective-permute-start | bytes 2359304 | tf_op jit(solution)/shard_map/ppermute | solution.py:326
  58.4 0.0 all-to-all-done
  58.4 2.5 %shares.1 = f32[3264,128]{1,0:T(8,128)S(1)} custom-call(bf16[32,13,8,128]{3,2,1,0:T(8,128)(2,1)} %bitcast.15.arrived_ref), custom_call_target="tpu_custom_call" | custom-call | flops 4000000000 | bytes 8000000 | tf_op jit(solution)/shard_map/shares/pallas_call | solution.py:300
  61.0 1.2 copy-done.8
  62.1 4.3 %all-to-all-start.1 = ((f32[8,51,8,128]{3,2,1,0:T(8,128)}), f32[8,51,8,128]{3,2,1,0:T(8,128)}, u32[]{:S(2)}, u32[]{:S(2)}) async-start(f32[8,51,8,128]{3,2,1,0:T(8,128)} %bitcast.30), calls=%async_computation.1 | async-start | bytes 3342336 | tf_op jit(solution)/shard_map/all_to_all | solution.py:377
  66.5 2.2 %pad_maximum_fusion = bf16[14,256,128]{2,1,0:T(8,128)(2,1)} fusion(bf16[12,256,128]{2,1,0:T(8,128)(2,1)} %get-tuple-element.3, bf16[2,256,128]{2,1,0:T(8,128)(2,1)S(1)} %slice.20), kind=kLoop, calls=%fused_computation | loop fusion | flops 458752 | bytes 1835008 | tf_op jit(solution)/shard_map/concatenate | solution.py:355
  68.6 3.1 %collective-permute-start.3 = (bf16[14,256,128]{2,1,0:T(8,128)(2,1)}, bf16[14,256,128]{2,1,0:T(8,128)(2,1)}, u32[]{:S(2)}, u32[]{:S(2)}) collective-permute-start(bf16[14,256,128]{2,1,0:T(8,128)(2,1)} %pad_maximum_fusion), channel_id=1, source_target_pairs={{0,6},{1,7},{2,4},{3,5},{4,2},{5,3},{6,0},{7,1},{8,14},{9,15},{10,... | collective-permute-start | bytes 2752520 | tf_op jit(solution)/shard_map/ppermute | solution.py:326
  71.8 3.0 %by_harmonic.2.refs_4_ = bf16[256,64,128]{2,1,0:T(8,128)(2,1)S(1)} custom-call(s32[1]{0:T(128)} %constant.131.clone.starts_ref, bf16[50,256,128]{2,1,0:T(8,128)(2,1)S(1)} %bitcast.24), custom_call_target="tpu_custom_call" | custom-call | bytes 14942208 | tf_op jit(solution)/shard_map/by_harmonic/pallas_call | solution.py:64
  74.8 0.0 copy-start.1
  74.8 1.9 %copy-done.1 = bf16[256,64,128]{2,1,0:T(8,128)(2,1)} copy-done((bf16[256,64,128]{2,1,0:T(8,128)(2,1)}, bf16[256,64,128]{2,1,0:T(8,128)(2,1)S(1)}, u32[]{:S(2)}) %copy-start.1) | copy-done | bytes 4194328
  76.7 0.1 stack.39.starts_ref
  76.8 2.8 %collective-permute-done.4.refs_1_ = bf16[12,256,128]{2,1,0:T(8,128)(2,1)} collective-permute-done((bf16[12,256,128]{2,1,0:T(8,128)(2,1)}, bf16[12,256,128]{2,1,0:T(8,128)(2,1)}, u32[]{:S(2)}, u32[]{:S(2)}) %collective-permute-start.4) | collective-permute-done | bytes 786464 | tf_op jit(solution)/shard_map/ppermute | solution.py:326
  79.6 0.5 collective-permute-start.5
  80.1 1.5 %collective-permute-start.6 = (bf16[12,256,128]{2,1,0:T(8,128)(2,1)}, bf16[12,256,128]{2,1,0:T(8,128)(2,1)S(1)}, u32[]{:S(2)}, u32[]{:S(2)}) collective-permute-start(bf16[12,256,128]{2,1,0:T(8,128)(2,1)} %collective-permute-done.4.refs_1_), channel_id=1, source_target_pairs={{0,192},{8,200},{16,208},{24,216},{32,224},{40,232},{48,240},{56,2... | collective-permute-start | bytes 2359304 | tf_op jit(solution)/shard_map/ppermute | solution.py:337
  81.6 0.1 pad_add_fusion.places_ref
  81.7 0.1 select_convert_fusion.1
  81.8 0.3 select_convert_fusion
  82.1 32.4 %collective-permute-done.3.refs_0_ = bf16[14,256,128]{2,1,0:T(8,128)(2,1)} collective-permute-done((bf16[14,256,128]{2,1,0:T(8,128)(2,1)}, bf16[14,256,128]{2,1,0:T(8,128)(2,1)}, u32[]{:S(2)}, u32[]{:S(2)}) %collective-permute-start.3) | collective-permute-done | bytes 917536 | tf_op jit(solution)/shard_map/ppermute | solution.py:326
  114.5 0.0 collective-permute-done.5.refs_2_
  114.5 0.0 collective-permute-done.6.refs_3_
  114.5 4.4 %by_harmonic.3.refs_5_ = bf16[256,64,128]{2,1,0:T(8,128)(2,1)S(1)} custom-call(s32[5]{0:T(128)S(1)} %stack.39.starts_ref, bf16[14,256,128]{2,1,0:T(8,128)(2,1)} %collective-permute-done.3.refs_0_, bf16[12,256,128]{2,1,0:T(8,128)(2,1)} %collective-permute-done.4.refs_1_, bf16[12,256,128]{2,1,0:T(8,128)(2,1)S(1)} %collective-permute-done.5.refs_2_, ...), custom_call_target="tpu_custom_call" | custom-call | bytes 14942208 | tf_op jit(solution)/shard_map/by_harmonic/pallas_call | solution.py:64
  119.0 2.0 %copy-done.3 = bf16[256,64,128]{2,1,0:T(8,128)(2,1)} copy-done((bf16[256,64,128]{2,1,0:T(8,128)(2,1)}, bf16[256,64,128]{2,1,0:T(8,128)(2,1)S(1)}, u32[]{:S(2)}) %copy-start.3) | copy-done | bytes 4194328
  121.0 0.0 all-to-all-done.1
  121.0 1.5 %reduce_sum.9 = f32[51,8,128]{2,1,0:T(8,128)S(1)} reduce(f32[8,51,8,128]{3,2,1,0:T(8,128)} %all-to-all-done.1, f32[]{:T(128)} %constant.129.clone.1), dimensions={0}, to_apply=%region_0.1 | reduce | flops 365568 | bytes 1880068 | tf_op jit(solution)/shard_map/reduce_sum | solution.py:378
  122.5 0.0 collective-permute-done.refs_1_
  122.5 0.0 collective-permute-done.2.refs_3_
  122.6 2.2 %copy-done.2 = bf16[256,64,128]{2,1,0:T(8,128)(2,1)S(1)} copy-done((bf16[256,64,128]{2,1,0:T(8,128)(2,1)S(1)}, bf16[256,64,128]{2,1,0:T(8,128)(2,1)}, u32[]{:S(2)}) %copy-start.2) | copy-done | bytes 4194328
  124.8 2.2 %copy-done.4 = bf16[256,64,128]{2,1,0:T(8,128)(2,1)S(1)} copy-done((bf16[256,64,128]{2,1,0:T(8,128)(2,1)S(1)}, bf16[256,64,128]{2,1,0:T(8,128)(2,1)}, u32[]{:S(2)}) %copy-start.4) | copy-done | bytes 4194328
  126.9 1.7 %copy-done.7 = bf16[256,4,9,128]{3,1,2,0:T(4,128)(2,1)S(1)} copy-done((bf16[256,4,9,128]{3,1,2,0:T(4,128)(2,1)S(1)}, bf16[256,4,9,128]{3,1,2,0:T(4,128)(2,1)}, u32[]{:S(2)}) %copy-start.7) | copy-done | bytes 2359320
  128.6 15.7 %score.1 = f32[16,128]{1,0:T(8,128)S(1)} custom-call(s32[4]{0:T(128)S(1)} %pad_add_fusion.places_ref, bf16[9216,128]{1,0:T(8,128)(2,1)S(1)} %bitcast.29, bf16[9216,128]{1,0:T(8,128)(2,1)} %collective-permute-done.refs_1_, bf16[9216,128]{1,0:T(8,128)(2,1)} %collective-permute-done.1.refs_2_, bf16[9216,128]{1,0:T(8,128)(2,1)} %collective-permute-done.2.refs_3_, ...), custom_call_target="tpu_custom_call" | custom-call | flops 29444014080 | bytes 20000000 | tf_op jit(solution)/shard_map/score/pallas_call | solution.py:171
  144.3 3.0 %collective-permute-start.7 = (f32[16,128]{1,0:T(8,128)S(1)}, f32[16,128]{1,0:T(8,128)S(1)}, u32[]{:S(2)}, u32[]{:S(2)}) collective-permute-start(f32[16,128]{1,0:T(8,128)S(1)} %score.1), channel_id=1, source_target_pairs={{0,6},{1,7},{2,4},{3,5},{4,2},{5,3},{6,0},{7,1},{8,14},{9,15},{10,... | collective-permute-start | bytes 24584 | tf_op jit(solution)/shard_map/ppermute | solution.py:326
  147.4 0.8 fusion.2
  148.2 1.1 collective-permute-done.7
  149.3 0.1 slice_select_fusion.1
  149.4 0.6 pad_maximum_fusion.1
  (19 shorter events, 0.1 us)
Async XLA Ops:
  0.6 53.4 %collective-permute-start.1 = (bf16[9216,128]{1,0:T(8,128)(2,1)}, bf16[9216,128]{1,0:T(8,128)(2,1)}, u32[]{:S(2)}, u32[]{:S(2)}) collective-permute-start(bf16[9216,128]{1,0:T(8,128)(2,1)} %bitcast.26), channel_id=1, source_target_pairs={{0,2},{1,3},{2,0},{3,1},{4,6},{5,7},{6,4},{7,5},{8,10},{9,11},{10,... | collective-permute-start | bytes 7077896 | tf_op jit(solution)/shard_map/ppermute | solution.py:326
  3.0 1.7 %copy-start.6 = (bf16[256,4,9,128]{3,1,2,0:T(4,128)(2,1)S(1)}, bf16[256,4,9,128]{3,1,2,0:T(4,128)(2,1)}, u32[]{:S(2)}) copy-start(bf16[256,4,9,128]{3,1,2,0:T(4,128)(2,1)} %param.7) | copy-start | bytes 7077892
  4.6 0.7 copy-start.9
  5.3 0.7 copy-start.10
  6.0 0.7 copy-start.11
  6.7 47.4 %copy-start = (bf16[256,50,128]{2,0,1:T(8,128)(2,1)S(1)}, bf16[256,50,128]{2,0,1:T(8,128)(2,1)}, u32[]{:S(2)}) copy-start(bf16[256,50,128]{2,0,1:T(8,128)(2,1)} %param.8) | copy-start | bytes 9830404
  7.9 1.0 copy-start.5
  8.8 49.6 %all-to-all-start = ((bf16[32,104,128]{2,1,0:T(8,128)(2,1)}), bf16[32,104,128]{2,1,0:T(8,128)(2,1)}, u32[]{:S(2)}, u32[]{:S(2)}) async-start(bf16[32,104,128]{2,1,0:T(8,128)(2,1)} %bitcast.25), calls=%async_computation | async-start | bytes 1703936 | tf_op jit(solution)/shard_map/all_to_all | solution.py:374
  17.8 104.7 %collective-permute-start = (bf16[9216,128]{1,0:T(8,128)(2,1)}, bf16[9216,128]{1,0:T(8,128)(2,1)}, u32[]{:S(2)}, u32[]{:S(2)}) collective-permute-start(bf16[9216,128]{1,0:T(8,128)(2,1)} %bitcast.27), channel_id=1, source_target_pairs={{0,1},{1,0},{2,3},{3,2},{4,5},{5,4},{6,7},{7,6},{8,9},{9,8},{10,11... | collective-permute-start | bytes 7077896 | tf_op jit(solution)/shard_map/ppermute | solution.py:326
  54.0 68.5 %collective-permute-start.2 = (bf16[9216,128]{1,0:T(8,128)(2,1)}, bf16[9216,128]{1,0:T(8,128)(2,1)}, u32[]{:S(2)}, u32[]{:S(2)}) collective-permute-start(bf16[9216,128]{1,0:T(8,128)(2,1)} %collective-permute-done.1.refs_2_), channel_id=1, source_target_pairs={{0,1},{1,0},{2,3},{3,2},{4,5},{5,4},{6,7},{7,6},{8,9},{9,8},{10,11... | collective-permute-start | bytes 7077896 | tf_op jit(solution)/shard_map/ppermute | solution.py:326
  55.4 24.2 %collective-permute-start.4 = (bf16[12,256,128]{2,1,0:T(8,128)(2,1)}, bf16[12,256,128]{2,1,0:T(8,128)(2,1)}, u32[]{:S(2)}, u32[]{:S(2)}) collective-permute-start(bf16[12,256,128]{2,1,0:T(8,128)(2,1)} %get-tuple-element.2), channel_id=1, source_target_pairs={{0,6},{1,7},{2,4},{3,5},{4,2},{5,3},{6,0},{7,1},{8,14},{9,15},{10,... | collective-permute-start | bytes 2359304 | tf_op jit(solution)/shard_map/ppermute | solution.py:326
  60.9 1.2 copy-start.8
  62.1 58.8 %all-to-all-start.1 = ((f32[8,51,8,128]{3,2,1,0:T(8,128)}), f32[8,51,8,128]{3,2,1,0:T(8,128)}, u32[]{:S(2)}, u32[]{:S(2)}) async-start(f32[8,51,8,128]{3,2,1,0:T(8,128)} %bitcast.30), calls=%async_computation.1 | async-start | bytes 3342336 | tf_op jit(solution)/shard_map/all_to_all | solution.py:377
  68.6 45.9 %collective-permute-start.3 = (bf16[14,256,128]{2,1,0:T(8,128)(2,1)}, bf16[14,256,128]{2,1,0:T(8,128)(2,1)}, u32[]{:S(2)}, u32[]{:S(2)}) collective-permute-start(bf16[14,256,128]{2,1,0:T(8,128)(2,1)} %pad_maximum_fusion), channel_id=1, source_target_pairs={{0,6},{1,7},{2,4},{3,5},{4,2},{5,3},{6,0},{7,1},{8,14},{9,15},{10,... | collective-permute-start | bytes 2752520 | tf_op jit(solution)/shard_map/ppermute | solution.py:326
  74.8 1.9 %copy-start.1 = (bf16[256,64,128]{2,1,0:T(8,128)(2,1)}, bf16[256,64,128]{2,1,0:T(8,128)(2,1)S(1)}, u32[]{:S(2)}) copy-start(bf16[256,64,128]{2,1,0:T(8,128)(2,1)S(1)} %by_harmonic.2.refs_4_) | copy-start | bytes 12582916
  79.6 34.9 %collective-permute-start.5 = (bf16[12,256,128]{2,1,0:T(8,128)(2,1)}, bf16[12,256,128]{2,1,0:T(8,128)(2,1)S(1)}, u32[]{:S(2)}, u32[]{:S(2)}) collective-permute-start(bf16[12,256,128]{2,1,0:T(8,128)(2,1)} %collective-permute-done.4.refs_1_), channel_id=1, source_target_pairs={{0,64},{8,72},{16,80},{24,88},{32,96},{40,104},{48,112},{56,120},{... | collective-permute-start | bytes 2359304 | tf_op jit(solution)/shard_map/ppermute | solution.py:337
  80.1 34.5 %collective-permute-start.6 = (bf16[12,256,128]{2,1,0:T(8,128)(2,1)}, bf16[12,256,128]{2,1,0:T(8,128)(2,1)S(1)}, u32[]{:S(2)}, u32[]{:S(2)}) collective-permute-start(bf16[12,256,128]{2,1,0:T(8,128)(2,1)} %collective-permute-done.4.refs_1_), channel_id=1, source_target_pairs={{0,192},{8,200},{16,208},{24,216},{32,224},{40,232},{48,240},{56,2... | collective-permute-start | bytes 2359304 | tf_op jit(solution)/shard_map/ppermute | solution.py:337
  119.0 2.0 %copy-start.3 = (bf16[256,64,128]{2,1,0:T(8,128)(2,1)}, bf16[256,64,128]{2,1,0:T(8,128)(2,1)S(1)}, u32[]{:S(2)}) copy-start(bf16[256,64,128]{2,1,0:T(8,128)(2,1)S(1)} %by_harmonic.3.refs_5_) | copy-start | bytes 12582916
  122.6 2.2 %copy-start.2 = (bf16[256,64,128]{2,1,0:T(8,128)(2,1)S(1)}, bf16[256,64,128]{2,1,0:T(8,128)(2,1)}, u32[]{:S(2)}) copy-start(bf16[256,64,128]{2,1,0:T(8,128)(2,1)} %copy-done.1) | copy-start | bytes 12582916
  124.7 2.2 %copy-start.4 = (bf16[256,64,128]{2,1,0:T(8,128)(2,1)S(1)}, bf16[256,64,128]{2,1,0:T(8,128)(2,1)}, u32[]{:S(2)}) copy-start(bf16[256,64,128]{2,1,0:T(8,128)(2,1)} %copy-done.3) | copy-start | bytes 12582916
  126.9 1.7 %copy-start.7 = (bf16[256,4,9,128]{3,1,2,0:T(4,128)(2,1)S(1)}, bf16[256,4,9,128]{3,1,2,0:T(4,128)(2,1)}, u32[]{:S(2)}) copy-start(bf16[256,4,9,128]{3,1,2,0:T(4,128)(2,1)} %param.7) | copy-start | bytes 7077892
  144.3 4.9 %collective-permute-start.7 = (f32[16,128]{1,0:T(8,128)S(1)}, f32[16,128]{1,0:T(8,128)S(1)}, u32[]{:S(2)}, u32[]{:S(2)}) collective-permute-start(f32[16,128]{1,0:T(8,128)S(1)} %score.1), channel_id=1, source_target_pairs={{0,6},{1,7},{2,4},{3,5},{4,2},{5,3},{6,0},{7,1},{8,14},{9,15},{10,... | collective-permute-start | bytes 24584 | tf_op jit(solution)/shard_map/ppermute | solution.py:326

commit v9 on v8

--- a/solution.py
+++ b/solution.py
@@ -102,19 +102,20 @@
         for t in range(CHUNK):
             slot = t % left_ref.shape[0]
             for g in range(groups):
-                a = fa[g, pl.ds(t * rows, rows), :]
-                b = fb[g, pl.ds((CHUNK - t) * rows, rows), :]
-                a_turned = pltpu.roll(a, cycles, 1) * sign
-                b_turned = pltpu.roll(b, cycles, 1) * (-sign)
-                if t == 0:
-                    b_turned = b_turned * paired + b * (1.0 - paired)
-                    a_turned = a_turned * paired
-                    b = b * paired
-                top = 2 * rows * g
-                left_ref[slot, pl.ds(top, rows), pl.ds(0, LANES)] = a
-                left_ref[slot, pl.ds(top, rows), pl.ds(LANES, LANES)] = b
-                left_ref[slot, pl.ds(top + rows, rows), pl.ds(0, LANES)] = a_turned
-                left_ref[slot, pl.ds(top + rows, rows), pl.ds(LANES, LANES)] = b_turned
+                block_rows = pl.ds(rows * g, rows)
+                left_ref[slot, block_rows, pl.ds(0, LANES)] = fa[g, pl.ds(t * rows, rows), :]
+                left_ref[slot, block_rows, pl.ds(LANES, LANES)] = fb[g, pl.ds((CHUNK - t) * rows, rows), :]
+            a = left_ref[slot, :, pl.ds(0, LANES)]
+            b = left_ref[slot, :, pl.ds(LANES, LANES)]
+            a_turned = pltpu.roll(a, cycles, 1) * sign
+            b_turned = pltpu.roll(b, cycles, 1) * (-sign)
+            if t == 0:
+                b_turned = b_turned * paired + b * (1.0 - paired)
+                a_turned = a_turned * paired
+                b = b * paired
+            straight = jnp.concatenate([a, b], axis=1).astype(jnp.bfloat16)
+            turned = jnp.concatenate([a_turned, b_turned], axis=1).astype(jnp.bfloat16)
+            left = jnp.concatenate([straight, turned], axis=0)
             m = j * CHUNK + t
             mirror = edge if t == 0 else 2 * half - m
             right = jnp.concatenate(
@@ -125,7 +126,7 @@
                 axis=1,
             )
             folded[pl.ds(m * pitch, all_rows), :] = lax.dot_general(
-                left_ref[slot].astype(jnp.bfloat16),
+                left,
                 right,
                 (((1,), (1,)), ((), ())),
                 preferred_element_type=jnp.float32,
@@ -138,8 +139,8 @@
     width = 2 * LANES
 
     def column(g, n):
-        even = folded[pl.ds(2 * rows * g + n, half, stride=pitch), :]
-        odd = folded[pl.ds(2 * rows * g + rows + n, half, stride=pitch), :]
+        even = folded[pl.ds(rows * g + n, half, stride=pitch), :]
+        odd = folded[pl.ds(rows * (groups + g) + n, half, stride=pitch), :]
         return jnp.concatenate([even, odd], axis=0).astype(jnp.bfloat16)
 
     def one_shift(s, best):
@@ -174,7 +175,7 @@
         out_specs=WHOLE,
         out_shape=jax.ShapeDtypeStruct((groups * each, LANES), jnp.float32),
         scratch_shapes=[
-            pltpu.VMEM((4, 2 * rows * groups, 2 * cycle_parts), jnp.float32),
+            pltpu.VMEM((4, rows * groups, 2 * cycle_parts), jnp.float32),
             pltpu.VMEM((groups, CHUNK * rows, cycle_parts), jnp.float32),
             pltpu.VMEM((groups, (CHUNK + 2) * rows, cycle_parts), jnp.float32),
             pltpu.VMEM(((2 * rows * groups + 1) * half, LANES), jnp.float32),
@@ -309,6 +310,36 @@
     )(arrived)
 
 
+def means_kernel(shares_ref, out_ref):
+    sources, extended, depth, cycle_parts = shares_ref.shape
+    class_count = extended - 1
+    lane = lax.broadcasted_iota(jnp.int32, (depth, cycle_parts), 1)
+
+    def summed(k):
+        total = shares_ref[0, k]
+        for source in range(1, sources):
+            total = total + shares_ref[source, k]
+        return total
+
+    weights = jnp.maximum(summed(class_count), 1.0)
+    for k in range(class_count):
+        weight = jnp.sum(jnp.where(lane == k, weights, 0.0), axis=1, keepdims=True)
+        out_ref[k] = summed(k) / weight
+
+
+def means_of(shares):
+    _, extended, depth, cycle_parts = shares.shape
+    return pl.pallas_call(
+        means_kernel,
+        in_specs=[WHOLE],
+        out_specs=WHOLE,
+        out_shape=jax.ShapeDtypeStruct((extended - 1, depth, cycle_parts), jnp.float32),
+        compiler_params=pltpu.CompilerParams(vmem_limit_bytes=6 * 1024 * 1024),
+        cost_estimate=pl.CostEstimate(flops=500_000, bytes_accessed=2_000_000, transcendentals=0),
+        name="means",
+    )(shares)
+
+
 def on_device(particles, references, class_ids, counts, shift_ids, weights):
     cls_index = lax.axis_index("cls")
     core = cls_index % 2
@@ -375,9 +406,7 @@
     sums = class_shares(arrived.reshape(doms, tiles, depth, cycle_parts), class_count, 2 * chips)
     sums = sums.reshape(2 * chips, class_count + 1, depth, cycle_parts)
     shares = lax.all_to_all(sums, "cls", 0, 0, tiled=True)
-    total = jnp.sum(shares, axis=0)
-    weight_sums = total[class_count, 0, :class_count]
-    class_means = total[:class_count] / jnp.maximum(weight_sums, 1.0)[:, None, None]
+    class_means = means_of(shares)
     class_means = jnp.transpose(class_means, (1, 0, 2))
 
     images = [flat, mate, partner, partner_mate]

time: 151 us -> 157 us (1.040)
  the two profiles are of different devices: /device:TPU:198 before, /device:TPU:8 now
where the time goes in v9:
time: 157 us; the launch traced here: 155 us
  waiting for transfers between devices  80.9 us (52%)
  Pallas kernels  27.4 us (17%)
  starting transfers between devices  26.4 us (17%)
  local copies, waits for them, and re-layouts  16.9 us (11%)
  other arithmetic  2.88 us (2%)
    ppermute x6, waiting for transfers between devices, move(): return lax.ppermute(value, 'cls', pairs)  80.3 us
    unnamed x24, local copies, waits for them, and re-layouts  15.7 us
    pallas_call x1, Pallas kernels, best_of_groups(): pl.pallas_call(functools.partial(score_kernel, scale, rows, shifts, group...  15.5 us
    all_to_all x1, starting transfers between devices, on_device(): lax.all_to_all(payload.reshape(doms, tiles * depth, cycle_parts), 'dom',...  11.4 us
    pallas_call x2, Pallas kernels, by_harmonic(): pl.pallas_call(functools.partial(gather_kernel, sizes), in_specs=[SCALARS...  7.42 us
    all_to_all x1, starting transfers between devices, on_device(): shares = lax.all_to_all(sums, 'cls', 0, 0, tiled=True)  5.93 us
    ppermute x6, starting transfers between devices, move(): return lax.ppermute(value, 'cls', pairs)  5.82 us
    ppermute x2, starting transfers between devices, around(): return lax.ppermute(value, 'dom', pairs)  3.24 us
  transfers between devices with their start and end apart: 10, of which 5 were waited for; matrix products, arithmetic and copies ran while one was open for 2% of the time, Pallas kernels for 18%

profile of v9, /device:TPU:8, one launch (start us, length us, event | category | flops | bytes accessed | tf_op | source)
XLA Modules:
  0.0 155.3 jit_solution(17632579050739440908)
XLA Ops:
  0.6 2.2 %collective-permute-start.1 = (bf16[9216,128]{1,0:T(8,128)(2,1)}, bf16[9216,128]{1,0:T(8,128)(2,1)}, u32[]{:S(2)}, u32[]{:S(2)}) collective-permute-start(bf16[9216,128]{1,0:T(8,128)(2,1)} %bitcast.23), channel_id=1, source_target_pairs={{0,2},{1,3},{2,0},{3,1},{4,6},{5,7},{6,4},{7,5},{8,10},{9,11},{10,... | collective-permute-start | bytes 7077896 | tf_op jit(solution)/shard_map/ppermute | solution.py:357
  2.9 0.0 collective-permute-start
  2.9 51.1 %collective-permute-done.1.refs_2_ = bf16[9216,128]{1,0:T(8,128)(2,1)} collective-permute-done((bf16[9216,128]{1,0:T(8,128)(2,1)}, bf16[9216,128]{1,0:T(8,128)(2,1)}, u32[]{:S(2)}, u32[]{:S(2)}) %collective-permute-start.1) | collective-permute-done | bytes 2359328 | tf_op jit(solution)/shard_map/ppermute | solution.py:357
  54.0 0.0 collective-permute-start.2
  54.0 0.7 convert_element_type.10.weight_ref
  54.7 1.7 %copy-done.6 = bf16[256,4,9,128]{3,1,2,0:T(4,128)(2,1)S(1)} copy-done((bf16[256,4,9,128]{3,1,2,0:T(4,128)(2,1)S(1)}, bf16[256,4,9,128]{3,1,2,0:T(4,128)(2,1)}, u32[]{:S(2)}) %copy-start.6) | copy-done | bytes 2359320
  56.4 0.7 copy-done.9
  57.1 0.7 copy-done.10
  57.7 0.7 copy-done.11
  58.4 1.2 listings.1
  59.6 0.0 copy-start.5
  59.6 0.9 copy-done.5
  60.5 11.4 %all-to-all-start = ((bf16[32,104,128]{2,1,0:T(8,128)(2,1)}), bf16[32,104,128]{2,1,0:T(8,128)(2,1)}, u32[]{:S(2)}, u32[]{:S(2)}) async-start(bf16[32,104,128]{2,1,0:T(8,128)(2,1)} %bitcast.22), calls=%async_computation | async-start | bytes 1703936 | tf_op jit(solution)/shard_map/all_to_all | solution.py:405
  72.0 0.0 copy-done
  72.0 1.0 dynamic-slice_bitcast_fusion
  73.0 1.6 %collective-permute-start.4 = (bf16[12,256,128]{2,1,0:T(8,128)(2,1)}, bf16[12,256,128]{2,1,0:T(8,128)(2,1)}, u32[]{:S(2)}, u32[]{:S(2)}) collective-permute-start(bf16[12,256,128]{2,1,0:T(8,128)(2,1)} %get-tuple-element.2), channel_id=1, source_target_pairs={{0,6},{1,7},{2,4},{3,5},{4,2},{5,3},{6,0},{7,1},{8,14},{9,15},{10,... | collective-permute-start | bytes 2359304 | tf_op jit(solution)/shard_map/ppermute | solution.py:357
  74.6 1.0 pad_maximum_fusion
  75.7 0.4 collective-permute-start.3
  76.1 3.0 %by_harmonic.2.refs_4_ = bf16[256,64,128]{2,1,0:T(8,128)(2,1)S(1)} custom-call(s32[1]{0:T(128)} %constant.130.clone.starts_ref, bf16[50,256,128]{2,1,0:T(8,128)(2,1)S(1)} %bitcast.21), custom_call_target="tpu_custom_call" | custom-call | bytes 14942208 | tf_op jit(solution)/shard_map/by_harmonic/pallas_call | solution.py:64
  79.1 1.9 %copy-done.1 = bf16[256,64,128]{2,1,0:T(8,128)(2,1)} copy-done((bf16[256,64,128]{2,1,0:T(8,128)(2,1)}, bf16[256,64,128]{2,1,0:T(8,128)(2,1)S(1)}, u32[]{:S(2)}) %copy-start.1) | copy-done | bytes 4194328
  81.1 0.1 stack.39.starts_ref
  81.2 12.6 %collective-permute-done.4.refs_1_ = bf16[12,256,128]{2,1,0:T(8,128)(2,1)} collective-permute-done((bf16[12,256,128]{2,1,0:T(8,128)(2,1)}, bf16[12,256,128]{2,1,0:T(8,128)(2,1)}, u32[]{:S(2)}, u32[]{:S(2)}) %collective-permute-start.4) | collective-permute-done | bytes 786464 | tf_op jit(solution)/shard_map/ppermute | solution.py:357
  93.8 1.7 %collective-permute-start.5 = (bf16[12,256,128]{2,1,0:T(8,128)(2,1)}, bf16[12,256,128]{2,1,0:T(8,128)(2,1)S(1)}, u32[]{:S(2)}, u32[]{:S(2)}) collective-permute-start(bf16[12,256,128]{2,1,0:T(8,128)(2,1)} %collective-permute-done.4.refs_1_), channel_id=1, source_target_pairs={{0,64},{8,72},{16,80},{24,88},{32,96},{40,104},{48,112},{56,120},{... | collective-permute-start | bytes 2359304 | tf_op jit(solution)/shard_map/ppermute | solution.py:368
  95.5 1.5 collective-permute-start.6
  97.0 0.1 pad_add_fusion.places_ref
  97.1 0.1 select_convert_fusion.1
  97.2 0.3 select_convert_fusion
  97.5 15.2 %collective-permute-done.3.refs_0_ = bf16[14,256,128]{2,1,0:T(8,128)(2,1)} collective-permute-done((bf16[14,256,128]{2,1,0:T(8,128)(2,1)}, bf16[14,256,128]{2,1,0:T(8,128)(2,1)}, u32[]{:S(2)}, u32[]{:S(2)}) %collective-permute-start.3) | collective-permute-done | bytes 917536 | tf_op jit(solution)/shard_map/ppermute | solution.py:357
  112.7 0.6 collective-permute-done.5.refs_2_
  113.3 0.0 collective-permute-done.6.refs_3_
  113.3 4.4 %by_harmonic.3.refs_5_ = bf16[256,64,128]{2,1,0:T(8,128)(2,1)S(1)} custom-call(s32[5]{0:T(128)S(1)} %stack.39.starts_ref, bf16[14,256,128]{2,1,0:T(8,128)(2,1)} %collective-permute-done.3.refs_0_, bf16[12,256,128]{2,1,0:T(8,128)(2,1)} %collective-permute-done.4.refs_1_, bf16[12,256,128]{2,1,0:T(8,128)(2,1)S(1)} %collective-permute-done.5.refs_2_, ...), custom_call_target="tpu_custom_call" | custom-call | bytes 14942208 | tf_op jit(solution)/shard_map/by_harmonic/pallas_call | solution.py:64
  117.7 2.0 %copy-done.3 = bf16[256,64,128]{2,1,0:T(8,128)(2,1)} copy-done((bf16[256,64,128]{2,1,0:T(8,128)(2,1)}, bf16[256,64,128]{2,1,0:T(8,128)(2,1)S(1)}, u32[]{:S(2)}) %copy-start.3) | copy-done | bytes 4194328
  119.7 0.0 all-to-all-done
  119.7 2.5 %shares.1 = f32[3264,128]{1,0:T(8,128)S(1)} custom-call(bf16[32,13,8,128]{3,2,1,0:T(8,128)(2,1)} %bitcast.15.arrived_ref), custom_call_target="tpu_custom_call" | custom-call | flops 4000000000 | bytes 8000000 | tf_op jit(solution)/shard_map/shares/pallas_call | solution.py:301
  122.3 1.2 copy-done.8
  123.4 5.9 %all-to-all-start.1 = ((f32[8,51,8,128]{3,2,1,0:T(8,128)}), f32[8,51,8,128]{3,2,1,0:T(8,128)S(1)}, u32[]{:S(2)}, u32[]{:S(2)}) async-start(f32[8,51,8,128]{3,2,1,0:T(8,128)} %bitcast.27), calls=%async_computation.1 | async-start | bytes 3342336 | tf_op jit(solution)/shard_map/all_to_all | solution.py:408
  129.3 0.0 collective-permute-done.refs_1_
  129.3 0.0 collective-permute-done.2.refs_3_
  129.4 2.2 %copy-done.2 = bf16[256,64,128]{2,1,0:T(8,128)(2,1)S(1)} copy-done((bf16[256,64,128]{2,1,0:T(8,128)(2,1)S(1)}, bf16[256,64,128]{2,1,0:T(8,128)(2,1)}, u32[]{:S(2)}) %copy-start.2) | copy-done | bytes 4194328
  131.5 2.2 %copy-done.4 = bf16[256,64,128]{2,1,0:T(8,128)(2,1)S(1)} copy-done((bf16[256,64,128]{2,1,0:T(8,128)(2,1)S(1)}, bf16[256,64,128]{2,1,0:T(8,128)(2,1)}, u32[]{:S(2)}) %copy-start.4) | copy-done | bytes 4194328
  133.7 1.7 %copy-done.7 = bf16[256,4,9,128]{3,1,2,0:T(4,128)(2,1)S(1)} copy-done((bf16[256,4,9,128]{3,1,2,0:T(4,128)(2,1)S(1)}, bf16[256,4,9,128]{3,1,2,0:T(4,128)(2,1)}, u32[]{:S(2)}) %copy-start.7) | copy-done | bytes 2359320
  135.4 15.5 %score.1 = f32[16,128]{1,0:T(8,128)S(1)} custom-call(s32[4]{0:T(128)S(1)} %pad_add_fusion.places_ref, bf16[9216,128]{1,0:T(8,128)(2,1)S(1)} %bitcast.26, bf16[9216,128]{1,0:T(8,128)(2,1)} %collective-permute-done.refs_1_, bf16[9216,128]{1,0:T(8,128)(2,1)} %collective-permute-done.1.refs_2_, bf16[9216,128]{1,0:T(8,128)(2,1)} %collective-permute-done.2.refs_3_, ...), custom_call_target="tpu_custom_call" | custom-call | flops 29444014080 | bytes 20000000 | tf_op jit(solution)/shard_map/score/pallas_call | solution.py:172
  150.9 1.5 collective-permute-start.7
  152.4 0.0 all-to-all-done.1.shares_ref
  152.4 0.8 means.1
  153.3 1.4 collective-permute-done.7
  154.6 0.1 slice_select_fusion.1
  154.7 0.6 pad_maximum_fusion.1
  (17 shorter events, 0.1 us)
Async XLA Ops:
  0.6 53.4 %collective-permute-start.1 = (bf16[9216,128]{1,0:T(8,128)(2,1)}, bf16[9216,128]{1,0:T(8,128)(2,1)}, u32[]{:S(2)}, u32[]{:S(2)}) collective-permute-start(bf16[9216,128]{1,0:T(8,128)(2,1)} %bitcast.23), channel_id=1, source_target_pairs={{0,2},{1,3},{2,0},{3,1},{4,6},{5,7},{6,4},{7,5},{8,10},{9,11},{10,... | collective-permute-start | bytes 7077896 | tf_op jit(solution)/shard_map/ppermute | solution.py:357
  2.9 126.5 %collective-permute-start = (bf16[9216,128]{1,0:T(8,128)(2,1)}, bf16[9216,128]{1,0:T(8,128)(2,1)}, u32[]{:S(2)}, u32[]{:S(2)}) collective-permute-start(bf16[9216,128]{1,0:T(8,128)(2,1)} %bitcast.24), channel_id=1, source_target_pairs={{0,1},{1,0},{2,3},{3,2},{4,5},{5,4},{6,7},{7,6},{8,9},{9,8},{10,11... | collective-permute-start | bytes 7077896 | tf_op jit(solution)/shard_map/ppermute | solution.py:357
  54.0 75.3 %collective-permute-start.2 = (bf16[9216,128]{1,0:T(8,128)(2,1)}, bf16[9216,128]{1,0:T(8,128)(2,1)}, u32[]{:S(2)}, u32[]{:S(2)}) collective-permute-start(bf16[9216,128]{1,0:T(8,128)(2,1)} %collective-permute-done.1.refs_2_), channel_id=1, source_target_pairs={{0,1},{1,0},{2,3},{3,2},{4,5},{5,4},{6,7},{7,6},{8,9},{9,8},{10,11... | collective-permute-start | bytes 7077896 | tf_op jit(solution)/shard_map/ppermute | solution.py:357
  54.7 1.7 %copy-start.6 = (bf16[256,4,9,128]{3,1,2,0:T(4,128)(2,1)S(1)}, bf16[256,4,9,128]{3,1,2,0:T(4,128)(2,1)}, u32[]{:S(2)}) copy-start(bf16[256,4,9,128]{3,1,2,0:T(4,128)(2,1)} %param.7) | copy-start | bytes 7077892
  56.4 0.7 copy-start.9
  57.1 0.7 copy-start.10
  57.7 0.7 copy-start.11
  58.4 13.6 %copy-start = (bf16[256,50,128]{2,0,1:T(8,128)(2,1)S(1)}, bf16[256,50,128]{2,0,1:T(8,128)(2,1)}, u32[]{:S(2)}) copy-start(bf16[256,50,128]{2,0,1:T(8,128)(2,1)} %param.8) | copy-start | bytes 9830404
  59.6 0.9 copy-start.5
  60.5 59.2 %all-to-all-start = ((bf16[32,104,128]{2,1,0:T(8,128)(2,1)}), bf16[32,104,128]{2,1,0:T(8,128)(2,1)}, u32[]{:S(2)}, u32[]{:S(2)}) async-start(bf16[32,104,128]{2,1,0:T(8,128)(2,1)} %bitcast.22), calls=%async_computation | async-start | bytes 1703936 | tf_op jit(solution)/shard_map/all_to_all | solution.py:405
  73.0 20.7 %collective-permute-start.4 = (bf16[12,256,128]{2,1,0:T(8,128)(2,1)}, bf16[12,256,128]{2,1,0:T(8,128)(2,1)}, u32[]{:S(2)}, u32[]{:S(2)}) collective-permute-start(bf16[12,256,128]{2,1,0:T(8,128)(2,1)} %get-tuple-element.2), channel_id=1, source_target_pairs={{0,6},{1,7},{2,4},{3,5},{4,2},{5,3},{6,0},{7,1},{8,14},{9,15},{10,... | collective-permute-start | bytes 2359304 | tf_op jit(solution)/shard_map/ppermute | solution.py:357
  75.7 37.0 %collective-permute-start.3 = (bf16[14,256,128]{2,1,0:T(8,128)(2,1)}, bf16[14,256,128]{2,1,0:T(8,128)(2,1)}, u32[]{:S(2)}, u32[]{:S(2)}) collective-permute-start(bf16[14,256,128]{2,1,0:T(8,128)(2,1)} %pad_maximum_fusion), channel_id=1, source_target_pairs={{0,6},{1,7},{2,4},{3,5},{4,2},{5,3},{6,0},{7,1},{8,14},{9,15},{10,... | collective-permute-start | bytes 2752520 | tf_op jit(solution)/shard_map/ppermute | solution.py:357
  79.1 2.0 %copy-start.1 = (bf16[256,64,128]{2,1,0:T(8,128)(2,1)}, bf16[256,64,128]{2,1,0:T(8,128)(2,1)S(1)}, u32[]{:S(2)}) copy-start(bf16[256,64,128]{2,1,0:T(8,128)(2,1)S(1)} %by_harmonic.2.refs_4_) | copy-start | bytes 12582916
  93.8 19.5 %collective-permute-start.5 = (bf16[12,256,128]{2,1,0:T(8,128)(2,1)}, bf16[12,256,128]{2,1,0:T(8,128)(2,1)S(1)}, u32[]{:S(2)}, u32[]{:S(2)}) collective-permute-start(bf16[12,256,128]{2,1,0:T(8,128)(2,1)} %collective-permute-done.4.refs_1_), channel_id=1, source_target_pairs={{0,64},{8,72},{16,80},{24,88},{32,96},{40,104},{48,112},{56,120},{... | collective-permute-start | bytes 2359304 | tf_op jit(solution)/shard_map/ppermute | solution.py:368
  95.5 17.8 %collective-permute-start.6 = (bf16[12,256,128]{2,1,0:T(8,128)(2,1)}, bf16[12,256,128]{2,1,0:T(8,128)(2,1)S(1)}, u32[]{:S(2)}, u32[]{:S(2)}) collective-permute-start(bf16[12,256,128]{2,1,0:T(8,128)(2,1)} %collective-permute-done.4.refs_1_), channel_id=1, source_target_pairs={{0,192},{8,200},{16,208},{24,216},{32,224},{40,232},{48,240},{56,2... | collective-permute-start | bytes 2359304 | tf_op jit(solution)/shard_map/ppermute | solution.py:368
  117.7 2.0 %copy-start.3 = (bf16[256,64,128]{2,1,0:T(8,128)(2,1)}, bf16[256,64,128]{2,1,0:T(8,128)(2,1)S(1)}, u32[]{:S(2)}) copy-start(bf16[256,64,128]{2,1,0:T(8,128)(2,1)S(1)} %by_harmonic.3.refs_5_) | copy-start | bytes 12582916
  122.2 1.2 copy-start.8
  123.4 29.0 %all-to-all-start.1 = ((f32[8,51,8,128]{3,2,1,0:T(8,128)}), f32[8,51,8,128]{3,2,1,0:T(8,128)S(1)}, u32[]{:S(2)}, u32[]{:S(2)}) async-start(f32[8,51,8,128]{3,2,1,0:T(8,128)} %bitcast.27), calls=%async_computation.1 | async-start | bytes 3342336 | tf_op jit(solution)/shard_map/all_to_all | solution.py:408
  129.4 2.2 %copy-start.2 = (bf16[256,64,128]{2,1,0:T(8,128)(2,1)S(1)}, bf16[256,64,128]{2,1,0:T(8,128)(2,1)}, u32[]{:S(2)}) copy-start(bf16[256,64,128]{2,1,0:T(8,128)(2,1)} %copy-done.1) | copy-start | bytes 12582916
  131.5 2.2 %copy-start.4 = (bf16[256,64,128]{2,1,0:T(8,128)(2,1)S(1)}, bf16[256,64,128]{2,1,0:T(8,128)(2,1)}, u32[]{:S(2)}) copy-start(bf16[256,64,128]{2,1,0:T(8,128)(2,1)} %copy-done.3) | copy-start | bytes 12582916
  133.7 1.7 %copy-start.7 = (bf16[256,4,9,128]{3,1,2,0:T(4,128)(2,1)S(1)}, bf16[256,4,9,128]{3,1,2,0:T(4,128)(2,1)}, u32[]{:S(2)}) copy-start(bf16[256,4,9,128]{3,1,2,0:T(4,128)(2,1)} %param.7) | copy-start | bytes 7077892
  150.9 3.7 %collective-permute-start.7 = (f32[16,128]{1,0:T(8,128)S(1)}, f32[16,128]{1,0:T(8,128)S(1)}, u32[]{:S(2)}, u32[]{:S(2)}) collective-permute-start(f32[16,128]{1,0:T(8,128)S(1)} %score.1), channel_id=1, source_target_pairs={{0,6},{1,7},{2,4},{3,5},{4,2},{5,3},{6,0},{7,1},{8,14},{9,15},{10,... | collective-permute-start | bytes 24584 | tf_op jit(solution)/shard_map/ppermute | solution.py:357

commit v10 on v9

--- a/solution.py
+++ b/solution.py
@@ -10,6 +10,8 @@
 
 
 CHUNK = 16
+SCORE_CHUNK = 32
+PITCH = CHUNK + 8
 LANES = 128
 WHOLE = pl.BlockSpec(memory_space=pltpu.VMEM)
 SCALARS = pl.BlockSpec(memory_space=pltpu.SMEM)
@@ -38,7 +40,7 @@
     pieces, out_ref, work = refs[: len(sizes)], refs[len(sizes)], refs[len(sizes) + 1]
     total = out_ref.shape[1]
     used = sum(map(sum, sizes))
-    work[pl.ds(used * CHUNK, (total - used) * CHUNK), :] = jnp.zeros(((total - used) * CHUNK, LANES), jnp.float32)
+    work[pl.ds(used * PITCH, (total - used) * PITCH), :] = jnp.zeros(((total - used) * PITCH, LANES), jnp.float32)
 
     def chunk(j, carry):
         base = pl.multiple_of(j * CHUNK, CHUNK)
@@ -46,13 +48,13 @@
         for parts, ref in zip(sizes, pieces):
             above = 0
             for size in parts:
-                block = ref[above : above + size, pl.ds(base, CHUNK), :].reshape(size * CHUNK, LANES)
-                first = pl.multiple_of(starts_ref[k] * CHUNK, CHUNK)
-                work[pl.ds(first, size * CHUNK), :] = block.astype(jnp.float32)
+                for row in range(size):
+                    first = pl.multiple_of((starts_ref[k] + row) * PITCH, 8)
+                    work[pl.ds(first, CHUNK), :] = ref[above + row, pl.ds(base, CHUNK), :].astype(jnp.float32)
                 above += size
                 k += 1
         for t in range(CHUNK):
-            out_ref[base + t] = work[pl.ds(t, total, stride=CHUNK), :].astype(jnp.bfloat16)
+            out_ref[base + t] = work[pl.ds(t, total, stride=PITCH), :].astype(jnp.bfloat16)
         return carry
 
     lax.fori_loop(0, out_ref.shape[0] // CHUNK, chunk, 0)
@@ -66,7 +68,7 @@
         in_specs=[SCALARS] + [WHOLE] * len(pieces),
         out_specs=WHOLE,
         out_shape=jax.ShapeDtypeStruct((angles, total, cycle_parts), jnp.bfloat16),
-        scratch_shapes=[pltpu.VMEM((total * CHUNK, cycle_parts), jnp.float32)],
+        scratch_shapes=[pltpu.VMEM((total * PITCH, cycle_parts), jnp.float32)],
         compiler_params=pltpu.CompilerParams(vmem_limit_bytes=14 * 1024 * 1024),
         cost_estimate=pl.CostEstimate(flops=0, bytes_accessed=2 * moved, transcendentals=0),
         name="by_harmonic",
@@ -84,14 +86,14 @@
     cycles = LANES // 2
     lane = lax.broadcasted_iota(jnp.int32, (1, LANES), 1)
     sign = jnp.where(lane < cycles, 1.0, -1.0)
-    block = CHUNK * rows
-    steps = half // CHUNK
+    block = SCORE_CHUNK * rows
+    steps = half // SCORE_CHUNK
 
     everyone = range(groups)
 
     def chunk(j, carry):
-        back = 2 * half - CHUNK - j * CHUNK
-        edge = jnp.where(j == 0, half, 2 * half - CHUNK * j)
+        back = 2 * half - SCORE_CHUNK - j * SCORE_CHUNK
+        edge = jnp.where(j == 0, half, 2 * half - SCORE_CHUNK * j)
         for g in everyone:
             fa[g] = images[g][pl.ds(pl.multiple_of(j * block, block), block), :].astype(jnp.float32)
             back_rows = pl.multiple_of(back * rows, block)
@@ -99,12 +101,12 @@
             edge_rows = pl.multiple_of(edge * rows, block)
             fb[g, pl.ds(block, 2 * rows), :] = images[g][pl.ds(edge_rows, 2 * rows), :].astype(jnp.float32)
         paired = jnp.where(j == 0, 0.0, 1.0)
-        for t in range(CHUNK):
+        for t in range(SCORE_CHUNK):
             slot = t % left_ref.shape[0]
             for g in range(groups):
                 block_rows = pl.ds(rows * g, rows)
                 left_ref[slot, block_rows, pl.ds(0, LANES)] = fa[g, pl.ds(t * rows, rows), :]
-                left_ref[slot, block_rows, pl.ds(LANES, LANES)] = fb[g, pl.ds((CHUNK - t) * rows, rows), :]
+                left_ref[slot, block_rows, pl.ds(LANES, LANES)] = fb[g, pl.ds((SCORE_CHUNK - t) * rows, rows), :]
             a = left_ref[slot, :, pl.ds(0, LANES)]
             b = left_ref[slot, :, pl.ds(LANES, LANES)]
             a_turned = pltpu.roll(a, cycles, 1) * sign
@@ -116,7 +118,7 @@
             straight = jnp.concatenate([a, b], axis=1).astype(jnp.bfloat16)
             turned = jnp.concatenate([a_turned, b_turned], axis=1).astype(jnp.bfloat16)
             left = jnp.concatenate([straight, turned], axis=0)
-            m = j * CHUNK + t
+            m = j * SCORE_CHUNK + t
             mirror = edge if t == 0 else 2 * half - m
             right = jnp.concatenate(
                 [
@@ -176,8 +178,8 @@
         out_shape=jax.ShapeDtypeStruct((groups * each, LANES), jnp.float32),
         scratch_shapes=[
             pltpu.VMEM((4, rows * groups, 2 * cycle_parts), jnp.float32),
-            pltpu.VMEM((groups, CHUNK * rows, cycle_parts), jnp.float32),
-            pltpu.VMEM((groups, (CHUNK + 2) * rows, cycle_parts), jnp.float32),
+            pltpu.VMEM((groups, SCORE_CHUNK * rows, cycle_parts), jnp.float32),
+            pltpu.VMEM((groups, (SCORE_CHUNK + 2) * rows, cycle_parts), jnp.float32),
             pltpu.VMEM(((2 * rows * groups + 1) * half, LANES), jnp.float32),
         ],
         compiler_params=pltpu.CompilerParams(vmem_limit_bytes=36 * 1024 * 1024),

time: 157 us -> 155 us (0.987)
  Pallas kernels: 27.4 us -> 24.5 us
    pallas_call x2, Pallas kernels: 7.42 us -> 5.12 us  [by_harmonic(): pl.pallas_call(functools.partial(gather_kernel, sizes), in_specs=[SCALARS...]
  transfers between devices with their start and end apart: 10 -> 10, of which waited for: 5 -> 5; matrix products, arithmetic and copies ran while one was open for 2% -> 2% of each run, Pallas kernels for 18% -> 16%
where the time goes in v10:
time: 155 us; the launch traced here: 154 us
  waiting for transfers between devices  82 us (53%)
  starting transfers between devices  26.4 us (17%)
  Pallas kernels  24.5 us (16%)
  local copies, waits for them, and re-layouts  16.9 us (11%)
  other arithmetic  2.88 us (2%)
    ppermute x6, waiting for transfers between devices, move(): return lax.ppermute(value, 'cls', pairs)  81.4 us
    unnamed x24, local copies, waits for them, and re-layouts  15.7 us
    pallas_call x1, Pallas kernels, best_of_groups(): pl.pallas_call(functools.partial(score_kernel, scale, rows, shifts, group...  14.9 us
    all_to_all x1, starting transfers between devices, on_device(): lax.all_to_all(payload.reshape(doms, tiles * depth, cycle_parts), 'dom',...  11.4 us
    all_to_all x1, starting transfers between devices, on_device(): shares = lax.all_to_all(sums, 'cls', 0, 0, tiled=True)  5.94 us
    ppermute x6, starting transfers between devices, move(): return lax.ppermute(value, 'cls', pairs)  5.83 us
    pallas_call x2, Pallas kernels, by_harmonic(): pl.pallas_call(functools.partial(gather_kernel, sizes), in_specs=[SCALARS...  5.12 us
    ppermute x2, starting transfers between devices, around(): return lax.ppermute(value, 'dom', pairs)  3.24 us
  transfers between devices with their start and end apart: 10, of which 5 were waited for; matrix products, arithmetic and copies ran while one was open for 2% of the time, Pallas kernels for 16%

profile of v10, /device:TPU:8, one launch (start us, length us, event | category | flops | bytes accessed | tf_op | source)
XLA Modules:
  0.0 153.6 jit_solution(7948050945935075802)
XLA Ops:
  0.6 2.2 %collective-permute-start.1 = (bf16[9216,128]{1,0:T(8,128)(2,1)}, bf16[9216,128]{1,0:T(8,128)(2,1)}, u32[]{:S(2)}, u32[]{:S(2)}) collective-permute-start(bf16[9216,128]{1,0:T(8,128)(2,1)} %bitcast.23), channel_id=1, source_target_pairs={{0,2},{1,3},{2,0},{3,1},{4,6},{5,7},{6,4},{7,5},{8,10},{9,11},{10,... | collective-permute-start | bytes 7077896 | tf_op jit(solution)/shard_map/ppermute | solution.py:359
  2.9 0.0 collective-permute-start
  2.9 51.1 %collective-permute-done.1.refs_2_ = bf16[9216,128]{1,0:T(8,128)(2,1)} collective-permute-done((bf16[9216,128]{1,0:T(8,128)(2,1)}, bf16[9216,128]{1,0:T(8,128)(2,1)}, u32[]{:S(2)}, u32[]{:S(2)}) %collective-permute-start.1) | collective-permute-done | bytes 2359328 | tf_op jit(solution)/shard_map/ppermute | solution.py:359
  54.0 0.0 collective-permute-start.2
  54.0 0.7 convert_element_type.10.weight_ref
  54.7 1.7 %copy-done.6 = bf16[256,4,9,128]{3,1,2,0:T(4,128)(2,1)S(1)} copy-done((bf16[256,4,9,128]{3,1,2,0:T(4,128)(2,1)S(1)}, bf16[256,4,9,128]{3,1,2,0:T(4,128)(2,1)}, u32[]{:S(2)}) %copy-start.6) | copy-done | bytes 2359320
  56.4 0.7 copy-done.9
  57.1 0.7 copy-done.10
  57.7 0.7 copy-done.11
  58.4 1.2 listings.1
  59.6 0.0 copy-start.5
  59.6 0.9 copy-done.5
  60.5 11.4 %all-to-all-start = ((bf16[32,104,128]{2,1,0:T(8,128)(2,1)}), bf16[32,104,128]{2,1,0:T(8,128)(2,1)}, u32[]{:S(2)}, u32[]{:S(2)}) async-start(bf16[32,104,128]{2,1,0:T(8,128)(2,1)} %bitcast.22), calls=%async_computation | async-start | bytes 1703936 | tf_op jit(solution)/shard_map/all_to_all | solution.py:407
  72.0 0.0 copy-done
  72.0 1.0 dynamic-slice_bitcast_fusion
  73.0 1.6 %collective-permute-start.4 = (bf16[12,256,128]{2,1,0:T(8,128)(2,1)}, bf16[12,256,128]{2,1,0:T(8,128)(2,1)}, u32[]{:S(2)}, u32[]{:S(2)}) collective-permute-start(bf16[12,256,128]{2,1,0:T(8,128)(2,1)} %get-tuple-element.2), channel_id=1, source_target_pairs={{0,6},{1,7},{2,4},{3,5},{4,2},{5,3},{6,0},{7,1},{8,14},{9,15},{10,... | collective-permute-start | bytes 2359304 | tf_op jit(solution)/shard_map/ppermute | solution.py:359
  74.6 1.0 pad_maximum_fusion
  75.7 0.4 collective-permute-start.3
  76.1 1.9 %by_harmonic.2.refs_4_ = bf16[256,64,128]{2,1,0:T(8,128)(2,1)S(1)} custom-call(s32[1]{0:T(128)} %constant.130.clone.starts_ref, bf16[50,256,128]{2,1,0:T(8,128)(2,1)S(1)} %bitcast.21), custom_call_target="tpu_custom_call" | custom-call | bytes 14942208 | tf_op jit(solution)/shard_map/by_harmonic/pallas_call | solution.py:66
  78.0 1.9 %copy-done.1 = bf16[256,64,128]{2,1,0:T(8,128)(2,1)} copy-done((bf16[256,64,128]{2,1,0:T(8,128)(2,1)}, bf16[256,64,128]{2,1,0:T(8,128)(2,1)S(1)}, u32[]{:S(2)}) %copy-start.1) | copy-done | bytes 4194328
  79.9 0.1 stack.39.starts_ref
  80.0 13.8 %collective-permute-done.4.refs_1_ = bf16[12,256,128]{2,1,0:T(8,128)(2,1)} collective-permute-done((bf16[12,256,128]{2,1,0:T(8,128)(2,1)}, bf16[12,256,128]{2,1,0:T(8,128)(2,1)}, u32[]{:S(2)}, u32[]{:S(2)}) %collective-permute-start.4) | collective-permute-done | bytes 786464 | tf_op jit(solution)/shard_map/ppermute | solution.py:359
  93.8 1.7 %collective-permute-start.5 = (bf16[12,256,128]{2,1,0:T(8,128)(2,1)}, bf16[12,256,128]{2,1,0:T(8,128)(2,1)S(1)}, u32[]{:S(2)}, u32[]{:S(2)}) collective-permute-start(bf16[12,256,128]{2,1,0:T(8,128)(2,1)} %collective-permute-done.4.refs_1_), channel_id=1, source_target_pairs={{0,64},{8,72},{16,80},{24,88},{32,96},{40,104},{48,112},{56,120},{... | collective-permute-start | bytes 2359304 | tf_op jit(solution)/shard_map/ppermute | solution.py:370
  95.5 1.5 collective-permute-start.6
  97.0 0.1 pad_add_fusion.places_ref
  97.1 0.1 select_convert_fusion.1
  97.2 0.3 select_convert_fusion
  97.5 15.2 %collective-permute-done.3.refs_0_ = bf16[14,256,128]{2,1,0:T(8,128)(2,1)} collective-permute-done((bf16[14,256,128]{2,1,0:T(8,128)(2,1)}, bf16[14,256,128]{2,1,0:T(8,128)(2,1)}, u32[]{:S(2)}, u32[]{:S(2)}) %collective-permute-start.3) | collective-permute-done | bytes 917536 | tf_op jit(solution)/shard_map/ppermute | solution.py:359
  112.7 0.6 collective-permute-done.5.refs_2_
  113.3 0.0 collective-permute-done.6.refs_3_
  113.3 3.3 %by_harmonic.3.refs_5_ = bf16[256,64,128]{2,1,0:T(8,128)(2,1)S(1)} custom-call(s32[5]{0:T(128)S(1)} %stack.39.starts_ref, bf16[14,256,128]{2,1,0:T(8,128)(2,1)} %collective-permute-done.3.refs_0_, bf16[12,256,128]{2,1,0:T(8,128)(2,1)} %collective-permute-done.4.refs_1_, bf16[12,256,128]{2,1,0:T(8,128)(2,1)S(1)} %collective-permute-done.5.refs_2_, ...), custom_call_target="tpu_custom_call" | custom-call | bytes 14942208 | tf_op jit(solution)/shard_map/by_harmonic/pallas_call | solution.py:66
  116.6 2.0 %copy-done.3 = bf16[256,64,128]{2,1,0:T(8,128)(2,1)} copy-done((bf16[256,64,128]{2,1,0:T(8,128)(2,1)}, bf16[256,64,128]{2,1,0:T(8,128)(2,1)S(1)}, u32[]{:S(2)}) %copy-start.3) | copy-done | bytes 4194328
  118.6 0.0 all-to-all-done
  118.6 2.5 %shares.1 = f32[3264,128]{1,0:T(8,128)S(1)} custom-call(bf16[32,13,8,128]{3,2,1,0:T(8,128)(2,1)} %bitcast.15.arrived_ref), custom_call_target="tpu_custom_call" | custom-call | flops 4000000000 | bytes 8000000 | tf_op jit(solution)/shard_map/shares/pallas_call | solution.py:303
  121.1 1.2 copy-done.8
  122.3 5.9 %all-to-all-start.1 = ((f32[8,51,8,128]{3,2,1,0:T(8,128)}), f32[8,51,8,128]{3,2,1,0:T(8,128)S(1)}, u32[]{:S(2)}, u32[]{:S(2)}) async-start(f32[8,51,8,128]{3,2,1,0:T(8,128)} %bitcast.27), calls=%async_computation.1 | async-start | bytes 3342336 | tf_op jit(solution)/shard_map/all_to_all | solution.py:410
  128.2 0.0 collective-permute-done.refs_1_
  128.2 0.0 collective-permute-done.2.refs_3_
  128.2 2.2 %copy-done.2 = bf16[256,64,128]{2,1,0:T(8,128)(2,1)S(1)} copy-done((bf16[256,64,128]{2,1,0:T(8,128)(2,1)S(1)}, bf16[256,64,128]{2,1,0:T(8,128)(2,1)}, u32[]{:S(2)}) %copy-start.2) | copy-done | bytes 4194328
  130.4 2.2 %copy-done.4 = bf16[256,64,128]{2,1,0:T(8,128)(2,1)S(1)} copy-done((bf16[256,64,128]{2,1,0:T(8,128)(2,1)S(1)}, bf16[256,64,128]{2,1,0:T(8,128)(2,1)}, u32[]{:S(2)}) %copy-start.4) | copy-done | bytes 4194328
  132.6 1.7 %copy-done.7 = bf16[256,4,9,128]{3,1,2,0:T(4,128)(2,1)S(1)} copy-done((bf16[256,4,9,128]{3,1,2,0:T(4,128)(2,1)S(1)}, bf16[256,4,9,128]{3,1,2,0:T(4,128)(2,1)}, u32[]{:S(2)}) %copy-start.7) | copy-done | bytes 2359320
  134.2 14.9 %score.1 = f32[16,128]{1,0:T(8,128)S(1)} custom-call(s32[4]{0:T(128)S(1)} %pad_add_fusion.places_ref, bf16[9216,128]{1,0:T(8,128)(2,1)S(1)} %bitcast.26, bf16[9216,128]{1,0:T(8,128)(2,1)} %collective-permute-done.refs_1_, bf16[9216,128]{1,0:T(8,128)(2,1)} %collective-permute-done.1.refs_2_, bf16[9216,128]{1,0:T(8,128)(2,1)} %collective-permute-done.2.refs_3_, ...), custom_call_target="tpu_custom_call" | custom-call | flops 29444014080 | bytes 20000000 | tf_op jit(solution)/shard_map/score/pallas_call | solution.py:174
  149.1 1.6 %collective-permute-start.7 = (f32[16,128]{1,0:T(8,128)S(1)}, f32[16,128]{1,0:T(8,128)S(1)}, u32[]{:S(2)}, u32[]{:S(2)}) collective-permute-start(f32[16,128]{1,0:T(8,128)S(1)} %score.1), channel_id=1, source_target_pairs={{0,6},{1,7},{2,4},{3,5},{4,2},{5,3},{6,0},{7,1},{8,14},{9,15},{10,... | collective-permute-start | bytes 24584 | tf_op jit(solution)/shard_map/ppermute | solution.py:359
  150.7 0.0 all-to-all-done.1.shares_ref
  150.7 0.8 means.1
  151.5 1.4 collective-permute-done.7
  152.9 0.1 slice_select_fusion.1
  153.0 0.6 pad_maximum_fusion.1
  (17 shorter events, 0.1 us)
Async XLA Ops:
  0.6 53.4 %collective-permute-start.1 = (bf16[9216,128]{1,0:T(8,128)(2,1)}, bf16[9216,128]{1,0:T(8,128)(2,1)}, u32[]{:S(2)}, u32[]{:S(2)}) collective-permute-start(bf16[9216,128]{1,0:T(8,128)(2,1)} %bitcast.23), channel_id=1, source_target_pairs={{0,2},{1,3},{2,0},{3,1},{4,6},{5,7},{6,4},{7,5},{8,10},{9,11},{10,... | collective-permute-start | bytes 7077896 | tf_op jit(solution)/shard_map/ppermute | solution.py:359
  2.9 125.3 %collective-permute-start = (bf16[9216,128]{1,0:T(8,128)(2,1)}, bf16[9216,128]{1,0:T(8,128)(2,1)}, u32[]{:S(2)}, u32[]{:S(2)}) collective-permute-start(bf16[9216,128]{1,0:T(8,128)(2,1)} %bitcast.24), channel_id=1, source_target_pairs={{0,1},{1,0},{2,3},{3,2},{4,5},{5,4},{6,7},{7,6},{8,9},{9,8},{10,11... | collective-permute-start | bytes 7077896 | tf_op jit(solution)/shard_map/ppermute | solution.py:359
  54.0 74.2 %collective-permute-start.2 = (bf16[9216,128]{1,0:T(8,128)(2,1)}, bf16[9216,128]{1,0:T(8,128)(2,1)}, u32[]{:S(2)}, u32[]{:S(2)}) collective-permute-start(bf16[9216,128]{1,0:T(8,128)(2,1)} %collective-permute-done.1.refs_2_), channel_id=1, source_target_pairs={{0,1},{1,0},{2,3},{3,2},{4,5},{5,4},{6,7},{7,6},{8,9},{9,8},{10,11... | collective-permute-start | bytes 7077896 | tf_op jit(solution)/shard_map/ppermute | solution.py:359
  54.7 1.7 %copy-start.6 = (bf16[256,4,9,128]{3,1,2,0:T(4,128)(2,1)S(1)}, bf16[256,4,9,128]{3,1,2,0:T(4,128)(2,1)}, u32[]{:S(2)}) copy-start(bf16[256,4,9,128]{3,1,2,0:T(4,128)(2,1)} %param.7) | copy-start | bytes 7077892
  56.4 0.7 copy-start.9
  57.1 0.7 copy-start.10
  57.7 0.7 copy-start.11
  58.4 13.6 %copy-start = (bf16[256,50,128]{2,0,1:T(8,128)(2,1)S(1)}, bf16[256,50,128]{2,0,1:T(8,128)(2,1)}, u32[]{:S(2)}) copy-start(bf16[256,50,128]{2,0,1:T(8,128)(2,1)} %param.8) | copy-start | bytes 9830404
  59.6 0.9 copy-start.5
  60.5 58.1 %all-to-all-start = ((bf16[32,104,128]{2,1,0:T(8,128)(2,1)}), bf16[32,104,128]{2,1,0:T(8,128)(2,1)}, u32[]{:S(2)}, u32[]{:S(2)}) async-start(bf16[32,104,128]{2,1,0:T(8,128)(2,1)} %bitcast.22), calls=%async_computation | async-start | bytes 1703936 | tf_op jit(solution)/shard_map/all_to_all | solution.py:407
  73.0 20.7 %collective-permute-start.4 = (bf16[12,256,128]{2,1,0:T(8,128)(2,1)}, bf16[12,256,128]{2,1,0:T(8,128)(2,1)}, u32[]{:S(2)}, u32[]{:S(2)}) collective-permute-start(bf16[12,256,128]{2,1,0:T(8,128)(2,1)} %get-tuple-element.2), channel_id=1, source_target_pairs={{0,6},{1,7},{2,4},{3,5},{4,2},{5,3},{6,0},{7,1},{8,14},{9,15},{10,... | collective-permute-start | bytes 2359304 | tf_op jit(solution)/shard_map/ppermute | solution.py:359
  75.7 37.0 %collective-permute-start.3 = (bf16[14,256,128]{2,1,0:T(8,128)(2,1)}, bf16[14,256,128]{2,1,0:T(8,128)(2,1)}, u32[]{:S(2)}, u32[]{:S(2)}) collective-permute-start(bf16[14,256,128]{2,1,0:T(8,128)(2,1)} %pad_maximum_fusion), channel_id=1, source_target_pairs={{0,6},{1,7},{2,4},{3,5},{4,2},{5,3},{6,0},{7,1},{8,14},{9,15},{10,... | collective-permute-start | bytes 2752520 | tf_op jit(solution)/shard_map/ppermute | solution.py:359
  78.0 2.0 %copy-start.1 = (bf16[256,64,128]{2,1,0:T(8,128)(2,1)}, bf16[256,64,128]{2,1,0:T(8,128)(2,1)S(1)}, u32[]{:S(2)}) copy-start(bf16[256,64,128]{2,1,0:T(8,128)(2,1)S(1)} %by_harmonic.2.refs_4_) | copy-start | bytes 12582916
  93.8 19.5 %collective-permute-start.5 = (bf16[12,256,128]{2,1,0:T(8,128)(2,1)}, bf16[12,256,128]{2,1,0:T(8,128)(2,1)S(1)}, u32[]{:S(2)}, u32[]{:S(2)}) collective-permute-start(bf16[12,256,128]{2,1,0:T(8,128)(2,1)} %collective-permute-done.4.refs_1_), channel_id=1, source_target_pairs={{0,64},{8,72},{16,80},{24,88},{32,96},{40,104},{48,112},{56,120},{... | collective-permute-start | bytes 2359304 | tf_op jit(solution)/shard_map/ppermute | solution.py:370
  95.5 17.8 %collective-permute-start.6 = (bf16[12,256,128]{2,1,0:T(8,128)(2,1)}, bf16[12,256,128]{2,1,0:T(8,128)(2,1)S(1)}, u32[]{:S(2)}, u32[]{:S(2)}) collective-permute-start(bf16[12,256,128]{2,1,0:T(8,128)(2,1)} %collective-permute-done.4.refs_1_), channel_id=1, source_target_pairs={{0,192},{8,200},{16,208},{24,216},{32,224},{40,232},{48,240},{56,2... | collective-permute-start | bytes 2359304 | tf_op jit(solution)/shard_map/ppermute | solution.py:370
  116.6 2.0 %copy-start.3 = (bf16[256,64,128]{2,1,0:T(8,128)(2,1)}, bf16[256,64,128]{2,1,0:T(8,128)(2,1)S(1)}, u32[]{:S(2)}) copy-start(bf16[256,64,128]{2,1,0:T(8,128)(2,1)S(1)} %by_harmonic.3.refs_5_) | copy-start | bytes 12582916
  121.1 1.2 copy-start.8
  122.3 28.4 %all-to-all-start.1 = ((f32[8,51,8,128]{3,2,1,0:T(8,128)}), f32[8,51,8,128]{3,2,1,0:T(8,128)S(1)}, u32[]{:S(2)}, u32[]{:S(2)}) async-start(f32[8,51,8,128]{3,2,1,0:T(8,128)} %bitcast.27), calls=%async_computation.1 | async-start | bytes 3342336 | tf_op jit(solution)/shard_map/all_to_all | solution.py:410
  128.2 2.2 %copy-start.2 = (bf16[256,64,128]{2,1,0:T(8,128)(2,1)S(1)}, bf16[256,64,128]{2,1,0:T(8,128)(2,1)}, u32[]{:S(2)}) copy-start(bf16[256,64,128]{2,1,0:T(8,128)(2,1)} %copy-done.1) | copy-start | bytes 12582916
  130.4 2.2 %copy-start.4 = (bf16[256,64,128]{2,1,0:T(8,128)(2,1)S(1)}, bf16[256,64,128]{2,1,0:T(8,128)(2,1)}, u32[]{:S(2)}) copy-start(bf16[256,64,128]{2,1,0:T(8,128)(2,1)} %copy-done.3) | copy-start | bytes 12582916
  132.6 1.7 %copy-start.7 = (bf16[256,4,9,128]{3,1,2,0:T(4,128)(2,1)S(1)}, bf16[256,4,9,128]{3,1,2,0:T(4,128)(2,1)}, u32[]{:S(2)}) copy-start(bf16[256,4,9,128]{3,1,2,0:T(4,128)(2,1)} %param.7) | copy-start | bytes 7077892
  149.1 3.7 %collective-permute-start.7 = (f32[16,128]{1,0:T(8,128)S(1)}, f32[16,128]{1,0:T(8,128)S(1)}, u32[]{:S(2)}, u32[]{:S(2)}) collective-permute-start(f32[16,128]{1,0:T(8,128)S(1)} %score.1), channel_id=1, source_target_pairs={{0,6},{1,7},{2,4},{3,5},{4,2},{5,3},{6,0},{7,1},{8,14},{9,15},{10,... | collective-permute-start | bytes 24584 | tf_op jit(solution)/shard_map/ppermute | solution.py:359
